TPU v7x, 32 devices: a whole 2x2x4 slice. The times are simulated.
32 devices in a mesh: shard: 4 (over z), ctx: 2 (over y), tp: 4 (over x, core).
Axes of the slice: x: 2, y: 2, z: 4, core: 2. Of those that a mesh axis runs over, the one named last changes fastest.
Arguments:
- inputs: bfloat16 [16, 1024, 512], P('shard', 'ctx'), may hold values from -6 to 6
- first_memory: float32 [16, 64, 512], P('shard'), may hold values from -6 to 6
- piece_start: int32 [16, 2], P('shard', 'ctx'), may hold values from 0 to 448, as said below
- piece_len: int32 [16, 2], P('shard', 'ctx'), may hold values from 64 to 256, as said below
- w_query: bfloat16 [512, 512], P(('shard', 'tp')), may hold values from -0.25 to 0.25
- w_key: bfloat16 [512, 512], P(('shard', 'tp')), may hold values from -0.25 to 0.25
- w_value: bfloat16 [512, 512], P(('shard', 'tp')), may hold values from -0.25 to 0.25
- w_out: bfloat16 [512, 512], P(('shard', 'tp')), may hold values from -1 to 1
- w_up: bfloat16 [512, 2048], P(('shard', 'tp')), may hold values from -0.25 to 0.25
- w_down: bfloat16 [2048, 512], P(('shard', 'tp')), may hold values from -0.125 to 0.125
- u_query: bfloat16 [512, 512], P(('shard', 'tp')), may hold values from -0.25 to 0.25
- u_key: bfloat16 [512, 512], P(('shard', 'tp')), may hold values from -0.25 to 0.25
- u_value: bfloat16 [512, 512], P(('shard', 'tp')), may hold values from -0.25 to 0.25
- u_out: bfloat16 [512, 512], P(('shard', 'tp')), may hold values from -1 to 1
- u_gate: bfloat16 [512, 512], P(('shard', 'tp')), may hold values from -0.25 to 0.25
- gain_attn: float32 [512], replicated, may hold values from 0.5 to 1.5
- gain_ffn: float32 [512], replicated, may hold values from 0.5 to 1.5
- gain_write: float32 [512], replicated, may hold values from 0.5 to 1.5
- gate_bias: float32 [512], replicated, may hold values from 1 to 3
- out_grad: bfloat16 [16, 1024, 512], P('shard', ('ctx', 'tp')), may hold values from -6 to 6
- memory_grad: float32 [16, 128, 512], P('shard', 'ctx'), may hold values from -6 to 6
Outputs:
- outputs: bfloat16 [16, 1024, 512], P('shard', ('ctx', 'tp'))
- memories_after: float32 [16, 128, 512], P('shard', 'ctx')
- input_grad: bfloat16 [16, 1024, 512], P('shard', ('ctx', 'tp'))
- memory_in_grad: float32 [16, 128, 512], P('shard', 'ctx')
- grad_w_query: float32 [512, 512], P(('shard', 'ctx'), 'tp')
- grad_w_key: float32 [512, 512], P(('shard', 'ctx'), 'tp')
- grad_w_value: float32 [512, 512], P(('shard', 'ctx'), 'tp')
- grad_w_out: float32 [512, 512], P(('shard', 'ctx', 'tp'))
- grad_w_up: float32 [512, 2048], P(('shard', 'ctx', 'tp'))
- grad_w_down: float32 [2048, 512], P(('shard', 'ctx', 'tp'))
- grad_u_query: float32 [512, 512], P(('shard', 'ctx'), 'tp')
- grad_u_key: float32 [512, 512], P(('shard', 'ctx'), 'tp')
- grad_u_value: float32 [512, 512], P(('shard', 'ctx'), 'tp')
- grad_u_out: float32 [512, 512], P('tp', ('shard', 'ctx'))
- grad_u_gate: float32 [512, 512], P('tp', ('shard', 'ctx'))
- grad_gain_attn: float32 [512], P(('shard', 'ctx', 'tp'))
- grad_gain_ffn: float32 [512], P(('shard', 'ctx', 'tp'))
- grad_gain_write: float32 [512], P(('shard', 'ctx', 'tp'))
- grad_gate_bias: float32 [512], P(('shard', 'ctx', 'tp'))
Inputs may be any that keep to these rules, and one draw needn't show every extreme that they name: `piece_len`: each segment has one picture piece of 64 to 256 tokens; some piece has exactly 256. A piece lies inside its segment: piece_start + piece_len <= 512.
All inputs are finite; a program needn't handle non-finite values.
Results may differ from a plain program's by a relative error of at most 0.03.
Values may be sent and summed in bfloat16 or wider, within the bound.
A program may use at most 128 MiB of HBM per device.

v0:
```python
from functools import partial

import jax
import jax.numpy as jnp
from jax import lax
from jax.sharding import PartitionSpec as P

HEAD_DIM = 64


EPS = 1e-05


def from_behind(array, axis, by):
    peers = lax.axis_size(axis)
    pairs = [(i, i + by) for i in range(peers) if 0 <= i + by < peers]
    return lax.ppermute(array, axis, pairs)


def norm_rows(values):
    centered = values - jnp.mean(values, axis=-1, keepdims=True)
    return centered * lax.rsqrt(jnp.mean(centered * centered, axis=-1, keepdims=True) + EPS)


def norm_back(values, upstream):
    centered = values - jnp.mean(values, axis=-1, keepdims=True)
    inverse = lax.rsqrt(jnp.mean(centered * centered, axis=-1, keepdims=True) + EPS)
    normed = centered * inverse
    middle = upstream - jnp.mean(upstream, axis=-1, keepdims=True)
    middle = middle - normed * jnp.mean(upstream * normed, axis=-1, keepdims=True)
    return (inverse * middle, normed)


def matmul(left, right):
    return jnp.dot(left, right, preferred_element_type=jnp.float32)


def matmul_tn(left, right):
    return lax.dot_general(
        left, right, (((0,), (0,)), ((), ())), preferred_element_type=jnp.float32
    )


def matmul_nt(left, right):
    return lax.dot_general(
        left, right, (((1,), (1,)), ((), ())), preferred_element_type=jnp.float32
    )


def split_heads(values, head_dim):
    return values.reshape(values.shape[0], values.shape[1] // head_dim, head_dim)


def allowed_keys(piece_first, length, slots, seg_len):
    row_ids = lax.broadcasted_iota(jnp.int32, (seg_len, seg_len), 0)
    col_ids = lax.broadcasted_iota(jnp.int32, (seg_len, seg_len), 1)
    inside = (
        (row_ids >= piece_first)
        & (row_ids < piece_first + length)
        & (col_ids >= piece_first)
        & (col_ids < piece_first + length)
    )
    tokens = (col_ids <= row_ids) | inside
    return jnp.concatenate([jnp.ones((seg_len, slots), jnp.bool_), tokens], axis=1)


def head_scores(queries, key_rows, allowed, head_dim):
    scores = jnp.einsum(
        "qhe,khe->hqk",
        split_heads(queries, head_dim),
        split_heads(key_rows, head_dim),
        preferred_element_type=jnp.float32,
    ) * head_dim ** (-0.5)
    return jnp.where(allowed[None], scores, -1e30)


def attend_forward(queries, key_rows, value_rows, allowed, head_dim):
    scores = head_scores(queries, key_rows, allowed, head_dim)
    peak = jnp.max(scores, axis=-1, keepdims=True)
    log_total = peak + jnp.log(jnp.sum(jnp.exp(scores - peak), axis=-1, keepdims=True))
    soft_probs = jnp.exp(scores - log_total).astype(jnp.bfloat16)
    mixed_heads = jnp.einsum(
        "hqk,khe->qhe",
        soft_probs,
        split_heads(value_rows, head_dim),
        preferred_element_type=jnp.float32,
    )
    return (mixed_heads.reshape(queries.shape[0], -1).astype(jnp.bfloat16), log_total)


def attend_back(queries, key_rows, value_rows, allowed, log_total, grad_mixed, head_dim):
    scale_factor = head_dim ** (-0.5)
    soft_probs = jnp.exp(head_scores(queries, key_rows, allowed, head_dim) - log_total)
    grad_heads = split_heads(grad_mixed, head_dim)
    key_heads = split_heads(key_rows, head_dim)
    grad_values = jnp.einsum(
        "hqk,qhe->khe",
        soft_probs.astype(jnp.bfloat16),
        grad_heads,
        preferred_element_type=jnp.float32,
    )
    grad_probs = jnp.einsum(
        "qhe,khe->hqk",
        grad_heads,
        split_heads(value_rows, head_dim),
        preferred_element_type=jnp.float32,
    )
    grad_scores = soft_probs * (
        grad_probs - jnp.sum(soft_probs * grad_probs, axis=-1, keepdims=True)
    )
    grad_scores = grad_scores.astype(jnp.bfloat16)
    grad_queries = (
        jnp.einsum("hqk,khe->qhe", grad_scores, key_heads, preferred_element_type=jnp.float32)
        * scale_factor
    )
    grad_keys = (
        jnp.einsum(
            "hqk,qhe->khe",
            grad_scores,
            split_heads(queries, head_dim),
            preferred_element_type=jnp.float32,
        )
        * scale_factor
    )
    return (
        grad_queries.reshape(queries.shape[0], -1).astype(jnp.bfloat16),
        grad_keys.reshape(key_rows.shape[0], -1).astype(jnp.bfloat16),
        grad_values.reshape(key_rows.shape[0], -1).astype(jnp.bfloat16),
    )


def pick_row(array, slot_index):
    return lax.dynamic_index_in_dim(array, slot_index, 0, keepdims=False)


def store_at(buffer, new_value, slot_index, is_valid):
    old_value = lax.dynamic_index_in_dim(buffer, slot_index, 0, keepdims=False)
    return lax.dynamic_update_index_in_dim(
        buffer, jnp.where(is_valid, new_value, old_value), slot_index, 0
    )


def local(
    inputs,
    first_memory,
    piece_start,
    piece_len,
    w_query,
    w_key,
    w_value,
    w_out,
    w_up,
    w_down,
    u_query,
    u_key,
    u_value,
    u_out,
    u_gate,
    gain_attn,
    gain_ffn,
    gain_write,
    gate_bias,
    out_grad,
    memory_grad,
):
    tp_index = lax.axis_index("tp")
    ctx_index = lax.axis_index("ctx")
    tp_count = lax.axis_size("tp")
    ctx_count = lax.axis_size("ctx")
    seq_count, seg_len, width = inputs.shape
    slots = first_memory.shape[1]
    row_share = seg_len // tp_count
    head_width = width // tp_count
    head_dim = HEAD_DIM
    head_count = head_width // head_dim
    mem_share = slots // tp_count
    row_first = tp_index * row_share
    full_weights = (
        lax.all_gather(w_query, ("shard", "tp"), axis=0, tiled=True),
        lax.all_gather(w_key, ("shard", "tp"), axis=0, tiled=True),
        lax.all_gather(w_value, ("shard", "tp"), axis=0, tiled=True),
        lax.all_gather(w_out, ("shard", "tp"), axis=0, tiled=True),
        lax.all_gather(w_up, ("shard", "tp"), axis=0, tiled=True),
        lax.all_gather(w_down, ("shard", "tp"), axis=0, tiled=True),
        lax.all_gather(u_query, ("shard", "tp"), axis=0, tiled=True),
        lax.all_gather(u_key, ("shard", "tp"), axis=0, tiled=True),
        lax.all_gather(u_value, ("shard", "tp"), axis=0, tiled=True),
        lax.all_gather(u_out, ("shard", "tp"), axis=0, tiled=True),
        lax.all_gather(u_gate, ("shard", "tp"), axis=0, tiled=True),
    )
    (
        query_full,
        key_full,
        value_full,
        out_full,
        up_full,
        down_full,
        uq_full,
        uk_full,
        uv_full,
        uo_full,
        gate_full,
    ) = full_weights
    ff_width = up_full.shape[1]

    def head_cols(matrix):
        return lax.dynamic_slice_in_dim(matrix, tp_index * head_width, head_width, 1)

    def head_rows(matrix):
        return lax.dynamic_slice_in_dim(matrix, tp_index * head_width, head_width, 0)

    query_cols = head_cols(query_full)
    key_cols = head_cols(key_full)
    value_cols = head_cols(value_full)
    uq_cols = head_cols(uq_full)
    uk_cols = head_cols(uk_full)
    uv_cols = head_cols(uv_full)
    out_rows = head_rows(out_full)
    uo_rows = head_rows(uo_full)
    gate_rows = head_rows(gate_full)
    slot_mask = jnp.ones((slots, slots + seg_len), jnp.bool_)

    def forward_unit(x_seg, memory, allowed):
        x_full = x_seg.astype(jnp.float32)
        x_share = lax.dynamic_slice_in_dim(x_full, row_first, row_share, 0)
        enc_in = (norm_rows(jnp.concatenate([memory, x_full], axis=0)) * gain_attn).astype(
            jnp.bfloat16
        )
        queries = matmul(enc_in[slots:], query_cols).astype(jnp.bfloat16)
        key_rows = matmul(enc_in, key_cols).astype(jnp.bfloat16)
        value_rows = matmul(enc_in, value_cols).astype(jnp.bfloat16)
        mixed, lse_enc = attend_forward(queries, key_rows, value_rows, allowed, head_dim)
        attn_share = lax.psum_scatter(
            matmul(mixed, out_rows).astype(jnp.bfloat16), "tp", scatter_dimension=0, tiled=True
        ).astype(jnp.float32)
        after_share = x_share + attn_share
        ffn_in = (norm_rows(after_share) * gain_ffn).astype(jnp.bfloat16)
        pre_act = matmul(ffn_in, up_full)
        activ = jax.nn.gelu(pre_act, approximate=True).astype(jnp.bfloat16)
        out_share = after_share + matmul(activ, down_full)
        outputs = lax.all_gather(out_share.astype(jnp.bfloat16), "tp", axis=0, tiled=True).astype(
            out_share.dtype
        )
        write_in = (norm_rows(jnp.concatenate([memory, outputs], axis=0)) * gain_write).astype(
            jnp.bfloat16
        )
        slot_queries = matmul(write_in[:slots], uq_cols).astype(jnp.bfloat16)
        slot_keys = matmul(write_in, uk_cols).astype(jnp.bfloat16)
        slot_values = matmul(write_in, uv_cols).astype(jnp.bfloat16)
        written, lse_write = attend_forward(
            slot_queries, slot_keys, slot_values, slot_mask, head_dim
        )
        gate_in = lax.dynamic_slice_in_dim(write_in[:slots], tp_index * head_width, head_width, 1)
        update, gate_pre = (
            lax.psum(matmul(written, uo_rows).astype(jnp.bfloat16), "tp").astype(jnp.float32),
            lax.psum(matmul(gate_in, gate_rows).astype(jnp.bfloat16), "tp").astype(jnp.float32),
        )
        gate_open = jax.nn.sigmoid(gate_pre + gate_bias)
        new_memory = gate_open * memory + (1.0 - gate_open) * jnp.tanh(update)
        kept_now = (
            queries,
            key_rows,
            value_rows,
            lse_enc,
            mixed,
            attn_share,
            pre_act,
            outputs,
            slot_queries,
            slot_keys,
            slot_values,
            lse_write,
            written,
            update,
            gate_pre,
            memory,
        )
        return (new_memory, out_share, kept_now)

    def backward_unit(x_seg, grad_share, memory_cot, allowed, kept_now):
        (
            queries,
            key_rows,
            value_rows,
            lse_enc,
            mixed_keep,
            attn_share,
            pre_act,
            outputs,
            slot_queries,
            slot_keys,
            slot_values,
            lse_write,
            written,
            update,
            gate_pre,
            memory,
        ) = kept_now
        x_full = x_seg.astype(jnp.float32)
        x_share = lax.dynamic_slice_in_dim(x_full, row_first, row_share, 0)
        write_in = (norm_rows(jnp.concatenate([memory, outputs], axis=0)) * gain_write).astype(
            jnp.bfloat16
        )
        gate_open = jax.nn.sigmoid(gate_pre + gate_bias)
        squashed = jnp.tanh(update)
        grad_gate = memory_cot * (memory - squashed) * gate_open * (1.0 - gate_open)
        grad_update = (memory_cot * (1.0 - gate_open) * (1.0 - squashed * squashed)).astype(
            jnp.bfloat16
        )
        grad_gate_low = grad_gate.astype(jnp.bfloat16)
        gate_in = lax.dynamic_slice_in_dim(write_in[:slots], tp_index * head_width, head_width, 1)
        grad_uo = matmul_tn(written, grad_update)
        grad_ugate = matmul_tn(gate_in, grad_gate_low)
        grad_written = matmul_nt(grad_update, uo_rows).astype(jnp.bfloat16)
        grad_gate_in = matmul_nt(grad_gate_low, gate_rows)
        grad_sq, grad_sk, grad_sv = attend_back(
            slot_queries, slot_keys, slot_values, slot_mask, lse_write, grad_written, head_dim
        )
        grad_uq = matmul_tn(write_in[:slots], grad_sq)
        grad_uk = matmul_tn(write_in, grad_sk)
        grad_uv = matmul_tn(write_in, grad_sv)
        write_mem = (
            matmul_nt(grad_sq, uq_cols)
            + matmul_nt(grad_sk[:slots], uk_cols)
            + matmul_nt(grad_sv[:slots], uv_cols)
        )
        write_mem = write_mem + lax.dynamic_update_slice(
            jnp.zeros((slots, width), jnp.float32), grad_gate_in, (0, tp_index * head_width)
        )
        key_part = lax.dynamic_slice_in_dim(grad_sk, slots, lax.axis_size("tp") * row_share, 0)
        value_part = lax.dynamic_slice_in_dim(grad_sv, slots, lax.axis_size("tp") * row_share, 0)
        write_tok = lax.psum_scatter(
            (matmul_nt(key_part, uk_cols) + matmul_nt(value_part, uv_cols)).astype(jnp.bfloat16),
            "tp",
            scatter_dimension=0,
            tiled=True,
        ).astype(jnp.float32)
        out_share = lax.dynamic_slice_in_dim(outputs, row_first, row_share, 0)
        back_tok, normed_tok = norm_back(out_share, write_tok * gain_write)
        back_wmem, normed_wmem = norm_back(memory, write_mem * gain_write)
        grad_gain_write = jnp.sum(write_tok * normed_tok, axis=0) + jnp.sum(
            write_mem * normed_wmem, axis=0
        )
        grad_y = grad_share.astype(jnp.float32) + back_tok
        after_share = x_share + attn_share
        ffn_in = (norm_rows(after_share) * gain_ffn).astype(jnp.bfloat16)
        activ, gelu_pull = jax.vjp(partial(jax.nn.gelu, approximate=True), pre_act)
        grad_y_low = grad_y.astype(jnp.bfloat16)
        grad_down = matmul_tn(activ.astype(jnp.bfloat16), grad_y_low)
        grad_activ = matmul_nt(grad_y_low, down_full)
        grad_pre = gelu_pull(grad_activ)[0].astype(jnp.bfloat16)
        grad_up = matmul_tn(ffn_in, grad_pre)
        grad_ffn_in = matmul_nt(grad_pre, up_full)
        back_ffn, normed_ffn = norm_back(after_share, grad_ffn_in * gain_ffn)
        grad_gain_ffn = jnp.sum(grad_ffn_in * normed_ffn, axis=0)
        grad_after = grad_y + back_ffn
        grad_after_low = grad_after.astype(jnp.bfloat16)
        grad_attn = lax.all_gather(grad_after_low, "tp", axis=0, tiled=True)
        grad_out = lax.dynamic_update_slice(
            jnp.zeros((width, width), jnp.float32),
            matmul_tn(mixed_keep, grad_attn),
            (tp_index * head_width, 0),
        )
        grad_mixed = matmul_nt(grad_attn, out_rows).astype(jnp.bfloat16)
        grad_q, grad_k, grad_v = attend_back(
            queries, key_rows, value_rows, allowed, lse_enc, grad_mixed, head_dim
        )
        enc_in = (norm_rows(jnp.concatenate([memory, x_full], axis=0)) * gain_attn).astype(
            jnp.bfloat16
        )
        grad_wq = matmul_tn(enc_in[slots:], grad_q)
        grad_wk = matmul_tn(enc_in, grad_k)
        grad_wv = matmul_tn(enc_in, grad_v)
        enc_mem = matmul_nt(grad_k[:slots], key_cols) + matmul_nt(grad_v[:slots], value_cols)
        key_part = lax.dynamic_slice_in_dim(grad_k, slots, lax.axis_size("tp") * row_share, 0)
        value_part = lax.dynamic_slice_in_dim(grad_v, slots, lax.axis_size("tp") * row_share, 0)
        enc_tok = lax.psum_scatter(
            (
                matmul_nt(grad_q, query_cols)
                + matmul_nt(key_part, key_cols)
                + matmul_nt(value_part, value_cols)
            ).astype(jnp.bfloat16),
            "tp",
            scatter_dimension=0,
            tiled=True,
        ).astype(jnp.float32)
        back_x, normed_x = norm_back(x_share, enc_tok * gain_attn)
        back_emem, normed_emem = norm_back(memory, enc_mem * gain_attn)
        grad_gain_attn = jnp.sum(enc_tok * normed_x, axis=0) + jnp.sum(
            enc_mem * normed_emem, axis=0
        )
        grad_x = (grad_after + back_x).astype(jnp.bfloat16)
        mem_in_grad = (
            lax.psum((back_wmem + back_emem).astype(jnp.bfloat16), "tp").astype(jnp.float32)
            + memory_cot * gate_open
        )
        grad_bias = jnp.sum(
            lax.dynamic_slice_in_dim(grad_gate, tp_index * mem_share, mem_share, 0), axis=0
        )
        head_terms = (grad_wq, grad_wk, grad_wv, grad_uq, grad_uk, grad_uv, grad_uo, grad_ugate)
        row_terms = (
            grad_out,
            grad_up,
            grad_down,
            grad_gain_attn,
            grad_gain_ffn,
            grad_gain_write,
            grad_bias,
        )
        return (grad_x, mem_in_grad, head_terms, row_terms)

    mixed_dims = (seg_len, head_width)
    layout = [
        ((seg_len, head_width), jnp.bfloat16),
        ((slots + seg_len, head_width), jnp.bfloat16),
        ((slots + seg_len, head_width), jnp.bfloat16),
        ((head_count, seg_len, 1), jnp.float32),
        (mixed_dims, jnp.bfloat16),
        ((row_share, width), jnp.float32),
        ((row_share, ff_width), jnp.float32),
        ((seg_len, width), jnp.float32),
        ((slots, head_width), jnp.bfloat16),
        ((slots + seg_len, head_width), jnp.bfloat16),
        ((slots + seg_len, head_width), jnp.bfloat16),
        ((head_count, slots, 1), jnp.float32),
        ((slots, head_width), jnp.bfloat16),
        ((slots, width), jnp.float32),
        ((slots, width), jnp.float32),
        ((slots, width), jnp.float32),
    ]
    kept_init = tuple((jnp.zeros((seq_count,) + dims_of, type_of) for dims_of, type_of in layout))
    steps_total = seq_count + ctx_count - 1
    start_column = piece_start[:, 0]
    length_column = piece_len[:, 0]

    def forward_turn(turn_no, loop_state):
        previous, kept_bufs, memories_buf, outputs_buf = loop_state
        seq_order = turn_no - ctx_index
        is_valid = (seq_order >= 0) & (seq_order < seq_count)
        picked = jnp.clip(seq_order, 0, seq_count - 1)
        incoming = from_behind(previous.astype(jnp.bfloat16), "ctx", 1).astype(previous.dtype)
        memory = jnp.where(ctx_index == 0, pick_row(first_memory, picked), incoming)
        allowed = allowed_keys(
            pick_row(start_column, picked), pick_row(length_column, picked), slots, seg_len
        )
        new_memory, out_share, kept_now = forward_unit(pick_row(inputs, picked), memory, allowed)
        kept_bufs = tuple(
            (
                store_at(buffer_now, value_now, picked, is_valid)
                for buffer_now, value_now in zip(kept_bufs, kept_now)
            )
        )
        memories_buf = store_at(memories_buf, new_memory, picked, is_valid)
        outputs_buf = store_at(outputs_buf, out_share.astype(jnp.bfloat16), picked, is_valid)
        return (new_memory, kept_bufs, memories_buf, outputs_buf)

    forward_init = (
        jnp.zeros((slots, width), jnp.float32),
        kept_init,
        jnp.zeros((seq_count, slots, width), jnp.float32),
        jnp.zeros((seq_count, row_share, width), jnp.bfloat16),
    )
    last_memory, kept_bufs, memories_buf, outputs_buf = lax.fori_loop(
        0, steps_total, forward_turn, forward_init
    )

    def backward_turn(turn_no, loop_state):
        previous, head_sums, row_sums, input_grad_buf, memory_in_buf = loop_state
        seq_order = turn_no - (ctx_count - 1 - ctx_index)
        is_valid = (seq_order >= 0) & (seq_order < seq_count)
        picked = jnp.clip(seq_order, 0, seq_count - 1)
        incoming = from_behind(previous.astype(jnp.bfloat16), "ctx", -1).astype(previous.dtype)
        memory_cot = pick_row(memory_grad, picked) + incoming
        allowed = allowed_keys(
            pick_row(start_column, picked), pick_row(length_column, picked), slots, seg_len
        )
        kept_now = tuple((pick_row(buffer_now, picked) for buffer_now in kept_bufs))
        grad_x, mem_in_grad, head_terms, row_terms = backward_unit(
            pick_row(inputs, picked), pick_row(out_grad, picked), memory_cot, allowed, kept_now
        )
        head_sums = tuple(
            (
                acc_now + jnp.where(is_valid, term_now, 0.0)
                for acc_now, term_now in zip(head_sums, head_terms)
            )
        )
        row_sums = tuple(
            (
                acc_now + jnp.where(is_valid, term_now, 0.0)
                for acc_now, term_now in zip(row_sums, row_terms)
            )
        )
        input_grad_buf = store_at(input_grad_buf, grad_x, picked, is_valid)
        memory_in_buf = store_at(memory_in_buf, mem_in_grad, picked, is_valid)
        return (mem_in_grad, head_sums, row_sums, input_grad_buf, memory_in_buf)

    head_init = tuple((jnp.zeros((width, head_width), jnp.float32) for item_no in range(6))) + (
        jnp.zeros((head_width, width), jnp.float32),
        jnp.zeros((head_width, width), jnp.float32),
    )
    row_init = (
        jnp.zeros((width, width), jnp.float32),
        jnp.zeros((width, ff_width), jnp.float32),
        jnp.zeros((ff_width, width), jnp.float32),
    ) + tuple((jnp.zeros((width,), jnp.float32) for item_no in range(4)))
    backward_init = (
        jnp.zeros((slots, width), jnp.float32),
        head_init,
        row_init,
        jnp.zeros((seq_count, row_share, width), jnp.bfloat16),
        jnp.zeros((seq_count, slots, width), jnp.float32),
    )
    last_grad, head_sums, row_sums, input_grad_buf, memory_in_buf = lax.fori_loop(
        0, steps_total, backward_turn, backward_init
    )
    head_out = (
        lax.psum_scatter(head_sums[0], ("shard", "ctx"), scatter_dimension=0, tiled=True),
        lax.psum_scatter(head_sums[1], ("shard", "ctx"), scatter_dimension=0, tiled=True),
        lax.psum_scatter(head_sums[2], ("shard", "ctx"), scatter_dimension=0, tiled=True),
        lax.psum_scatter(head_sums[3], ("shard", "ctx"), scatter_dimension=0, tiled=True),
        lax.psum_scatter(head_sums[4], ("shard", "ctx"), scatter_dimension=0, tiled=True),
        lax.psum_scatter(head_sums[5], ("shard", "ctx"), scatter_dimension=0, tiled=True),
        lax.psum_scatter(head_sums[6], ("shard", "ctx"), scatter_dimension=1, tiled=True),
        lax.psum_scatter(head_sums[7], ("shard", "ctx"), scatter_dimension=1, tiled=True),
    )
    row_out = lax.psum_scatter(row_sums, ("shard", "ctx", "tp"), scatter_dimension=0, tiled=True)
    grad_wq, grad_wk, grad_wv, grad_uq, grad_uk, grad_uv, grad_uo, grad_ugate = head_out
    grad_out, grad_up, grad_down, grad_gain_attn, grad_gain_ffn, grad_gain_write, grad_bias = (
        row_out
    )
    return (
        outputs_buf,
        memories_buf,
        input_grad_buf,
        memory_in_buf,
        grad_wq,
        grad_wk,
        grad_wv,
        grad_out,
        grad_up,
        grad_down,
        grad_uq,
        grad_uk,
        grad_uv,
        grad_uo,
        grad_ugate,
        grad_gain_attn,
        grad_gain_ffn,
        grad_gain_write,
        grad_bias,
    )


def solution(mesh):
    placed = (
        P("shard", "ctx", None),
        P("shard", None, None),
        P("shard", "ctx"),
        P("shard", "ctx"),
        P(("shard", "tp"), None),
        P(("shard", "tp"), None),
        P(("shard", "tp"), None),
        P(("shard", "tp"), None),
        P(("shard", "tp"), None),
        P(("shard", "tp"), None),
        P(("shard", "tp"), None),
        P(("shard", "tp"), None),
        P(("shard", "tp"), None),
        P(("shard", "tp"), None),
        P(("shard", "tp"), None),
        P(),
        P(),
        P(),
        P(),
        P("shard", ("ctx", "tp"), None),
        P("shard", "ctx", None),
    )
    return jax.shard_map(
        local,
        mesh=mesh,
        in_specs=placed,
        out_specs=(
            P("shard", ("ctx", "tp"), None),
            P("shard", "ctx", None),
            P("shard", ("ctx", "tp"), None),
            P("shard", "ctx", None),
            P(("shard", "ctx"), "tp"),
            P(("shard", "ctx"), "tp"),
            P(("shard", "ctx"), "tp"),
            P(("shard", "ctx", "tp"), None),
            P(("shard", "ctx", "tp"), None),
            P(("shard", "ctx", "tp"), None),
            P(("shard", "ctx"), "tp"),
            P(("shard", "ctx"), "tp"),
            P(("shard", "ctx"), "tp"),
            P("tp", ("shard", "ctx")),
            P("tp", ("shard", "ctx")),
            P(("shard", "ctx", "tp")),
            P(("shard", "ctx", "tp")),
            P(("shard", "ctx", "tp")),
            P(("shard", "ctx", "tp")),
        ),
        check_vma=False,
    )
```

profile of v0, /device:TPU:0, one launch (start us, length us, event | category | flops | bytes accessed | tf_op | source)
XLA Modules:
  0.0 2524.0 jit_solution(6178373379626595032)
XLA Ops:
  8.9 25.0 all_gather.54
  34.6 19.9 all_gather.55
  55.2 21.1 all_gather.56
  77.0 19.6 all_gather.57
  97.2 21.4 all_gather.60
  119.3 18.9 all_gather.61
  138.8 20.4 all_gather.62
  159.9 18.9 all_gather.63
  179.4 20.5 all_gather.64
  218.8 607.0 %while.104 = (s32[]{:T(128)}, bf16[64,512]{1,0:T(8,128)(2,1)}, bf16[4,512,128]{1,2,0:T(8,128)(2,1)}, bf16[4,576,128]{2,1,0:T(8,128)(2,1)}, bf16[4,576,128]{2,1,0...) while((s32[]{:T(128)}, bf16[64,512]{1,0:T(8,128)(2,1)}, ...), condition=%wide.region_14.15_spmd.clone, body=%wide.region_0.14_spmd.clone.sunk | while | flops 1189498112 | bytes 77861680 | solution.py:463
  264.5 6.8 reduce-scatter.37.cloned.1.call-done
  278.6 6.8 all_gather.69
  304.6 30.7 %all-reduce.13.cloned.1.call-done = (bf16[64,512]{1,0:T(8,128)(2,1)}, bf16[64,512]{1,0:T(8,128)(2,1)}) async-done(((bf16[64,512]{1,0:T(8,128)(2,1)}, bf16[64,512]{1,0:T(8,128)(2,1)}), (bf16[64,512]{1,0:T(8,128)(2,1)}, bf16[64,512]{1,0:T(8,128)(2,1)})) %all-reduce.13.cloned.1.call-update) | async-done | bytes 131088 | tf_op jit(solution)/shard_map/while/body/eval_jaxpr/psum | solution.py:255
  383.7 9.9 reduce-scatter.37.cloned.1.call-done
  400.8 6.8 all_gather.69
  426.8 30.8 %all-reduce.13.cloned.1.call-done = (bf16[64,512]{1,0:T(8,128)(2,1)}, bf16[64,512]{1,0:T(8,128)(2,1)}) async-done(((bf16[64,512]{1,0:T(8,128)(2,1)}, bf16[64,512]{1,0:T(8,128)(2,1)}), (bf16[64,512]{1,0:T(8,128)(2,1)}, bf16[64,512]{1,0:T(8,128)(2,1)})) %all-reduce.13.cloned.1.call-update) | async-done | bytes 131088 | tf_op jit(solution)/shard_map/while/body/eval_jaxpr/psum | solution.py:255
  506.0 9.8 reduce-scatter.37.cloned.1.call-done
  523.0 6.8 all_gather.69
  549.0 30.7 %all-reduce.13.cloned.1.call-done = (bf16[64,512]{1,0:T(8,128)(2,1)}, bf16[64,512]{1,0:T(8,128)(2,1)}) async-done(((bf16[64,512]{1,0:T(8,128)(2,1)}, bf16[64,512]{1,0:T(8,128)(2,1)}), (bf16[64,512]{1,0:T(8,128)(2,1)}, bf16[64,512]{1,0:T(8,128)(2,1)})) %all-reduce.13.cloned.1.call-update) | async-done | bytes 131088 | tf_op jit(solution)/shard_map/while/body/eval_jaxpr/psum | solution.py:255
  628.2 9.9 reduce-scatter.37.cloned.1.call-done
  645.3 6.8 all_gather.69
  671.2 30.7 %all-reduce.13.cloned.1.call-done = (bf16[64,512]{1,0:T(8,128)(2,1)}, bf16[64,512]{1,0:T(8,128)(2,1)}) async-done(((bf16[64,512]{1,0:T(8,128)(2,1)}, bf16[64,512]{1,0:T(8,128)(2,1)}), (bf16[64,512]{1,0:T(8,128)(2,1)}, bf16[64,512]{1,0:T(8,128)(2,1)})) %all-reduce.13.cloned.1.call-update) | async-done | bytes 131088 | tf_op jit(solution)/shard_map/while/body/eval_jaxpr/psum | solution.py:255
  750.3 9.9 reduce-scatter.37.cloned.1.call-done
  767.4 6.8 all_gather.69
  793.3 30.7 %all-reduce.13.cloned.1.call-done = (bf16[64,512]{1,0:T(8,128)(2,1)}, bf16[64,512]{1,0:T(8,128)(2,1)}) async-done(((bf16[64,512]{1,0:T(8,128)(2,1)}, bf16[64,512]{1,0:T(8,128)(2,1)}), (bf16[64,512]{1,0:T(8,128)(2,1)}, bf16[64,512]{1,0:T(8,128)(2,1)})) %all-reduce.13.cloned.1.call-update) | async-done | bytes 131088 | tf_op jit(solution)/shard_map/while/body/eval_jaxpr/psum | solution.py:255
  828.6 758.1 %while.105 = (s32[]{:T(128)}, bf16[64,512]{1,0:T(8,128)(2,1)S(1)}, f32[512,128]{1,0:T(8,128)}, f32[512,128]{1,0:T(8,128)}, f32[512,128]{1,0:T(8,128)}, /*index=5...) while((s32[]{:T(128)}, bf16[64,512]{1,0:T(8,128)(2,1)S(1)}, ...), condition=%wide.region_49.50_spmd.clone, body=%wide.region_15.49_spmd.clone.sunk | while | flops 2460809216 | bytes 153924048 | solution.py:513
  880.1 14.0 reduce-scatter.39.cloned.1.call-done
  902.8 6.9 all_gather.70
  938.9 13.2 all-reduce.15.cloned.1.call-done
  953.8 22.4 reduce-scatter.41.cloned.1.call-done
  1033.5 12.2 reduce-scatter.39.cloned.1.call-done
  1054.4 6.9 all_gather.70
  1085.2 5.8 select_add_fusion.13
  1091.0 5.1 select_add_fusion.12
  1096.1 7.5 all-reduce.15.cloned.1.call-done
  1105.4 22.4 reduce-scatter.41.cloned.1.call-done
  1185.0 12.2 reduce-scatter.39.cloned.1.call-done
  1205.9 6.9 all_gather.70
  1236.7 5.8 select_add_fusion.13
  1242.5 5.1 select_add_fusion.12
  1247.6 7.5 all-reduce.15.cloned.1.call-done
  1256.9 22.6 reduce-scatter.41.cloned.1.call-done
  1336.7 12.2 reduce-scatter.39.cloned.1.call-done
  1357.6 6.9 all_gather.70
  1388.4 5.8 select_add_fusion.13
  1399.3 7.5 all-reduce.15.cloned.1.call-done
  1408.6 22.4 reduce-scatter.41.cloned.1.call-done
  1488.2 12.2 reduce-scatter.39.cloned.1.call-done
  1509.1 6.9 all_gather.70
  1540.0 5.8 select_add_fusion.13
  1550.8 7.5 all-reduce.15.cloned.1.call-done
  1560.1 22.4 reduce-scatter.41.cloned.1.call-done
  1595.7 39.5 %all-reduce.7 = (f32[512]{0:T(512)S(1)}, f32[512]{0:T(512)S(1)}, f32[512]{0:T(512)S(1)}, f32[512]{0:T(512)S(1)}) all-reduce(f32[512]{0:T(512)S(1)} %copy-done.82, f32[512]{0:T(512)S(1)} %copy-done.80, f32[512]{0:T(512)S(1)} %copy-done.85, f32[512]{0:T(512)S(1)} %copy-done.81), channel_id=16, replica_groups=mesh['shard'=4,'ctx'=2,'tp'=4] {'shard','ctx','tp'}, use_global_device_ids=true, to_apply=%region_61.62.clone | all-reduce | flops 2048 | bytes 16384
  1637.5 15.3 reduce-scatter.15.cloned.1.call-done
  1652.8 64.2 %reduce-scatter.17.cloned.1.call-done = f32[64,128]{1,0:T(8,128)} async-done(((f32[512,128]{1,0:T(8,128)}), f32[64,128]{1,0:T(8,128)}) %reduce-scatter.17.cloned.1.call-update) | async-done | bytes 32784 | tf_op jit(solution)/shard_map/reduce_scatter | solution.py:518
  1717.0 64.0 %reduce-scatter.19.cloned.1.call-done = f32[64,128]{1,0:T(8,128)} async-done(((f32[512,128]{1,0:T(8,128)}), f32[64,128]{1,0:T(8,128)}) %reduce-scatter.19.cloned.1.call-update) | async-done | bytes 32784 | tf_op jit(solution)/shard_map/reduce_scatter | solution.py:519
  1781.0 64.1 %reduce-scatter.27.cloned.1.call-done = f32[64,128]{1,0:T(8,128)} async-done(((f32[512,128]{1,0:T(8,128)}), f32[64,128]{1,0:T(8,128)}) %reduce-scatter.27.cloned.1.call-update) | async-done | bytes 32784 | tf_op jit(solution)/shard_map/reduce_scatter | solution.py:520
  1845.1 64.2 %reduce-scatter.29.cloned.1.call-done = f32[64,128]{1,0:T(8,128)} async-done(((f32[512,128]{1,0:T(8,128)}), f32[64,128]{1,0:T(8,128)}) %reduce-scatter.29.cloned.1.call-update) | async-done | bytes 32784 | tf_op jit(solution)/shard_map/reduce_scatter | solution.py:521
  1909.3 64.0 %reduce-scatter.31.cloned.1.call-done = f32[64,128]{1,0:T(8,128)} async-done(((f32[512,128]{1,0:T(8,128)}), f32[64,128]{1,0:T(8,128)}) %reduce-scatter.31.cloned.1.call-update) | async-done | bytes 32784 | tf_op jit(solution)/shard_map/reduce_scatter | solution.py:522
  1973.3 64.2 %reduce-scatter.33.cloned.1.call-done = f32[128,64]{0,1:T(8,128)} async-done(((f32[128,512]{0,1:T(8,128)}), f32[128,64]{0,1:T(8,128)}) %reduce-scatter.33.cloned.1.call-update) | async-done | bytes 32784 | tf_op jit(solution)/shard_map/reduce_scatter | solution.py:523
  2037.5 64.2 %reduce-scatter.35.cloned.1.call-done = f32[128,64]{0,1:T(8,128)} async-done(((f32[128,512]{0,1:T(8,128)}), f32[128,64]{0,1:T(8,128)}) %reduce-scatter.35.cloned.1.call-update) | async-done | bytes 32784 | tf_op jit(solution)/shard_map/reduce_scatter | solution.py:524
  2101.7 136.5 %reduce-scatter.21.cloned.1.call-done = f32[16,512]{1,0:T(8,128)} async-done(((f32[512,512]{1,0:T(8,128)}), f32[16,512]{1,0:T(8,128)}) %reduce-scatter.21.cloned.1.call-update) | async-done | bytes 32784 | tf_op jit(solution)/shard_map/reduce_scatter | solution.py:526
  2238.2 139.6 %reduce-scatter.23.cloned.1.call-done = f32[16,2048]{1,0:T(8,128)} async-done(((f32[512,2048]{1,0:T(8,128)}), f32[16,2048]{1,0:T(8,128)}) %reduce-scatter.23.cloned.1.call-update) | async-done | bytes 131088 | tf_op jit(solution)/shard_map/reduce_scatter | solution.py:526
  2377.8 139.7 %reduce-scatter.25.cloned.1.call-done = f32[64,512]{1,0:T(8,128)} async-done(((f32[2048,512]{1,0:T(8,128)}), f32[64,512]{1,0:T(8,128)}) %reduce-scatter.25.cloned.1.call-update) | async-done | bytes 131088 | tf_op jit(solution)/shard_map/reduce_scatter | solution.py:526
  (1895 shorter events, 864.6 us)
Async XLA Ops:
  7.2 69.8 %copy-start.91 = (bf16[32,512]{1,0:T(8,128)(2,1)S(1)}, bf16[32,512]{1,0:T(8,128)(2,1)}, u32[]{:S(2)}) copy-start(bf16[32,512]{1,0:T(8,128)(2,1)} %param.32) | copy-start | bytes 98308
  7.2 90.0 %copy-start.92 = (bf16[32,512]{1,0:T(8,128)(2,1)S(1)}, bf16[32,512]{1,0:T(8,128)(2,1)}, u32[]{:S(2)}) copy-start(bf16[32,512]{1,0:T(8,128)(2,1)} %param.39) | copy-start | bytes 98308
  7.2 193.3 %all-gather.3.cloned.1.call-start = ((), (), s32[]{:S(2)}) async-start(), calls=%async_computation.14 | async-start | bytes 2228224 | tf_op jit(solution)/shard_map/all_gather | solution.py:183
  7.9 192.6 %all-gather.5.cloned.1.call-start = ((), (), s32[]{:S(2)}) async-start(), calls=%async_computation.15 | async-start | bytes 2228224 | tf_op jit(solution)/shard_map/all_gather | solution.py:184
  8.7 110.6 %copy-start.93 = (bf16[32,512]{1,0:T(8,128)(2,1)S(1)}, bf16[32,512]{1,0:T(8,128)(2,1)}, u32[]{:S(2)}) copy-start(bf16[32,512]{1,0:T(8,128)(2,1)} %param.37) | copy-start | bytes 98308
  34.6 104.2 %copy-start.94 = (bf16[32,512]{1,0:T(8,128)(2,1)S(1)}, bf16[32,512]{1,0:T(8,128)(2,1)}, u32[]{:S(2)}) copy-start(bf16[32,512]{1,0:T(8,128)(2,1)} %param.35) | copy-start | bytes 98308
  55.2 104.7 %copy-start.95 = (bf16[32,512]{1,0:T(8,128)(2,1)S(1)}, bf16[32,512]{1,0:T(8,128)(2,1)}, u32[]{:S(2)}) copy-start(bf16[32,512]{1,0:T(8,128)(2,1)} %param.36) | copy-start | bytes 98308
  77.0 102.4 %copy-start.96 = (bf16[32,512]{1,0:T(8,128)(2,1)S(1)}, bf16[32,512]{1,0:T(8,128)(2,1)}, u32[]{:S(2)}) copy-start(bf16[32,512]{1,0:T(8,128)(2,1)} %param.38) | copy-start | bytes 98308
  218.8 52.5 %reduce-scatter.37.cloned.1.call-start = ((), (), s32[]{:S(2)}) async-start(), calls=%async_computation.27 | async-start | bytes 655360 | tf_op jit(solution)/shard_map/while/body/eval_jaxpr/reduce_scatter | solution.py:233
  218.8 19.8 collective-permute-start
  253.4 81.9 %all-reduce.13.cloned.1.call-start = ((), (), s32[]{:S(2)}) async-start(), calls=%async_computation.28 | async-start | bytes 262144 | tf_op jit(solution)/shard_map/while/body/eval_jaxpr/psum | solution.py:255
  337.1 56.5 %reduce-scatter.37.cloned.1.call-start = ((), (), s32[]{:S(2)}) async-start(), calls=%async_computation.27 | async-start | bytes 655360 | tf_op jit(solution)/shard_map/while/body/eval_jaxpr/reduce_scatter | solution.py:233
  337.9 19.8 collective-permute-start
  372.6 85.0 %all-reduce.13.cloned.1.call-start = ((), (), s32[]{:S(2)}) async-start(), calls=%async_computation.28 | async-start | bytes 262144 | tf_op jit(solution)/shard_map/while/body/eval_jaxpr/psum | solution.py:255
  459.4 56.4 %reduce-scatter.37.cloned.1.call-start = ((), (), s32[]{:S(2)}) async-start(), calls=%async_computation.27 | async-start | bytes 655360 | tf_op jit(solution)/shard_map/while/body/eval_jaxpr/reduce_scatter | solution.py:233
  460.2 19.8 collective-permute-start
  494.9 84.8 %all-reduce.13.cloned.1.call-start = ((), (), s32[]{:S(2)}) async-start(), calls=%async_computation.28 | async-start | bytes 262144 | tf_op jit(solution)/shard_map/while/body/eval_jaxpr/psum | solution.py:255
  581.5 56.5 %reduce-scatter.37.cloned.1.call-start = ((), (), s32[]{:S(2)}) async-start(), calls=%async_computation.27 | async-start | bytes 655360 | tf_op jit(solution)/shard_map/while/body/eval_jaxpr/reduce_scatter | solution.py:233
  582.4 19.9 collective-permute-start
  617.1 84.8 %all-reduce.13.cloned.1.call-start = ((), (), s32[]{:S(2)}) async-start(), calls=%async_computation.28 | async-start | bytes 262144 | tf_op jit(solution)/shard_map/while/body/eval_jaxpr/psum | solution.py:255
  703.7 56.5 %reduce-scatter.37.cloned.1.call-start = ((), (), s32[]{:S(2)}) async-start(), calls=%async_computation.27 | async-start | bytes 655360 | tf_op jit(solution)/shard_map/while/body/eval_jaxpr/reduce_scatter | solution.py:233
  704.5 19.9 collective-permute-start
  739.2 84.8 %all-reduce.13.cloned.1.call-start = ((), (), s32[]{:S(2)}) async-start(), calls=%async_computation.28 | async-start | bytes 262144 | tf_op jit(solution)/shard_map/while/body/eval_jaxpr/psum | solution.py:255
  828.9 65.2 %reduce-scatter.39.cloned.1.call-start = ((), (), s32[]{:S(2)}) async-start(), calls=%async_computation.29 | async-start | bytes 655360 | tf_op jit(solution)/shard_map/while/body/eval_jaxpr/reduce_scatter | solution.py:332
  829.7 33.6 %collective-permute-start.1 = (bf16[64,512]{1,0:T(8,128)(2,1)}, bf16[64,512]{1,0:T(8,128)(2,1)}, u32[]{:S(2)}, u32[]{:S(2)}) collective-permute-start(bf16[64,512]{1,0:T(8,128)(2,1)} %select_convert_fusion.5), channel_id=1, source_target_pairs={{4,0},{5,1},{6,2},{7,3},{12,8},{13,9},{14,10},{15,11},{20,16},{21,... | collective-permute-start | bytes 196616 | tf_op jit(solution)/shard_map/while/body/eval_jaxpr/ppermute | solution.py:17
  856.2 55.4 %copy-start.13 = (bf16[1,576,128]{1,2,0:T(8,128)(2,1)}, bf16[1,576,128]{1,2,0:T(8,128)(2,1)S(1)}, u32[]{:S(2)}) copy-start(bf16[1,576,128]{1,2,0:T(8,128)(2,1)S(1)} %copy.132) | copy-start | bytes 442372 | tf_op jit(solution)/shard_map/while
  870.6 81.5 %all-reduce.15.cloned.1.call-start = ((), (), s32[]{:S(2)}) async-start(), calls=%async_computation.30 | async-start | bytes 131072 | tf_op jit(solution)/shard_map/while/body/eval_jaxpr/psum | solution.py:394
  920.5 55.8 %reduce-scatter.41.cloned.1.call-start = ((), (), s32[]{:S(2)}) async-start(), calls=%async_computation.31 | async-start | bytes 655360 | tf_op jit(solution)/shard_map/while/body/eval_jaxpr/reduce_scatter | solution.py:377
  936.1 44.4 %copy-start.17 = (bf16[512,128]{1,0:T(8,128)(2,1)S(1)}, bf16[512,128]{1,0:T(8,128)(2,1)}, u32[]{:S(2)}) copy-start(bf16[512,128]{1,0:T(8,128)(2,1)} %get-tuple-element.4712) | copy-start | bytes 393220 | tf_op jit(solution)/shard_map/while
  980.5 65.2 %reduce-scatter.39.cloned.1.call-start = ((), (), s32[]{:S(2)}) async-start(), calls=%async_computation.29 | async-start | bytes 655360 | tf_op jit(solution)/shard_map/while/body/eval_jaxpr/reduce_scatter | solution.py:332
  981.2 33.6 %collective-permute-start.1 = (bf16[64,512]{1,0:T(8,128)(2,1)}, bf16[64,512]{1,0:T(8,128)(2,1)}, u32[]{:S(2)}, u32[]{:S(2)}) collective-permute-start(bf16[64,512]{1,0:T(8,128)(2,1)} %select_convert_fusion.5), channel_id=1, source_target_pairs={{4,0},{5,1},{6,2},{7,3},{12,8},{13,9},{14,10},{15,11},{20,16},{21,... | collective-permute-start | bytes 196616 | tf_op jit(solution)/shard_map/while/body/eval_jaxpr/ppermute | solution.py:17
  1007.7 55.5 %copy-start.13 = (bf16[1,576,128]{1,2,0:T(8,128)(2,1)}, bf16[1,576,128]{1,2,0:T(8,128)(2,1)S(1)}, u32[]{:S(2)}) copy-start(bf16[1,576,128]{1,2,0:T(8,128)(2,1)S(1)} %copy.132) | copy-start | bytes 442372 | tf_op jit(solution)/shard_map/while
  1022.1 81.5 %all-reduce.15.cloned.1.call-start = ((), (), s32[]{:S(2)}) async-start(), calls=%async_computation.30 | async-start | bytes 131072 | tf_op jit(solution)/shard_map/while/body/eval_jaxpr/psum | solution.py:394
  1072.0 55.8 %reduce-scatter.41.cloned.1.call-start = ((), (), s32[]{:S(2)}) async-start(), calls=%async_computation.31 | async-start | bytes 655360 | tf_op jit(solution)/shard_map/while/body/eval_jaxpr/reduce_scatter | solution.py:377
  1091.0 41.0 %copy-start.17 = (bf16[512,128]{1,0:T(8,128)(2,1)S(1)}, bf16[512,128]{1,0:T(8,128)(2,1)}, u32[]{:S(2)}) copy-start(bf16[512,128]{1,0:T(8,128)(2,1)} %get-tuple-element.4712) | copy-start | bytes 393220 | tf_op jit(solution)/shard_map/while
  1132.0 65.2 %reduce-scatter.39.cloned.1.call-start = ((), (), s32[]{:S(2)}) async-start(), calls=%async_computation.29 | async-start | bytes 655360 | tf_op jit(solution)/shard_map/while/body/eval_jaxpr/reduce_scatter | solution.py:332
  1132.8 33.6 %collective-permute-start.1 = (bf16[64,512]{1,0:T(8,128)(2,1)}, bf16[64,512]{1,0:T(8,128)(2,1)}, u32[]{:S(2)}, u32[]{:S(2)}) collective-permute-start(bf16[64,512]{1,0:T(8,128)(2,1)} %select_convert_fusion.5), channel_id=1, source_target_pairs={{4,0},{5,1},{6,2},{7,3},{12,8},{13,9},{14,10},{15,11},{20,16},{21,... | collective-permute-start | bytes 196616 | tf_op jit(solution)/shard_map/while/body/eval_jaxpr/ppermute | solution.py:17
  1159.2 55.5 %copy-start.13 = (bf16[1,576,128]{1,2,0:T(8,128)(2,1)}, bf16[1,576,128]{1,2,0:T(8,128)(2,1)S(1)}, u32[]{:S(2)}) copy-start(bf16[1,576,128]{1,2,0:T(8,128)(2,1)S(1)} %copy.132) | copy-start | bytes 442372 | tf_op jit(solution)/shard_map/while
  1173.6 81.5 %all-reduce.15.cloned.1.call-start = ((), (), s32[]{:S(2)}) async-start(), calls=%async_computation.30 | async-start | bytes 131072 | tf_op jit(solution)/shard_map/while/body/eval_jaxpr/psum | solution.py:394
  1223.5 55.9 %reduce-scatter.41.cloned.1.call-start = ((), (), s32[]{:S(2)}) async-start(), calls=%async_computation.31 | async-start | bytes 655360 | tf_op jit(solution)/shard_map/while/body/eval_jaxpr/reduce_scatter | solution.py:377
  1242.5 41.2 %copy-start.17 = (bf16[512,128]{1,0:T(8,128)(2,1)S(1)}, bf16[512,128]{1,0:T(8,128)(2,1)}, u32[]{:S(2)}) copy-start(bf16[512,128]{1,0:T(8,128)(2,1)} %get-tuple-element.4712) | copy-start | bytes 393220 | tf_op jit(solution)/shard_map/while
  1283.7 65.2 %reduce-scatter.39.cloned.1.call-start = ((), (), s32[]{:S(2)}) async-start(), calls=%async_computation.29 | async-start | bytes 655360 | tf_op jit(solution)/shard_map/while/body/eval_jaxpr/reduce_scatter | solution.py:332
  1284.5 33.6 %collective-permute-start.1 = (bf16[64,512]{1,0:T(8,128)(2,1)}, bf16[64,512]{1,0:T(8,128)(2,1)}, u32[]{:S(2)}, u32[]{:S(2)}) collective-permute-start(bf16[64,512]{1,0:T(8,128)(2,1)} %select_convert_fusion.5), channel_id=1, source_target_pairs={{4,0},{5,1},{6,2},{7,3},{12,8},{13,9},{14,10},{15,11},{20,16},{21,... | collective-permute-start | bytes 196616 | tf_op jit(solution)/shard_map/while/body/eval_jaxpr/ppermute | solution.py:17
  1310.9 55.5 %copy-start.13 = (bf16[1,576,128]{1,2,0:T(8,128)(2,1)}, bf16[1,576,128]{1,2,0:T(8,128)(2,1)S(1)}, u32[]{:S(2)}) copy-start(bf16[1,576,128]{1,2,0:T(8,128)(2,1)S(1)} %copy.132) | copy-start | bytes 442372 | tf_op jit(solution)/shard_map/while
  1325.3 81.5 %all-reduce.15.cloned.1.call-start = ((), (), s32[]{:S(2)}) async-start(), calls=%async_computation.30 | async-start | bytes 131072 | tf_op jit(solution)/shard_map/while/body/eval_jaxpr/psum | solution.py:394
  1375.2 55.8 %reduce-scatter.41.cloned.1.call-start = ((), (), s32[]{:S(2)}) async-start(), calls=%async_computation.31 | async-start | bytes 655360 | tf_op jit(solution)/shard_map/while/body/eval_jaxpr/reduce_scatter | solution.py:377
  1394.2 41.0 %copy-start.17 = (bf16[512,128]{1,0:T(8,128)(2,1)S(1)}, bf16[512,128]{1,0:T(8,128)(2,1)}, u32[]{:S(2)}) copy-start(bf16[512,128]{1,0:T(8,128)(2,1)} %get-tuple-element.4712) | copy-start | bytes 393220 | tf_op jit(solution)/shard_map/while
  1435.2 65.2 %reduce-scatter.39.cloned.1.call-start = ((), (), s32[]{:S(2)}) async-start(), calls=%async_computation.29 | async-start | bytes 655360 | tf_op jit(solution)/shard_map/while/body/eval_jaxpr/reduce_scatter | solution.py:332
  1436.0 33.6 %collective-permute-start.1 = (bf16[64,512]{1,0:T(8,128)(2,1)}, bf16[64,512]{1,0:T(8,128)(2,1)}, u32[]{:S(2)}, u32[]{:S(2)}) collective-permute-start(bf16[64,512]{1,0:T(8,128)(2,1)} %select_convert_fusion.5), channel_id=1, source_target_pairs={{4,0},{5,1},{6,2},{7,3},{12,8},{13,9},{14,10},{15,11},{20,16},{21,... | collective-permute-start | bytes 196616 | tf_op jit(solution)/shard_map/while/body/eval_jaxpr/ppermute | solution.py:17
  1462.5 55.5 %copy-start.13 = (bf16[1,576,128]{1,2,0:T(8,128)(2,1)}, bf16[1,576,128]{1,2,0:T(8,128)(2,1)S(1)}, u32[]{:S(2)}) copy-start(bf16[1,576,128]{1,2,0:T(8,128)(2,1)S(1)} %copy.132) | copy-start | bytes 442372 | tf_op jit(solution)/shard_map/while
  1476.8 81.5 %all-reduce.15.cloned.1.call-start = ((), (), s32[]{:S(2)}) async-start(), calls=%async_computation.30 | async-start | bytes 131072 | tf_op jit(solution)/shard_map/while/body/eval_jaxpr/psum | solution.py:394
  1526.8 55.8 %reduce-scatter.41.cloned.1.call-start = ((), (), s32[]{:S(2)}) async-start(), calls=%async_computation.31 | async-start | bytes 655360 | tf_op jit(solution)/shard_map/while/body/eval_jaxpr/reduce_scatter | solution.py:377
  1545.8 41.0 %copy-start.17 = (bf16[512,128]{1,0:T(8,128)(2,1)S(1)}, bf16[512,128]{1,0:T(8,128)(2,1)}, u32[]{:S(2)}) copy-start(bf16[512,128]{1,0:T(8,128)(2,1)} %get-tuple-element.4712) | copy-start | bytes 393220 | tf_op jit(solution)/shard_map/while
  1586.8 66.0 %reduce-scatter.15.cloned.1.call-start = ((), (), s32[]{:S(2)}) async-start(), calls=%async_computation.16 | async-start | bytes 294912 | tf_op jit(solution)/shard_map/reduce_scatter | solution.py:517
  1587.5 129.5 %reduce-scatter.17.cloned.1.call-start = ((), (), s32[]{:S(2)}) async-start(), calls=%async_computation.17 | async-start | bytes 294912 | tf_op jit(solution)/shard_map/reduce_scatter | solution.py:518
  1588.3 192.7 %reduce-scatter.19.cloned.1.call-start = ((), (), s32[]{:S(2)}) async-start(), calls=%async_computation.18 | async-start | bytes 294912 | tf_op jit(solution)/shard_map/reduce_scatter | solution.py:519
  1588.8 256.2 %reduce-scatter.27.cloned.1.call-start = ((), (), s32[]{:S(2)}) async-start(), calls=%async_computation.22 | async-start | bytes 294912 | tf_op jit(solution)/shard_map/reduce_scatter | solution.py:520
  1589.6 319.7 %reduce-scatter.29.cloned.1.call-start = ((), (), s32[]{:S(2)}) async-start(), calls=%async_computation.23 | async-start | bytes 294912 | tf_op jit(solution)/shard_map/reduce_scatter | solution.py:521
  1590.3 383.0 %reduce-scatter.31.cloned.1.call-start = ((), (), s32[]{:S(2)}) async-start(), calls=%async_computation.24 | async-start | bytes 294912 | tf_op jit(solution)/shard_map/reduce_scatter | solution.py:522
  1590.9 446.6 %reduce-scatter.33.cloned.1.call-start = ((), (), s32[]{:S(2)}) async-start(), calls=%async_computation.25 | async-start | bytes 294912 | tf_op jit(solution)/shard_map/reduce_scatter | solution.py:523
  1592.8 508.9 %reduce-scatter.35.cloned.1.call-start = ((), (), s32[]{:S(2)}) async-start(), calls=%async_computation.26 | async-start | bytes 294912 | tf_op jit(solution)/shard_map/reduce_scatter | solution.py:524
  1593.7 644.6 %reduce-scatter.21.cloned.1.call-start = ((), (), s32[]{:S(2)}) async-start(), calls=%async_computation.19 | async-start | bytes 1081344 | tf_op jit(solution)/shard_map/reduce_scatter | solution.py:526
  1594.3 783.5 %reduce-scatter.23.cloned.1.call-start = ((), (), s32[]{:S(2)}) async-start(), calls=%async_computation.20 | async-start | bytes 4325376 | tf_op jit(solution)/shard_map/reduce_scatter | solution.py:526
  1594.9 922.6 %reduce-scatter.25.cloned.1.call-start = ((), (), s32[]{:S(2)}) async-start(), calls=%async_computation.21 | async-start | bytes 4325376 | tf_op jit(solution)/shard_map/reduce_scatter | solution.py:526
  (407 other events, 3080.8 us)
Sparse Core Ops, SparseCore 0:
  10.2 45.7 all-gather.2
  58.2 44.0 all-gather.4
  253.5 17.6 reduce-scatter.36
  303.4 31.9 all-reduce.12
  372.8 20.7 reduce-scatter.36
  425.6 31.9 all-reduce.12
  495.1 20.7 reduce-scatter.36
  547.8 31.8 all-reduce.12
  617.2 20.7 reduce-scatter.36
  670.0 31.8 all-reduce.12
  739.4 20.7 reduce-scatter.36
  792.1 31.8 all-reduce.12
  870.7 23.4 reduce-scatter.38
  920.6 31.4 all-reduce.14
  954.5 21.6 reduce-scatter.40
  1022.2 23.4 reduce-scatter.38
  1072.1 31.4 all-reduce.14
  1106.1 21.6 reduce-scatter.40
  1173.7 23.4 reduce-scatter.38
  1223.6 31.4 all-reduce.14
  1257.8 21.6 reduce-scatter.40
  1325.4 23.4 reduce-scatter.38
  1375.3 31.4 all-reduce.14
  1409.3 21.6 reduce-scatter.40
  1477.0 23.4 reduce-scatter.38
  1526.9 31.4 all-reduce.14
  1560.8 21.6 reduce-scatter.40
  1591.5 61.2 reduce-scatter.14
  1656.7 60.2 reduce-scatter.16
  1720.7 60.1 reduce-scatter.18
  1784.9 60.1 reduce-scatter.26
  1849.0 60.2 reduce-scatter.28
  1913.0 60.2 reduce-scatter.30
  1977.2 60.2 reduce-scatter.32
  2041.4 60.2 reduce-scatter.34
  2104.4 133.8 reduce-scatter.20
  2241.0 136.7 reduce-scatter.22
  2380.8 136.6 reduce-scatter.24
where the time goes:
time: 2530 us; the launch traced here: 2520 us
  waiting for transfers between devices  1310 us (52%)
  matrix products  359 us (14%)
  blocking collectives  294 us (12%)
  local copies, waits for them, and re-layouts  274 us (11%)
  other arithmetic  230 us (9%)
  starting transfers between devices  27.6 us (1%)
    reduce_scatter x3, waiting for transfers between devices, local(): lax.psum_scatter(row_sums, ('shard', 'ctx', 'tp'), scatter_dimension=0, t...  416 us
    psum x5, waiting for transfers between devices, forward_unit(): lax.psum(matmul(written, uo_rows).astype(jnp.bfloat16), 'tp')  154 us
    dot_general x55, matrix products, matmul_tn(): lax.dot_general(left, right, (((0,), (0,)), ((), ())), preferred_element_...  117 us
    reduce_scatter x5, waiting for transfers between devices, backward_unit(): lax.psum_scatter((matmul_nt(grad_q, query_cols) + matmul_nt(key_part, key...  112 us
    dot_general x55, matrix products, matmul(): return jnp.dot(left, right, preferred_element_type=jnp.float32)  105 us
    dynamic_slice x75, local copies, waits for them, and re-layouts, store_at(): old_value = lax.dynamic_index_in_dim(buffer, slot_index, 0, keepdims=False)  103 us
    dot_general x75, matrix products, matmul_nt(): lax.dot_general(left, right, (((1,), (1,)), ((), ())), preferred_element_...  101 us
    dynamic_update_slice x45, other arithmetic, store_at(): lax.dynamic_update_index_in_dim(buffer, jnp.where(is_valid, new_value, ol...  71.7 us
  transfers between devices with their start and end apart: 48, of which 36 were waited for; matrix products, arithmetic and copies ran while one was open for 19% of the time, Pallas kernels for 0%

commit v1 on v0

v1 whole, which is shorter than its diff:
```python
from functools import partial

import jax
import jax.numpy as jnp
from jax import lax
from jax.experimental import pallas as pl
from jax.experimental.pallas import tpu as pltpu
from jax.sharding import PartitionSpec as P

F32 = jnp.float32
BF = jnp.bfloat16
MESH = pl.DeviceIdType.MESH
HEAD = 64
EPS = 1e-05
NEG = -1e30
VMEM_LIMIT = 67000000

WQ, WK, WV, WO, WUP, WDOWN, UQ, UK, UV, UO, UGATE = 0, 1, 2, 3, 4, 8, 12, 13, 14, 15, 16
TILES = 17


def dot(a, b):
    return lax.dot_general(a, b, (((1,), (0,)), ((), ())), preferred_element_type=F32)


def dot_nt(a, b):
    return lax.dot_general(a, b, (((1,), (1,)), ((), ())), preferred_element_type=F32)


def dot_tn(a, b):
    return lax.dot_general(a, b, (((0,), (0,)), ((), ())), preferred_element_type=F32)


def rows_at(i, size):
    return pl.ds(pl.multiple_of(i * size, size), size)


def loop(count, unroll=1):
    def run(body):
        def step(i, carry):
            body(i)
            return carry

        lax.fori_loop(0, count, step, 0, unroll=unroll)

    return run


def normed(v):
    mean = jnp.mean(v, axis=-1, keepdims=True)
    centered = v - mean
    inv = lax.rsqrt(jnp.mean(centered * centered, axis=-1, keepdims=True) + EPS)
    return centered * inv, inv


def norm_pull(e, gain, hat, inv):
    h = e * gain
    m0 = jnp.mean(h, axis=-1, keepdims=True)
    m1 = jnp.mean(h * hat, axis=-1, keepdims=True)
    return inv * (h - m0 - hat * m1)


def lane_block(width, block):
    return lax.broadcasted_iota(jnp.int32, (1, width), 1) // block


class Weights:
    def __init__(self, ref):
        self.ref = ref
        self.blocks, _, self.rows, self.width = ref.shape

    def cols(self, tile, start, size):
        got = self.ref[:, tile, :, pl.ds(start, size)]
        return got.reshape(self.blocks * self.rows, size)

    def row_part(self, tile, part, parts):
        count = self.blocks // parts
        got = self.ref[pl.ds(part * count, count), tile]
        return got.reshape(count * self.rows, self.width)

    def down_cols(self, chunk, chunks, start, size):
        count = self.blocks // chunks
        got = self.ref[pl.ds(chunk * count, count), WDOWN : WDOWN + 4, :, pl.ds(start, size)]
        return got.reshape(count * 4 * self.rows, size)

    def down_rows(self, part, parts):
        count = self.blocks // parts
        got = self.ref[pl.ds(part * count, count), WDOWN : WDOWN + 4]
        return got.reshape(count * 4 * self.rows, self.width)


def unit_scratch(tokens, slots, width, ff):
    r = tokens + slots
    heads = width // HEAD
    quads = width // 256
    v = pltpu.VMEM
    return dict(
        mem=v((slots, width), F32),
        bias=v((tokens, tokens), F32),
        xh=v((r, width), F32),
        xr=v((r, 1), F32),
        enc=v((r, width), BF),
        q=v((tokens, width), BF),
        k=v((r, width), BF),
        v=v((r, width), BF),
        kt=v((width, r), BF),
        vt=v((width, r), BF),
        pt=v((heads, r, tokens), BF),
        mixt=v((width, tokens), BF),
        af=v((tokens, width), F32),
        ah=v((tokens, width), F32),
        ar=v((tokens, 1), F32),
        fin=v((tokens, width), BF),
        act=v((ff // 512, tokens, 512), BF),
        dg=v((ff // 512, tokens, 512), BF),
        y=v((tokens, width), F32),
        yh=v((tokens, width), F32),
        yr=v((tokens, 1), F32),
        wri=v((r, width), BF),
        sq=v((slots, width), BF),
        sk=v((r, width), BF),
        sv=v((r, width), BF),
        spt=v((quads, r, 256), BF),
        wrt=v((slots, width), BF),
        gate=v((slots, width), F32),
        f1=v((slots, width), F32),
        f2=v((slots, width), F32),
        gm=v((slots, width), F32),
        gup=v((slots, width), BF),
        ggl=v((slots, width), BF),
        dsq=v((slots, width), BF),
        dsk=v((r, width), BF),
        dsv=v((r, width), BF),
        e=v((r, width), F32),
        gy=v((tokens, width), F32),
        gyb=v((tokens, width), BF),
        bwm=v((slots, width), F32),
        gpre=v((ff // 512, tokens, 512), BF),
        gab=v((tokens, width), BF),
        gmx=v((tokens, width), BF),
        dst=v((2, r, tokens), BF),
        dqt=v((width, tokens), BF),
        dq=v((tokens, width), BF),
        dk=v((r, width), BF),
        dv=v((r, width), BF),
    )


class Unit:
    def __init__(self, refs, w, x, gains, small):
        self.__dict__.update(refs)
        self.w = w
        self.x = x
        self.gains = gains
        self.small = small
        self.tokens, self.width = x.shape
        self.slots = self.mem.shape[0]
        self.r = self.tokens + self.slots
        self.ff = self.act.shape[0] * 512

    def gain(self, i):
        return self.gains[i : i + 1, :]

    def make_bias(self, first, length):
        t = self.tokens

        @loop(t // 64)
        def _(i):
            key = lax.broadcasted_iota(jnp.int32, (64, t), 0) + i * 64
            query = lax.broadcasted_iota(jnp.int32, (64, t), 1)
            last = first + length
            inside = (key >= first) & (key < last) & (query >= first) & (query < last)
            seen = (key <= query) | inside
            self.bias[rows_at(i, 64), :] = jnp.where(seen, 0.0, NEG).astype(F32)

    def norm_in(self, rows, values):
        hat, inv = normed(values)
        self.xh[rows, :] = hat
        self.xr[rows, :] = inv
        self.enc[rows, :] = (hat * self.gain(0)).astype(BF)

    def tokens_in(self):
        @loop(self.tokens // 32, unroll=2)
        def _(i):
            rows = rows_at(i, 32)
            self.norm_in(rows, self.x[rows, :].astype(F32))

    def project_tokens(self):
        t = self.tokens

        @loop(self.width // 256)
        def _(n):
            cols = rows_at(n, 256)
            enc = self.enc[0:t, :]
            got = dot(enc, self.w.cols(WQ, n * 256, 256)).astype(BF)
            self.q[:, cols] = got * BF(HEAD**-0.5)
            self.k[0:t, cols] = dot(enc, self.w.cols(WK, n * 256, 256)).astype(BF)
            self.v[0:t, cols] = dot(enc, self.w.cols(WV, n * 256, 256)).astype(BF)

    def memory_in(self):
        t, r = self.tokens, self.r
        self.norm_in(slice(t, r), self.mem[...])
        enc = self.enc[t:r, :]
        self.k[t:r, :] = dot(enc, self.w.cols(WK, 0, self.width)).astype(BF)
        self.v[t:r, :] = dot(enc, self.w.cols(WV, 0, self.width)).astype(BF)
        self.vt[...] = self.v[...].T

    def attend(self):
        t, r = self.tokens, self.r

        @loop(self.width // 128)
        def _(p):
            cols = rows_at(p, 128)
            keys = self.k[:, cols]
            half = lane_block(128, HEAD)
            for hh in range(2):
                feats = pl.ds(pl.multiple_of(p * 128 + hh * HEAD, HEAD), HEAD)
                values = self.vt[feats, :]
                for n in range(t // 256):
                    qc = slice(n * 256, n * 256 + 256)
                    q = self.q[qc, cols]
                    q = jnp.where(half == hh, q, jnp.zeros_like(q))
                    s = dot_nt(keys, q)
                    s_tok = s[0:t] + self.bias[:, qc]
                    s_mem = s[t:r]
                    peak = jnp.maximum(
                        jnp.max(s_tok, axis=0, keepdims=True), jnp.max(s_mem, axis=0, keepdims=True)
                    )
                    e_tok = jnp.exp(s_tok - peak)
                    e_mem = jnp.exp(s_mem - peak)
                    inv = 1.0 / (
                        jnp.sum(e_tok, axis=0, keepdims=True)
                        + jnp.sum(e_mem, axis=0, keepdims=True)
                    )
                    probs = jnp.concatenate([e_tok * inv, e_mem * inv], axis=0).astype(BF)
                    self.pt[2 * p + hh, :, qc] = probs
                    self.mixt[feats, qc] = dot(values, probs).astype(BF)

    def after_attention(self):
        t = self.tokens
        self.gmx[...] = self.mixt[...].T

        @loop(self.width // 256)
        def _(n):
            cols = rows_at(n, 256)
            got = dot(self.gmx[...], self.w.cols(WO, n * 256, 256))
            self.af[:, cols] = self.x[:, cols].astype(F32) + got

        @loop(t // 32, unroll=2)
        def _(i):
            rows = rows_at(i, 32)
            hat, inv = normed(self.af[rows, :])
            self.ah[rows, :] = hat
            self.ar[rows, :] = inv
            self.fin[rows, :] = (hat * self.gain(1)).astype(BF)

    def feed_forward(self):
        t = self.tokens
        for j in range(self.ff // 512):

            @loop(2)
            def _(n, j=j):
                cols = rows_at(n, 256)
                weights = self.w.cols(WUP + j, n * 256, 256)
                for m in range(t // 128):
                    rows = slice(m * 128, m * 128 + 128)
                    pre = dot(self.fin[rows, :], weights)
                    c = 0.7978845608028654
                    sq = pre * pre
                    th = jnp.tanh(pre * (c + (c * 0.044715) * sq))
                    half = 0.5 + 0.5 * th
                    self.act[j, rows, cols] = (pre * half).astype(BF)
                    slope = half + (0.5 * pre) * (1.0 - th * th) * (c + (3 * c * 0.044715) * sq)
                    self.dg[j, rows, cols] = slope.astype(BF)

        @loop(self.width // 256)
        def _(n):
            cols = rows_at(n, 256)
            total = self.af[:, cols]
            for j in range(self.ff // 512):
                total = total + dot(
                    self.act[j], self.w.down_cols(j, self.ff // 512, n * 256, 256)
                )
            self.y[:, cols] = total

        @loop(t // 32, unroll=2)
        def _(i):
            rows = rows_at(i, 32)
            hat, inv = normed(self.y[rows, :])
            self.yh[rows, :] = hat
            self.yr[rows, :] = inv
            self.wri[rows, :] = (hat * self.gain(2)).astype(BF)

        self.wri[t : self.r, :] = (self.xh[t : self.r, :] * self.gain(2)).astype(BF)

    def spread_heads(self, rows, g):
        part = rows[:, g * 256 : g * 256 + 256]
        block = lane_block(256, HEAD)
        return jnp.concatenate(
            [jnp.where(block == h, part, jnp.zeros_like(part)) for h in range(4)], axis=0
        )

    def gather_heads(self, stacked):
        block = lane_block(256, HEAD)
        s = self.slots
        total = jnp.where(block == 0, stacked[0:s], 0.0)
        for h in range(1, 4):
            total = total + jnp.where(block == h, stacked[h * s : h * s + s], 0.0)
        return total

    def write_memory(self):
        t, r = self.tokens, self.r

        @loop(self.width // 256)
        def _(n):
            cols = rows_at(n, 256)
            wri = self.wri[...]
            self.sk[:, cols] = dot(wri, self.w.cols(UK, n * 256, 256)).astype(BF)
            self.sv[:, cols] = dot(wri, self.w.cols(UV, n * 256, 256)).astype(BF)

        wm = self.wri[t:r, :]
        sq = dot(wm, self.w.cols(UQ, 0, self.width)).astype(BF)
        self.sq[...] = sq * BF(HEAD**-0.5)
        for g in range(self.width // 256):
            cols = slice(g * 256, g * 256 + 256)
            s = dot_nt(self.sk[:, cols], self.spread_heads(self.sq[...], g))
            e = jnp.exp(s - jnp.max(s, axis=0, keepdims=True))
            probs = (e * (1.0 / jnp.sum(e, axis=0, keepdims=True))).astype(BF)
            self.spt[g] = probs
            self.wrt[:, cols] = self.gather_heads(dot_tn(probs, self.sv[:, cols])).astype(BF)
        th = jnp.tanh(dot(self.wrt[...], self.w.cols(UO, 0, self.width)))
        pre = dot(wm, self.w.cols(UGATE, 0, self.width))
        gate = jax.nn.sigmoid(pre + self.gain(3))
        mem = self.mem[...]
        self.gate[...] = gate
        self.f1[...] = (mem - th) * gate * (1.0 - gate)
        self.f2[...] = (1.0 - gate) * (1.0 - th * th)
        return gate * mem + (1.0 - gate) * th

    def backward_early(self):
        self.kt[...] = self.k[...].T

    def write_back(self, out_grad):
        t, r, s = self.tokens, self.r, self.slots
        gm = self.gm[...]
        ggp = gm * self.f1[...]
        gup = (gm * self.f2[...]).astype(BF)
        ggl = ggp.astype(BF)
        self.gup[...] = gup
        self.ggl[...] = ggl
        self.small[3:4, :] = jnp.sum(ggp, axis=0, keepdims=True)
        gwr = dot_nt(gup, self.w.row_part(UO, 0, 1)).astype(BF)
        for g in range(self.width // 256):
            cols = slice(g * 256, g * 256 + 256)
            grads = self.spread_heads(gwr, g)
            dp = dot_nt(self.sv[:, cols], grads)
            probs = self.spt[g]
            pf = probs.astype(F32)
            ds = (pf * (dp - jnp.sum(pf * dp, axis=0, keepdims=True))).astype(BF)
            self.dsv[:, cols] = dot(probs, grads).astype(BF)
            self.dsk[:, cols] = dot(ds, self.spread_heads(self.sq[...], g)).astype(BF)
            dq = self.gather_heads(dot_tn(ds, self.sk[:, cols])) * HEAD**-0.5
            self.dsq[:, cols] = dq.astype(BF)

        @loop(2)
        def _(n):
            cols = rows_at(n, self.width // 2)
            self.e[:, cols] = dot_nt(self.dsk[...], self.w.row_part(UK, n, 2)) + dot_nt(
                self.dsv[...], self.w.row_part(UV, n, 2)
            )

        em = self.e[t:r, :] + dot_nt(self.dsq[...], self.w.row_part(UQ, 0, 1))
        em = em + dot_nt(ggl, self.w.row_part(UGATE, 0, 1))
        hat = self.xh[t:r, :]
        self.bwm[...] = norm_pull(em, self.gain(2), hat, self.xr[t:r, :])
        self.small[2:3, :] = jnp.sum(em * hat, axis=0, keepdims=True)

        @loop(t // 32, unroll=2)
        def _(i):
            rows = rows_at(i, 32)
            e = self.e[rows, :]
            hat = self.yh[rows, :]
            self.small[2:3, :] += jnp.sum(e * hat, axis=0, keepdims=True)
            grad = out_grad[rows, :].astype(F32) + norm_pull(e, self.gain(2), hat, self.yr[rows, :])
            self.gy[rows, :] = grad
            self.gyb[rows, :] = grad.astype(BF)

    def feed_forward_back(self):
        t = self.tokens
        chunks = self.ff // 512

        for j in range(chunks):

            @loop(2)
            def _(n, j=j):
                cols = rows_at(n, 256)
                weights = self.w.down_rows(2 * j + n, 2 * chunks)
                for m in range(t // 128):
                    rows = slice(m * 128, m * 128 + 128)
                    got = dot_nt(self.gyb[rows, :], weights)
                    self.gpre[j, rows, cols] = (got * self.dg[j, rows, cols].astype(F32)).astype(BF)

        @loop(2)
        def _(n):
            cols = rows_at(n, self.width // 2)
            total = dot_nt(self.gpre[0], self.w.row_part(WUP, n, 2))
            for j in range(1, chunks):
                total = total + dot_nt(self.gpre[j], self.w.row_part(WUP + j, n, 2))
            self.e[0:t, cols] = total

        self.small[1:2, :] = jnp.zeros((1, self.width), F32)

        @loop(t // 32, unroll=2)
        def _(i):
            rows = rows_at(i, 32)
            e = self.e[rows, :]
            hat = self.ah[rows, :]
            self.small[1:2, :] += jnp.sum(e * hat, axis=0, keepdims=True)
            grad = self.gy[rows, :] + norm_pull(e, self.gain(1), hat, self.ar[rows, :])
            self.gy[rows, :] = grad
            self.gab[rows, :] = grad.astype(BF)

    def attend_back(self):
        t, r = self.tokens, self.r

        @loop(2)
        def _(n):
            cols = rows_at(n, self.width // 2)
            self.gmx[:, cols] = dot_nt(self.gab[...], self.w.row_part(WO, n, 2)).astype(BF)

        @loop(self.width // 128)
        def _(p):
            cols = rows_at(p, 128)
            values = self.v[:, cols]
            half = lane_block(128, HEAD)
            for hh in range(2):
                feats = pl.ds(pl.multiple_of(p * 128 + hh * HEAD, HEAD), HEAD)
                keys = self.kt[feats, :]
                for n in range(t // 256):
                    qc = slice(n * 256, n * 256 + 256)
                    g = self.gmx[qc, cols]
                    g = jnp.where(half == hh, g, jnp.zeros_like(g))
                    dp = dot_nt(values, g)
                    pf = self.pt[2 * p + hh, :, qc].astype(F32)
                    ds = (pf * (dp - jnp.sum(pf * dp, axis=0, keepdims=True))).astype(BF)
                    self.dst[hh, :, qc] = ds
                    self.dqt[feats, qc] = (dot(keys, ds) * HEAD**-0.5).astype(BF)
            g = self.gmx[:, cols]
            q = self.q[:, cols]
            dv = jnp.where(half == 0, dot(self.pt[2 * p], g), dot(self.pt[2 * p + 1], g))
            self.dv[:, cols] = dv.astype(BF)
            dk = jnp.where(half == 0, dot(self.dst[0], q), dot(self.dst[1], q))
            self.dk[:, cols] = dk.astype(BF)

        self.dq[...] = self.dqt[...].T

    def enter_back(self, input_grad):
        t, r = self.tokens, self.r

        @loop(2)
        def _(n):
            cols = rows_at(n, self.width // 2)
            self.e[:, cols] = dot_nt(self.dk[...], self.w.row_part(WK, n, 2)) + dot_nt(
                self.dv[...], self.w.row_part(WV, n, 2)
            )
            self.e[0:t, cols] += dot_nt(self.dq[...], self.w.row_part(WQ, n, 2))

        e = self.e[t:r, :]
        hat = self.xh[t:r, :]
        self.small[0:1, :] = jnp.sum(e * hat, axis=0, keepdims=True)
        mem_grad = self.gm[...] * self.gate[...] + self.bwm[...]
        mem_grad = mem_grad + norm_pull(e, self.gain(0), hat, self.xr[t:r, :])

        @loop(t // 32, unroll=2)
        def _(i):
            rows = rows_at(i, 32)
            e = self.e[rows, :]
            hat = self.xh[rows, :]
            self.small[0:1, :] += jnp.sum(e * hat, axis=0, keepdims=True)
            grad = self.gy[rows, :] + norm_pull(e, self.gain(0), hat, self.xr[rows, :])
            input_grad[rows, :] = grad.astype(BF)

        return mem_grad


class Packing:
    HEADS = dict(wq=0, wk=1, wv=2, uq=3, uk=4, uv=5, uo=6, ugate=7)

    def __init__(self, shards, ctxs, width, ff):
        self.shards, self.ctxs, self.width, self.ff = shards, ctxs, width, ff
        self.head_rows = width // (shards * ctxs)
        self.row_rows = width // (shards * ctxs * 4)
        self.down_rows = ff // (shards * ctxs * 4)
        self.at_down = 0
        self.at_up = self.at_down + self.down_rows * (width // 128)
        self.at_wo = self.at_up + self.row_rows * (ff // 128)
        self.at_heads = self.at_wo + self.row_rows * (width // 128)
        self.rows = self.at_heads + 8 * self.head_rows

    @property
    def shape(self):
        return (self.shards, self.ctxs, 2, 2, self.rows, 128)


def weight_grads(u, g, pk, names):
    width = u.width
    tile = 256

    def store_head(at, m, got):
        h = pk.head_rows
        per = tile // h
        for i in range(per):
            s = m * (per // pk.ctxs) + i // pk.ctxs
            for t in range(4):
                g[s, i % pk.ctxs, t // 2, t % 2, at : at + h, :] = got[
                    i * h : i * h + h, t * 128 : t * 128 + 128
                ]

    def store_rows(at, h, m, got, chunk0):
        per = tile // h
        for i in range(per):
            if per % (pk.ctxs * 4) == 0:
                s, c = m * (per // (pk.ctxs * 4)) + i // (pk.ctxs * 4), (i // 4) % pk.ctxs
            else:
                owner = m * (per // 4) + i // 4
                s, c = lax.div(owner, pk.ctxs), lax.rem(owner, pk.ctxs)
            for j in range(got.shape[1] // 128):
                lo = at + (chunk0 + j) * h
                g[s, c, (i // 2) % 2, i % 2, lo : lo + h, :] = got[
                    i * h : i * h + h, j * 128 : j * 128 + 128
                ]

    def head(name, left, right):
        at = pk.at_heads + pk.HEADS[name] * pk.head_rows

        @loop(width // tile)
        def _(m):
            lt = left[:, rows_at(m, tile)].T
            store_head(at, m, dot(lt, right[...]).astype(BF))

    t, r = u.tokens, u.r
    if "ff" in names:
        for j in range(u.ff // 512):

            @loop(512 // tile)
            def _(m, j=j):
                lt = u.act[j, :, rows_at(m, tile)].T
                got = dot(lt, u.gyb[...]).astype(BF)
                store_rows(pk.at_down, pk.down_rows, m + j * (512 // tile), got, 0)

        @loop(width // tile)
        def _(m):
            lt = u.fin[:, rows_at(m, tile)].T
            for j in range(u.ff // 512):
                store_rows(pk.at_up, pk.row_rows, m, dot(lt, u.gpre[j]).astype(BF), 4 * j)

    if "wo" in names:

        @loop(width // tile)
        def _(m):
            got = dot(u.mixt[rows_at(m, tile), :], u.gab[...]).astype(BF)
            store_rows(pk.at_wo, pk.row_rows, m, got, 0)

    if "write" in names:
        head("uq", u.wri.at[t:r], u.dsq)
        head("uk", u.wri, u.dsk)
        head("uv", u.wri, u.dsv)
        head("uo", u.gup, u.wrt)
        head("ugate", u.ggl, u.wri.at[t:r])
    if "enter" in names:
        head("wq", u.enc.at[0:t], u.dq)
        head("wk", u.enc, u.dk)
        head("wv", u.enc, u.dv)


def unit_kernel(
    ctxs, pk, names, first, length, w, x, first_memory, gains, out_grad, memory_grad, *rest
):
    outs, scratch = rest[:6], rest[6:]
    outputs, memory_out, input_grad, memory_in, grads, small = outs
    refs = dict(zip(names, scratch[: len(names)]))
    u = Unit(refs, Weights(w), x, gains, small)
    if ctxs > 1:
        m_send, m_recv, g_send, g_recv, sems = scratch[len(names) :]
        c = lax.axis_index("ctx")
        greet([(c > 0, {"ctx": c - 1}), (c < ctxs - 1, {"ctx": c + 1})])

        def memory_copy(to):
            return pltpu.make_async_remote_copy(
                src_ref=m_send, dst_ref=m_recv, send_sem=sems.at[0], recv_sem=sems.at[1],
                device_id={"ctx": to}, device_id_type=MESH,
            )

        def grad_copy(to):
            return pltpu.make_async_remote_copy(
                src_ref=g_send, dst_ref=g_recv, send_sem=sems.at[2], recv_sem=sems.at[3],
                device_id={"ctx": to}, device_id_type=MESH,
            )

    u.make_bias(first[0], length[0])
    u.tokens_in()
    u.project_tokens()
    if ctxs > 1:

        @pl.when(c == 0)
        def _():
            u.mem[...] = first_memory[...]

        @pl.when(c > 0)
        def _():
            memory_copy(c - 1).wait_recv()
            u.mem[...] = m_recv[...].astype(F32)
    else:
        u.mem[...] = first_memory[...]
    u.memory_in()
    u.attend()
    u.after_attention()
    u.feed_forward()
    after = u.write_memory()
    memory_out[...] = after
    if ctxs > 1:
        m_send[...] = after.astype(BF)

        @pl.when(c < ctxs - 1)
        def _():
            memory_copy(c + 1).start()

    outputs[...] = u.y[...].astype(BF)
    u.backward_early()
    u.gm[...] = memory_grad[...]
    if ctxs > 1:

        @pl.when(c < ctxs - 1)
        def _():
            grad_copy(c + 1).wait_recv()
            u.gm[...] += g_recv[...].astype(F32)

    u.write_back(out_grad)
    u.feed_forward_back()
    u.attend_back()
    back = u.enter_back(input_grad)
    memory_in[...] = back
    if ctxs > 1:
        g_send[...] = back.astype(BF)

        @pl.when(c > 0)
        def _():
            grad_copy(c - 1).start()

    weight_grads(u, grads, pk, ("ff", "wo", "write", "enter"))
    if ctxs > 1:

        @pl.when(c < ctxs - 1)
        def _():
            memory_copy(c + 1).wait_send()

        @pl.when(c > 0)
        def _():
            grad_copy(c - 1).wait_send()


def run_unit(ctxs, pk, first, length, w, x, first_memory, gains, out_grad, memory_grad):
    tokens, width = x.shape
    slots = first_memory.shape[0]
    scratch = unit_scratch(tokens, slots, width, pk.ff)
    vm = pl.BlockSpec(memory_space=pltpu.VMEM)
    sm = pl.BlockSpec(memory_space=pltpu.SMEM)
    extra = []
    params = dict(vmem_limit_bytes=VMEM_LIMIT)
    if ctxs > 1:
        extra = [pltpu.VMEM((slots, width), BF)] * 4 + [pltpu.SemaphoreType.DMA((4,))]
        params.update(collective_id=1, has_side_effects=True)
    shape = jax.ShapeDtypeStruct
    return pl.pallas_call(
        partial(unit_kernel, ctxs, pk, tuple(scratch)),
        out_shape=(
            shape((tokens, width), BF),
            shape((slots, width), F32),
            shape((tokens, width), BF),
            shape((slots, width), F32),
            shape(pk.shape, BF),
            shape((8, width), F32),
        ),
        in_specs=[sm, sm] + [vm] * 6,
        out_specs=(vm,) * 6,
        scratch_shapes=list(scratch.values()) + extra,
        compiler_params=pltpu.CompilerParams(**params),
        name="unit",
    )(first, length, w, x, first_memory, gains, out_grad, memory_grad)


GROUPS = ((0, 3), (3, 8), (8, 12), (12, 17))


def greet(peers):
    barrier = pltpu.get_barrier_semaphore()
    count = 0
    for cond, device in peers:

        @pl.when(cond)
        def _(device=device):
            pl.semaphore_signal(barrier, inc=1, device_id=device, device_id_type=MESH)

        count = count + jnp.where(cond, 1, 0)
    pl.semaphore_wait(barrier, count)


class Gather:
    def __init__(self, shards, w, send, recv):
        self.n, self.w, self.send, self.recv = shards, w, send, recv
        self.s = lax.axis_index("shard")
        self.t = lax.axis_index("tp")
        self.partner = self.t + 1 - 2 * lax.rem(self.t, 2)
        self.across = lax.rem(self.t + 2, 4)

    def copy(self, kind, source, tp, g, device):
        lo, hi = GROUPS[g]
        block = self.w.at[source * 4 + tp, lo:hi]
        return pltpu.make_async_remote_copy(
            src_ref=block, dst_ref=block, send_sem=self.send.at[kind, source, g],
            recv_sem=self.recv.at[kind, source, g], device_id=device, device_id_type=MESH,
        )

    def up(self, source, g):
        return self.copy(0, source, self.t, g, {"shard": self.s + 1})

    def down(self, source, g):
        return self.copy(1, source, self.t, g, {"shard": self.s - 1})

    def to_partner(self, source, g):
        return self.copy(2, source, self.t, g, {"tp": self.partner})

    def from_partner(self, source, g):
        return self.copy(2, source, self.partner, g, {"tp": self.partner})

    def to_across(self, source, g):
        return self.copy(3, source, self.t, g, {"tp": self.across})

    def from_across(self, source, g):
        return self.copy(3, source, self.across, g, {"tp": self.across})

    def relay(self, source, g):
        return self.copy(4, source, self.across, g, {"tp": self.partner})

    def from_relay(self, source, g):
        other = lax.rem(self.partner + 2, 4)
        return self.copy(4, source, other, g, {"tp": self.partner})

    def start_own(self, g):
        s, n = self.s, self.n
        if n > 1:

            @pl.when(s < n - 1)
            def _():
                self.up(s, g).start()

            @pl.when(s > 0)
            def _():
                self.down(s, g).start()

        self.to_across(s, g).start()
        self.to_partner(s, g).start()

    def line_step(self, d, g):
        s, n = self.s, self.n

        @pl.when(s - d >= 0)
        def _():
            self.up(s - d, g).wait_recv()

            @pl.when(s < n - 1)
            def _():
                self.up(s - d, g).start()

            self.to_across(s - d, g).start()
            self.to_partner(s - d, g).start()

        @pl.when(s + d <= n - 1)
        def _():
            self.down(s + d, g).wait_recv()

            @pl.when(s > 0)
            def _():
                self.down(s + d, g).start()

            self.to_across(s + d, g).start()
            self.to_partner(s + d, g).start()

    def across_step(self, d, g):
        s, n = self.s, self.n
        for source, cond in ((s - d, s - d >= 0), (s + d, s + d <= n - 1))[: 1 if d == 0 else 2]:

            @pl.when(cond)
            def _(source=source):
                self.from_across(source, g).wait_recv()
                self.relay(source, g).start()

    def finish(self, g):
        s, n = self.s, self.n
        for source in range(n):
            self.from_partner(source, g).wait_recv()
            self.from_relay(source, g).wait_recv()

    def drain(self, g):
        s, n = self.s, self.n
        for source in range(n):
            self.to_across(source, g).wait_send()
            self.to_partner(source, g).wait_send()
            self.relay(source, g).wait_send()

            @pl.when(jnp.logical_and(s >= source, s < n - 1))
            def _(source=source):
                self.up(source, g).wait_send()

            @pl.when(jnp.logical_and(s <= source, s > 0))
            def _(source=source):
                self.down(source, g).wait_send()


def line_peers(n):
    s = lax.axis_index("shard")
    return [(s > 0, {"shard": s - 1}), (s < n - 1, {"shard": s + 1})] if n > 1 else []


def tp_peers():
    t = lax.axis_index("tp")
    return [(t >= 0, {"tp": lax.rem(t + d, 4)}) for d in (1, 2, 3)]


def own_tiles(weights, w, own, sems):
    names = [WQ, WK, WV, WO, WUP, WDOWN, UQ, UK, UV, UO, UGATE]
    rows = w.shape[2]
    out = []
    for name, ref in zip(names, weights):
        parts = {WUP: 4, WDOWN: 4}.get(name, 1)
        for j in range(parts):
            src = ref
            if name == WUP:
                src = ref.at[:, j * 512 : j * 512 + 512]
            if name == WDOWN:
                src = ref.at[j * rows : j * rows + rows]
            out.append(pltpu.make_async_copy(src, w.at[own, name + j], sems.at[name + j]))
    return out


def gather_kernel(shards, *refs):
    weights, out_grad, w, og = refs[:11], refs[11], refs[12], refs[13]
    local, send, recv, og_send, og_recv = refs[14:]
    s, t = lax.axis_index("shard"), lax.axis_index("tp")
    copies = own_tiles(weights, w, s * 4 + t, local)
    for c in copies:
        c.start()
    mine = pltpu.make_async_copy(out_grad.at[t], og.at[t], og_send.at[0])
    mine.start()
    greet(line_peers(shards) + tp_peers())
    gather = Gather(shards, w, send, recv)

    def og_copy(d):
        to = lax.rem(t + d, 4)
        return pltpu.make_async_remote_copy(
            src_ref=out_grad.at[to], dst_ref=og.at[t], send_sem=og_send.at[d],
            recv_sem=og_recv.at[d], device_id={"tp": to}, device_id_type=MESH,
        )

    groups = range(len(GROUPS))
    for g in groups:
        for c in copies[GROUPS[g][0] : GROUPS[g][1]]:
            c.wait()
        gather.start_own(g)
    for d in range(1, shards):
        for g in groups:
            gather.line_step(d, g)
        for g in groups:
            gather.across_step(d - 1, g)
    for d in (1, 2, 3):
        og_copy(d).start()
    for g in groups:
        gather.across_step(shards - 1, g)
    for g in groups:
        gather.finish(g)
    for d in (1, 2, 3):
        og_copy(d).wait_recv()
        og_copy(d).wait_send()
    mine.wait()
    for g in groups:
        gather.drain(g)


def run_gather(shards, weights, out_grad):
    rows, width = weights[0].shape
    share = out_grad.shape[1]
    vm = pl.BlockSpec(memory_space=pltpu.VMEM)
    hbm = pl.BlockSpec(memory_space=pl.ANY)
    dma = pltpu.SemaphoreType.DMA
    shape = jax.ShapeDtypeStruct
    return pl.pallas_call(
        partial(gather_kernel, shards),
        out_shape=(shape((shards * 4, TILES, rows, width), BF), shape((4, share, width), BF)),
        in_specs=[hbm] * 12,
        out_specs=(vm, vm),
        scratch_shapes=[
            dma((TILES,)), dma((5, shards, len(GROUPS))), dma((5, shards, len(GROUPS))), dma((4,)), dma((4,)),
        ],
        compiler_params=pltpu.CompilerParams(
            vmem_limit_bytes=VMEM_LIMIT, collective_id=2, has_side_effects=True
        ),
        name="gather",
    )(*weights, out_grad)


class Reduce:
    def __init__(self, shards, g, r1, r2, r3, zu, zd, send, recv):
        self.n = shards
        self.g, self.r1, self.r2, self.r3, self.zu, self.zd = g, r1, r2, r3, zu, zd
        self.send, self.recv = send, recv
        self.s, self.c, self.t = (lax.axis_index(a) for a in ("shard", "ctx", "tp"))
        self.core = lax.rem(self.t, 2)
        self.x = lax.div(self.t, 2)
        self.partner = {"tp": self.t + 1 - 2 * self.core}
        self.across = {"tp": lax.rem(self.t + 2, 4)}
        self.beside = {"ctx": 1 - self.c}

    def copy(self, src, dst, sem, device):
        return pltpu.make_async_remote_copy(
            src_ref=src, dst_ref=dst, send_sem=self.send.at[sem], recv_sem=self.recv.at[sem],
            device_id=device, device_id_type=MESH,
        )

    def sem(self, kind, chunk):
        return chunk * 9 + kind

    def first(self, k, rows):
        src = self.g.at[:, :, :, 1 - self.core, rows]
        return self.copy(src, self.r1.at[:, :, :, rows], self.sem(0, k), self.partner)

    def second(self, k, rows):
        if k % 2 == 0:
            src, device = self.r1.at[:, :, 1 - self.x, rows], self.across
        else:
            src, device = self.r1.at[:, 1 - self.c, :, rows], self.beside
        return self.copy(src, self.r2.at[:, :, rows], self.sem(1, k), device)

    def third(self, k, rows):
        if k % 2 == 0:
            src, device = self.r2.at[:, 1 - self.c, rows], self.beside
        else:
            src, device = self.r2.at[:, 1 - self.x, rows], self.across
        return self.copy(src, self.r3.at[:, rows], self.sem(2, k), device)

    def add_first(self, k, rows):
        self.first(k, rows).wait_recv()
        for i in range(self.r1.shape[0]):
            for j in range(2):
                for x in range(2):
                    self.r1[i, j, x, rows] += self.g[i, j, x, self.core, rows]
        self.second(k, rows).start()

    def add_second(self, k, rows):
        self.second(k, rows).wait_recv()
        for i in range(self.n):
            for j in range(2):
                if k % 2 == 0:
                    self.r2[i, j, rows] += self.r1[i, j, self.x, rows]
                else:
                    self.r2[i, j, rows] += self.r1[i, self.c, j, rows]
        self.third(k, rows).start()

    def add_third(self, k, rows):
        self.third(k, rows).wait_recv()
        own = self.c if k % 2 == 0 else self.x
        for i in range(self.n):
            self.r3[i, rows] += self.r2[i, own, rows]

    def line(self, k, rows, d, up, first):
        buf = self.zu if up else self.zd
        src = self.r3 if first else buf
        device = {"shard": self.s + 1} if up else {"shard": self.s - 1}
        sem = self.sem(3 + (0 if up else 3) + (d - 1 if up else d), k)
        return self.copy(src.at[d, rows], buf.at[d, rows], sem, device)

    def along(self, k, rows, drain=False):
        s, n = self.s, self.n

        def send(d, up, first):
            copy = self.line(k, rows, d, up, first)
            if drain:
                copy.wait_send()
                return
            if not first:
                self.line(k, rows, d, up, first).wait_recv()
                buf = self.zu if up else self.zd
                buf[d, rows] += self.r3[d, rows]
            copy.start()

        for d in range(n - 1, 0, -1):
            e = n - 1 - d

            @pl.when(s == 0)
            def _(d=d):
                send(d, True, True)

            @pl.when(s == n - 1)
            def _(e=e):
                send(e, False, True)

        for d in range(n - 1, 0, -1):
            e = n - 1 - d

            @pl.when(jnp.logical_and(s > 0, s < d))
            def _(d=d):
                send(d, True, False)

            @pl.when(jnp.logical_and(s < n - 1, s > e))
            def _(e=e):
                send(e, False, False)

    def arrive(self, k, rows):
        s, n = self.s, self.n
        for d in range(n):
            if d > 0:

                @pl.when(s == d)
                def _(d=d):
                    self.line(k, rows, d, True, False).wait_recv()
                    self.r3[d, rows] += self.zu[d, rows]

            if d < n - 1:

                @pl.when(s == d)
                def _(d=d):
                    self.line(k, rows, d, False, False).wait_recv()
                    self.r3[d, rows] += self.zd[d, rows]

    def drain(self, k, rows):
        self.first(k, rows).wait_send()
        self.second(k, rows).wait_send()
        self.third(k, rows).wait_send()
        self.along(k, rows, drain=True)


class SmallSum:
    def __init__(self, shards, own, got, send, recv):
        self.n, self.own, self.got, self.send, self.recv = shards, own, got, send, recv
        self.s, self.c, self.t = (lax.axis_index(a) for a in ("shard", "ctx", "tp"))

    def copy(self, i):
        device = [
            {"tp": self.t + 1 - 2 * lax.rem(self.t, 2)},
            {"tp": lax.rem(self.t + 2, 4)},
            {"ctx": 1 - self.c},
            {"shard": self.s + 1},
            {"shard": self.s - 1},
        ][i]
        return pltpu.make_async_remote_copy(
            src_ref=self.own.at[i], dst_ref=self.got.at[i], send_sem=self.send.at[i],
            recv_sem=self.recv.at[i], device_id=device, device_id_type=MESH,
        )

    def start(self, value):
        self.own[0] = value
        self.copy(0).start()

    def step(self, i):
        self.copy(i).wait_recv()
        self.own[i + 1] = self.own[i] + self.got[i]
        if i < 2:
            self.copy(i + 1).start()

    def line(self, out):
        s, n = self.s, self.n
        mine = self.own[3]
        self.own[4] = mine
        out[...] = mine

        @pl.when(s > 0)
        def _():
            self.copy(3).wait_recv()
            self.own[3] = mine + self.got[3]
            out[...] += self.got[3]

        @pl.when(s < n - 1)
        def _():
            self.copy(3).start()
            self.copy(4).wait_recv()
            self.own[4] = mine + self.got[4]
            out[...] += self.got[4]

        @pl.when(s > 0)
        def _():
            self.copy(4).start()

    def drain(self):
        for i in range(3):
            self.copy(i).wait_send()

        @pl.when(self.s < self.n - 1)
        def _():
            self.copy(3).wait_send()

        @pl.when(self.s > 0)
        def _():
            self.copy(4).wait_send()


class Spread:
    def __init__(self, refs, send, recv):
        self.refs, self.send, self.recv = refs, send, recv
        self.t = lax.axis_index("tp")

    def copy(self, i, d):
        src, dst, split = self.refs[i]
        to = lax.rem(self.t + d, 4)
        if split:
            share = dst.shape[1]
            src = src.at[pl.ds(pl.multiple_of(to * share, share), share)]
        dst = dst.at[self.t]
        if d == 0:
            return pltpu.make_async_copy(src, dst, self.send.at[i, d])
        return pltpu.make_async_remote_copy(
            src_ref=src, dst_ref=dst, send_sem=self.send.at[i, d], recv_sem=self.recv.at[i, d],
            device_id={"tp": to}, device_id_type=MESH,
        )

    def start(self, i):
        for d in (1, 2, 3, 0):
            self.copy(i, d).start()

    def finish(self, i):
        for d in (1, 2, 3):
            self.copy(i, d).wait_recv()
            self.copy(i, d).wait_send()
        self.copy(i, 0).wait()


def store_owned(pk, total, outs):
    wq, wk, wv, wo, up, down, uq, uk, uv, uo, ugate = outs
    h = pk.head_rows
    for name, ref in dict(wq=wq, wk=wk, wv=wv, uq=uq, uk=uk, uv=uv).items():
        at = pk.at_heads + pk.HEADS[name] * h
        ref[...] = total(at, h)
    for name, ref in dict(uo=uo, ugate=ugate).items():
        at = pk.at_heads + pk.HEADS[name] * h
        ref[...] = total(at, h).T
    for at, r, ref in ((pk.at_wo, pk.row_rows, wo), (pk.at_up, pk.row_rows, up), (pk.at_down, pk.down_rows, down)):
        for j in range(ref.shape[1] // 128):
            ref[:, j * 128 : j * 128 + 128] = total(at + j * r, r)


def reduce_kernel(shards, pk, chunks, grads, small, y, mem, xg, mig, *refs):
    spread_outs, small_out, weight_outs = refs[:4], refs[4], refs[5:16]
    r1, r2, r3, zu, zd, own, got, send, recv, s_send, s_recv, o_send, o_recv = refs[16:]
    c = lax.axis_index("ctx")
    greet(line_peers(shards) + tp_peers() + [(c >= 0, {"ctx": 1 - c})])
    red = Reduce(shards, grads, r1, r2, r3, zu, zd, send, recv)
    rows = [pl.ds(lo, hi - lo) for lo, hi in chunks]
    n = len(rows)
    for k in range(n):
        red.first(k, rows[k]).start()
    sums = SmallSum(shards, own, got, s_send, s_recv)
    sums.start(small[...])
    spread = Spread(
        [(y, spread_outs[0], True), (mem, spread_outs[1], False), (xg, spread_outs[2], True), (mig, spread_outs[3], False)],
        o_send, o_recv,
    )
    for i in range(4):
        spread.start(i)
    for step in range(n + 4):
        if step < n:
            red.add_first(step, rows[step])
        if step < 3:
            sums.step(step)
        if 0 <= step - 1 < n:
            red.add_second(step - 1, rows[step - 1])
        if 0 <= step - 2 < n:
            red.add_third(step - 2, rows[step - 2])
            red.along(step - 2, rows[step - 2])
        if 0 <= step - 4 < n:
            red.arrive(step - 4, rows[step - 4])
    sums.line(small_out)
    s = lax.axis_index("shard")
    store_owned(pk, lambda at, size: r3[s, at : at + size, :].astype(F32), weight_outs)
    for i in range(4):
        spread.finish(i)
    sums.drain()
    for k in range(n):
        red.drain(k, rows[k])


def run_reduce(shards, pk, chunks, grads, small, y, mem, xg, mig):
    vm = pl.BlockSpec(memory_space=pltpu.VMEM)
    hbm = pl.BlockSpec(memory_space=pl.ANY)
    dma = pltpu.SemaphoreType.DMA
    shape = jax.ShapeDtypeStruct
    tokens, width = y.shape
    slots = mem.shape[0]
    h = pk.head_rows
    head, turned = shape((h, 128), F32), shape((128, h), F32)
    outs = (
        shape((4, tokens // 4, width), BF), shape((4, slots, width), F32),
        shape((4, tokens // 4, width), BF), shape((4, slots, width), F32),
        shape((8, width), F32),
        head, head, head, shape((pk.row_rows, width), F32), shape((pk.row_rows, pk.ff), F32),
        shape((pk.down_rows, width), F32), head, head, head, turned, turned,
    )
    v = pltpu.VMEM
    n = shards
    return pl.pallas_call(
        partial(reduce_kernel, shards, pk, chunks),
        out_shape=outs,
        in_specs=[vm] * 6,
        out_specs=(hbm,) * 4 + (vm,) * 12,
        scratch_shapes=[
            v((n, 2, 2, pk.rows, 128), BF), v((n, 2, pk.rows, 128), BF), v((n, pk.rows, 128), BF),
            v((n, pk.rows, 128), BF), v((n, pk.rows, 128), BF),
            v((5, 8, width), F32), v((5, 8, width), F32),
            dma((9 * len(chunks),)), dma((9 * len(chunks),)), dma((5,)), dma((5,)), dma((4, 4)), dma((4, 4)),
        ],
        compiler_params=pltpu.CompilerParams(
            vmem_limit_bytes=VMEM_LIMIT, collective_id=3, has_side_effects=True
        ),
        name="reduce",
    )(grads, small, y, mem, xg, mig)


def full_gradients(pk, grads):
    groups, owners = pk.shards * pk.ctxs, pk.shards * pk.ctxs * 4
    by_head = grads.reshape(groups, 4, pk.rows, 128)
    by_owner = grads.reshape(owners, pk.rows, 128)

    def head(name):
        at = pk.at_heads + pk.HEADS[name] * pk.head_rows
        got = by_head[:, :, at : at + pk.head_rows]
        return got.transpose(0, 2, 1, 3).reshape(pk.width, pk.width).astype(F32)

    def rows(at, h, n):
        got = by_owner[:, at : at + h * n].reshape(owners, n, h, 128)
        return got.transpose(0, 2, 1, 3).reshape(owners * h, n * 128).astype(F32)

    return (
        head("wq"), head("wk"), head("wv"),
        rows(pk.at_wo, pk.row_rows, pk.width // 128),
        rows(pk.at_up, pk.row_rows, pk.ff // 128),
        rows(pk.at_down, pk.down_rows, pk.width // 128),
        head("uq"), head("uk"), head("uv"), head("uo").T, head("ugate").T,
    )


def local(
    inputs, first_memory, piece_start, piece_len,
    w_query, w_key, w_value, w_out, w_up, w_down, u_query, u_key, u_value, u_out, u_gate,
    gain_attn, gain_ffn, gain_write, gate_bias, out_grad, memory_grad,
):
    shards, ctxs, tps = (lax.axis_size(a) for a in ("shard", "ctx", "tp"))
    s, c, t = (lax.axis_index(a) for a in ("shard", "ctx", "tp"))
    seqs, tokens, width = inputs.shape
    ff = w_up.shape[1]
    assert seqs == tps == 4 and tokens == width == 512 and ff == 2048

    def mine(array):
        return lax.dynamic_index_in_dim(array, t, 0, keepdims=False)

    weights = (w_query, w_key, w_value, w_out, w_up, w_down, u_query, u_key, u_value, u_out, u_gate)
    gathered, og = run_gather(shards, weights, out_grad)
    gains = jnp.stack([gain_attn, gain_ffn, gain_write, gate_bias] * 2)
    direct = ctxs == 2 and width % (shards * ctxs * tps * 16) == 0
    pk = Packing(shards if direct else 4, 2, width, ff)
    y, mem, xg, mig, grads, small = run_unit(
        ctxs, pk, mine(piece_start), mine(piece_len), gathered, mine(inputs), mine(first_memory),
        gains, og.reshape(tokens, width), mine(memory_grad),
    )
    every = ("shard", "ctx", "tp")
    if direct:
        bounds = [pk.rows * i // 4 // 16 * 16 for i in range(5)]
        chunks = tuple(zip(bounds[:-1], bounds[1:]))
        got = run_reduce(shards, pk, chunks, grads, small, y, mem, xg, mig)
        owner = (s * ctxs + c) * tps + t
        share = width // (shards * ctxs * tps)
        vectors = lax.dynamic_slice_in_dim(got[4][:4], owner * share, share, 1)
        return got[:4] + got[5:16] + tuple(vectors[i] for i in range(4))
    share = tokens // tps

    def rows_out(array):
        return lax.all_to_all(array.reshape(tps, share, width), "tp", 0, 0, tiled=True)

    full = full_gradients(pk, grads)
    out = [rows_out(y), lax.all_gather(mem, "tp"), rows_out(xg), lax.all_gather(mig, "tp")]
    for i, g in enumerate(full):
        if i in (3, 4, 5):
            out.append(lax.psum_scatter(g, every, scatter_dimension=0, tiled=True))
            continue
        sum_dim = 1 if i >= 9 else 0
        cut = lax.psum_scatter(g, "tp", scatter_dimension=1 - sum_dim, tiled=True)
        out.append(lax.psum_scatter(cut, ("shard", "ctx"), scatter_dimension=sum_dim, tiled=True))
    for i in range(4):
        out.append(lax.psum_scatter(small[i], every, scatter_dimension=0, tiled=True))
    return tuple(out)


def solution(mesh):
    cut = P(("shard", "tp"), None)
    head, rows, turned = P(("shard", "ctx"), "tp"), P(("shard", "ctx", "tp"), None), P("tp", ("shard", "ctx"))
    vector = P(("shard", "ctx", "tp"))
    over_rows, over_ctx = P("shard", ("ctx", "tp"), None), P("shard", "ctx", None)
    return jax.shard_map(
        local,
        mesh=mesh,
        in_specs=(over_ctx, P("shard", None, None), P("shard", "ctx"), P("shard", "ctx"))
        + (cut,) * 11 + (P(),) * 4 + (over_rows, over_ctx),
        out_specs=(over_rows, over_ctx, over_rows, over_ctx)
        + (head,) * 3 + (rows,) * 3 + (head,) * 3 + (turned,) * 2 + (vector,) * 4,
        check_vma=False,
    )
```

time: 2530 us -> 329 us (0.13)
  waiting for transfers between devices: 1310 us -> 0 us
  matrix products: 359 us -> 0 us
  Pallas kernels: 0 us -> 297 us
  blocking collectives: 294 us -> 0 us
  local copies, waits for them, and re-layouts: 274 us -> 30.9 us
  other arithmetic: 230 us -> 0 us
  starting transfers between devices: 27.6 us -> 0 us
    reduce_scatter x26 -> x0, waiting for transfers between devices: 1100 us -> none  [the longest x3 416 us: local(): lax.psum_scatter(row_sums, ('shard', 'ctx', 'tp'), scatter_dimension=0, t...]
    dot_general x255 -> x0, matrix products: 359 us -> none  [the longest x55 117 us: matmul_tn(): lax.dot_general(left, right, (((0,), (0,)), ((), ())), preferred_element_...]
    pallas_call x0 -> x3, Pallas kernels: none -> 297 us  [the longest x1 122 us: run_unit(): pl.pallas_call(partial(unit_kernel, ctxs, pk, tuple(scratch)), out_shape=...]
    all_gather x19 -> x0, blocking collectives: 254 us -> none  [the longest x5 34.6 us: backward_unit(): grad_attn = lax.all_gather(grad_after_low, 'tp', axis=0, tiled=True)]
    psum x10 -> x0, waiting for transfers between devices: 197 us -> none  [the longest x5 154 us: forward_unit(): lax.psum(matmul(written, uo_rows).astype(jnp.bfloat16), 'tp')]
    dynamic_slice x164 -> x2, local copies, waits for them, and re-layouts: 173 us -> 1.34 us  [the longest x1 1.26 us: mine(): return lax.dynamic_index_in_dim(array, t, 0, keepdims=False)]
    dynamic_update_slice x45 -> x0, other arithmetic: 71.7 us -> none  [store_at(): lax.dynamic_update_index_in_dim(buffer, jnp.where(is_valid, new_value, ol...]
    reduce_sum x95 -> x0, other arithmetic: 64.6 us -> none  [the longest x20 19.8 us: norm_back(): centered = values - jnp.mean(values, axis=-1, keepdims=True)]
  transfers between devices with their start and end apart: 48 -> 0, of which waited for: 36 -> 0; matrix products, arithmetic and copies ran while one was open for 19% -> 0% of each run, Pallas kernels for 0% -> 0%
where the time goes in v1:
time: 329 us; the launch traced here: 328 us
  Pallas kernels  297 us (90%)
  local copies, waits for them, and re-layouts  30.9 us (9%)
    pallas_call x1, Pallas kernels, run_unit(): pl.pallas_call(partial(unit_kernel, ctxs, pk, tuple(scratch)), out_shape=...  122 us
    pallas_call x1, Pallas kernels, run_reduce(): pl.pallas_call(partial(reduce_kernel, shards, pk, chunks), out_shape=outs...  112 us
    pallas_call x1, Pallas kernels, run_gather(): pl.pallas_call(partial(gather_kernel, shards), out_shape=(shape((shards *...  62.3 us
    unnamed x15, local copies, waits for them, and re-layouts  23.3 us

profile of v1, /device:TPU:0, one launch (start us, length us, event | category | flops | bytes accessed | tf_op | source)
XLA Modules:
  0.0 328.1 jit_solution(9041948457643729005)
XLA Ops:
  0.7 1.3 constant_dynamic-slice_fusion.1
  1.9 1.4 stack.23.gains
  3.4 1.7 dynamic-slice_bitcast_fusion.1
  5.0 1.9 dynamic-slice_bitcast_fusion.x
  6.9 62.3 %gather.1 = (bf16[16,17,32,512]{3,2,1,0:T(8,128)(2,1)}, bf16[4,128,512]{2,1,0:T(8,128)(2,1)}) custom-call(bf16[32,512]{1,0:T(8,128)(2,1)} %refs_0_.1, bf16[32,512]{1,0:T(8,128)(2,1)} %refs_1_.1, bf16[32,512]{1,0:T(8,128)(2,1)} %refs_2_.1, bf16[32,512]{1,0:T(8,128)(2,1)} %refs_3_.1, bf16[32,2048]{1,0:T(8,128)(2,1)} %refs_4_.1, bf16[128,512]{1,0:T(8,128)(2,1)} %refs_5_.1, ...), custom_call_target="tpu_custom_call" | custom-call | tf_op jit(solution)/shard_map/gather/pallas_call | solution.py:896
  69.2 121.9 %unit.1 = (bf16[512,512]{1,0:T(8,128)(2,1)}, f32[64,512]{1,0:T(8,128)}, bf16[512,512]{1,0:T(8,128)(2,1)}, f32[64,512]{1,0:T(8,128)}, bf16[4,2,2,2,1088,128]{5,4,3,2,1,0:T(8,128)(2,1)}, /*index=5*/f32[8,512]{1,0:T(8,128)}) custom-call(s32[1]{0:T(128)} %bitcast.first, s32[1]{0:T(128)} %bitcast.1.length, bf16[16,17,32,512]{3,2,1,0:T(8,128)(2,1)} %get-tuple-element.43.w, ...), custom_call_target="tpu_custom_call" | custom-call | tf_op jit(solution)/shard_map/unit/pallas_call | solution.py:674
  191.1 112.4 %reduce.1 = (bf16[4,128,512]{2,1,0:T(8,128)(2,1)}, f32[4,64,512]{2,1,0:T(8,128)}, bf16[4,128,512]{2,1,0:T(8,128)(2,1)}, f32[4,64,512]{2,1,0:T(8,128)}, f32[8,512...) custom-call(bf16[4,2,2,2,1088,128]{5,4,3,2,1,0:T(8,128)(2,1)} %get-t, ...), custom_call_target="tpu_custom_call" | custom-call | tf_op jit(solution)/shard_map/reduce/pallas_call | solution.py:1207
  303.5 0.7 slice.15
  304.2 0.1 constant_dynamic-slice_fusion
  304.3 0.5 slice_bitcast_fusion
  304.8 1.5 copy.40
  306.4 1.5 copy.41
  307.9 1.9 copy.55
  309.8 1.9 copy.56
  311.6 1.9 copy.57
  313.5 1.9 copy.58
  315.4 1.4 copy.59
  316.7 1.4 copy.60
  318.1 1.4 copy.61
  319.5 1.4 copy.62
  320.9 1.6 copy.63
  322.4 1.6 copy.64
  324.0 1.4 copy.65
  325.4 1.4 copy.66
  326.7 1.4 copy.67

commit v2 on v1

--- a/solution.py
+++ b/solution.py
@@ -96,7 +96,6 @@
     v = pltpu.VMEM
     return dict(
         mem=v((slots, width), F32),
-        bias=v((tokens, tokens), F32),
         xh=v((r, width), F32),
         xr=v((r, 1), F32),
         enc=v((r, width), BF),
@@ -113,7 +112,6 @@
         fin=v((tokens, width), BF),
         act=v((ff // 512, tokens, 512), BF),
         dg=v((ff // 512, tokens, 512), BF),
-        y=v((tokens, width), F32),
         yh=v((tokens, width), F32),
         yr=v((tokens, 1), F32),
         wri=v((r, width), BF),
@@ -171,7 +169,7 @@
             last = first + length
             inside = (key >= first) & (key < last) & (query >= first) & (query < last)
             seen = (key <= query) | inside
-            self.bias[rows_at(i, 64), :] = jnp.where(seen, 0.0, NEG).astype(F32)
+            self.e[rows_at(i, 64), :] = jnp.where(seen, 0.0, NEG).astype(F32)
 
     def norm_in(self, rows, values):
         hat, inv = normed(values)
@@ -205,11 +203,12 @@
         self.v[t:r, :] = dot(enc, self.w.cols(WV, 0, self.width)).astype(BF)
         self.vt[...] = self.v[...].T
 
-    def attend(self):
+    def attend(self, first, count):
         t, r = self.tokens, self.r
 
-        @loop(self.width // 128)
-        def _(p):
+        @loop(count)
+        def _(i):
+            p = i + first
             cols = rows_at(p, 128)
             keys = self.k[:, cols]
             half = lane_block(128, HEAD)
@@ -221,7 +220,7 @@
                     q = self.q[qc, cols]
                     q = jnp.where(half == hh, q, jnp.zeros_like(q))
                     s = dot_nt(keys, q)
-                    s_tok = s[0:t] + self.bias[:, qc]
+                    s_tok = s[0:t] + self.e[0:t, qc]
                     s_mem = s[t:r]
                     peak = jnp.maximum(
                         jnp.max(s_tok, axis=0, keepdims=True), jnp.max(s_mem, axis=0, keepdims=True)
@@ -254,7 +253,7 @@
             self.ar[rows, :] = inv
             self.fin[rows, :] = (hat * self.gain(1)).astype(BF)
 
-    def feed_forward(self):
+    def feed_forward_up(self):
         t = self.tokens
         for j in range(self.ff // 512):
 
@@ -273,6 +272,9 @@
                     slope = half + (0.5 * pre) * (1.0 - th * th) * (c + (3 * c * 0.044715) * sq)
                     self.dg[j, rows, cols] = slope.astype(BF)
 
+    def feed_forward_down(self):
+        t = self.tokens
+
         @loop(self.width // 256)
         def _(n):
             cols = rows_at(n, 256)
@@ -281,12 +283,12 @@
                 total = total + dot(
                     self.act[j], self.w.down_cols(j, self.ff // 512, n * 256, 256)
                 )
-            self.y[:, cols] = total
+            self.af[:, cols] = total
 
         @loop(t // 32, unroll=2)
         def _(i):
             rows = rows_at(i, 32)
-            hat, inv = normed(self.y[rows, :])
+            hat, inv = normed(self.af[rows, :])
             self.yh[rows, :] = hat
             self.yr[rows, :] = inv
             self.wri[rows, :] = (hat * self.gain(2)).astype(BF)
@@ -381,7 +383,7 @@
             e = self.e[rows, :]
             hat = self.yh[rows, :]
             self.small[2:3, :] += jnp.sum(e * hat, axis=0, keepdims=True)
-            grad = out_grad[rows, :].astype(F32) + norm_pull(e, self.gain(2), hat, self.yr[rows, :])
+            grad = out_grad(i) + norm_pull(e, self.gain(2), hat, self.yr[rows, :])
             self.gy[rows, :] = grad
             self.gyb[rows, :] = grad.astype(BF)
 
@@ -420,16 +422,18 @@
             self.gy[rows, :] = grad
             self.gab[rows, :] = grad.astype(BF)
 
-    def attend_back(self):
-        t, r = self.tokens, self.r
-
+    def project_back(self):
         @loop(2)
         def _(n):
             cols = rows_at(n, self.width // 2)
             self.gmx[:, cols] = dot_nt(self.gab[...], self.w.row_part(WO, n, 2)).astype(BF)
 
-        @loop(self.width // 128)
-        def _(p):
+    def attend_back(self, first, count):
+        t, r = self.tokens, self.r
+
+        @loop(count)
+        def _(i):
+            p = i + first
             cols = rows_at(p, 128)
             values = self.v[:, cols]
             half = lane_block(128, HEAD)
@@ -452,10 +456,9 @@
             dk = jnp.where(half == 0, dot(self.dst[0], q), dot(self.dst[1], q))
             self.dk[:, cols] = dk.astype(BF)
 
-        self.dq[...] = self.dqt[...].T
-
     def enter_back(self, input_grad):
         t, r = self.tokens, self.r
+        self.dq[...] = self.dqt[...].T
 
         @loop(2)
         def _(n):
@@ -484,18 +487,20 @@
 
 
 class Packing:
-    HEADS = dict(wq=0, wk=1, wv=2, uq=3, uk=4, uv=5, uo=6, ugate=7)
-
     def __init__(self, shards, ctxs, width, ff):
         self.shards, self.ctxs, self.width, self.ff = shards, ctxs, width, ff
-        self.head_rows = width // (shards * ctxs)
+        self.head_rows = h = width // (shards * ctxs)
         self.row_rows = width // (shards * ctxs * 4)
         self.down_rows = ff // (shards * ctxs * 4)
-        self.at_down = 0
+        self.heads = dict(uq=0, uk=h, uv=2 * h, uo=3 * h, ugate=4 * h)
+        self.at_down = 5 * h
         self.at_up = self.at_down + self.down_rows * (width // 128)
         self.at_wo = self.at_up + self.row_rows * (ff // 128)
-        self.at_heads = self.at_wo + self.row_rows * (width // 128)
-        self.rows = self.at_heads + 8 * self.head_rows
+        at = self.at_wo + self.row_rows * (width // 128)
+        self.heads.update(wq=at, wk=at + h, wv=at + 2 * h)
+        self.rows = at + 3 * h
+        bounds = (0, self.at_down, self.at_up, self.at_wo, at + h, self.rows)
+        self.chunks = tuple(zip(bounds[:-1], bounds[1:]))
 
     @property
     def shape(self):
@@ -531,7 +536,7 @@
                 ]
 
     def head(name, left, right):
-        at = pk.at_heads + pk.HEADS[name] * pk.head_rows
+        at = pk.heads[name]
 
         @loop(width // tile)
         def _(m):
@@ -539,7 +544,7 @@
             store_head(at, m, dot(lt, right[...]).astype(BF))
 
     t, r = u.tokens, u.r
-    if "ff" in names:
+    if "down" in names:
         for j in range(u.ff // 512):
 
             @loop(512 // tile)
@@ -547,6 +552,8 @@
                 lt = u.act[j, :, rows_at(m, tile)].T
                 got = dot(lt, u.gyb[...]).astype(BF)
                 store_rows(pk.at_down, pk.down_rows, m + j * (512 // tile), got, 0)
+
+    if "up" in names:
 
         @loop(width // tile)
         def _(m):
@@ -567,126 +574,11 @@
         head("uv", u.wri, u.dsv)
         head("uo", u.gup, u.wrt)
         head("ugate", u.ggl, u.wri.at[t:r])
-    if "enter" in names:
+    if "wq" in names:
         head("wq", u.enc.at[0:t], u.dq)
+    if "wkv" in names:
         head("wk", u.enc, u.dk)
         head("wv", u.enc, u.dv)
-
-
-def unit_kernel(
-    ctxs, pk, names, first, length, w, x, first_memory, gains, out_grad, memory_grad, *rest
-):
-    outs, scratch = rest[:6], rest[6:]
-    outputs, memory_out, input_grad, memory_in, grads, small = outs
-    refs = dict(zip(names, scratch[: len(names)]))
-    u = Unit(refs, Weights(w), x, gains, small)
-    if ctxs > 1:
-        m_send, m_recv, g_send, g_recv, sems = scratch[len(names) :]
-        c = lax.axis_index("ctx")
-        greet([(c > 0, {"ctx": c - 1}), (c < ctxs - 1, {"ctx": c + 1})])
-
-        def memory_copy(to):
-            return pltpu.make_async_remote_copy(
-                src_ref=m_send, dst_ref=m_recv, send_sem=sems.at[0], recv_sem=sems.at[1],
-                device_id={"ctx": to}, device_id_type=MESH,
-            )
-
-        def grad_copy(to):
-            return pltpu.make_async_remote_copy(
-                src_ref=g_send, dst_ref=g_recv, send_sem=sems.at[2], recv_sem=sems.at[3],
-                device_id={"ctx": to}, device_id_type=MESH,
-            )
-
-    u.make_bias(first[0], length[0])
-    u.tokens_in()
-    u.project_tokens()
-    if ctxs > 1:
-
-        @pl.when(c == 0)
-        def _():
-            u.mem[...] = first_memory[...]
-
-        @pl.when(c > 0)
-        def _():
-            memory_copy(c - 1).wait_recv()
-            u.mem[...] = m_recv[...].astype(F32)
-    else:
-        u.mem[...] = first_memory[...]
-    u.memory_in()
-    u.attend()
-    u.after_attention()
-    u.feed_forward()
-    after = u.write_memory()
-    memory_out[...] = after
-    if ctxs > 1:
-        m_send[...] = after.astype(BF)
-
-        @pl.when(c < ctxs - 1)
-        def _():
-            memory_copy(c + 1).start()
-
-    outputs[...] = u.y[...].astype(BF)
-    u.backward_early()
-    u.gm[...] = memory_grad[...]
-    if ctxs > 1:
-
-        @pl.when(c < ctxs - 1)
-        def _():
-            grad_copy(c + 1).wait_recv()
-            u.gm[...] += g_recv[...].astype(F32)
-
-    u.write_back(out_grad)
-    u.feed_forward_back()
-    u.attend_back()
-    back = u.enter_back(input_grad)
-    memory_in[...] = back
-    if ctxs > 1:
-        g_send[...] = back.astype(BF)
-
-        @pl.when(c > 0)
-        def _():
-            grad_copy(c - 1).start()
-
-    weight_grads(u, grads, pk, ("ff", "wo", "write", "enter"))
-    if ctxs > 1:
-
-        @pl.when(c < ctxs - 1)
-        def _():
-            memory_copy(c + 1).wait_send()
-
-        @pl.when(c > 0)
-        def _():
-            grad_copy(c - 1).wait_send()
-
-
-def run_unit(ctxs, pk, first, length, w, x, first_memory, gains, out_grad, memory_grad):
-    tokens, width = x.shape
-    slots = first_memory.shape[0]
-    scratch = unit_scratch(tokens, slots, width, pk.ff)
-    vm = pl.BlockSpec(memory_space=pltpu.VMEM)
-    sm = pl.BlockSpec(memory_space=pltpu.SMEM)
-    extra = []
-    params = dict(vmem_limit_bytes=VMEM_LIMIT)
-    if ctxs > 1:
-        extra = [pltpu.VMEM((slots, width), BF)] * 4 + [pltpu.SemaphoreType.DMA((4,))]
-        params.update(collective_id=1, has_side_effects=True)
-    shape = jax.ShapeDtypeStruct
-    return pl.pallas_call(
-        partial(unit_kernel, ctxs, pk, tuple(scratch)),
-        out_shape=(
-            shape((tokens, width), BF),
-            shape((slots, width), F32),
-            shape((tokens, width), BF),
-            shape((slots, width), F32),
-            shape(pk.shape, BF),
-            shape((8, width), F32),
-        ),
-        in_specs=[sm, sm] + [vm] * 6,
-        out_specs=(vm,) * 6,
-        scratch_shapes=list(scratch.values()) + extra,
-        compiler_params=pltpu.CompilerParams(**params),
-        name="unit",
-    )(first, length, w, x, first_memory, gains, out_grad, memory_grad)
 
 
 GROUPS = ((0, 3), (3, 8), (8, 12), (12, 17))
@@ -706,45 +598,51 @@
 
 
 class Gather:
-    def __init__(self, shards, w, send, recv):
-        self.n, self.w, self.send, self.recv = shards, w, send, recv
-        self.s = lax.axis_index("shard")
-        self.t = lax.axis_index("tp")
-        self.partner = self.t + 1 - 2 * lax.rem(self.t, 2)
-        self.across = lax.rem(self.t + 2, 4)
-
-    def copy(self, kind, source, tp, g, device):
+    UP, DOWN, PAIR, ACROSS, PAIR_ACROSS, BESIDE, PAIR_BESIDE, FAR, PAIR_FAR = range(9)
+
+    def __init__(self, shards, halved, w, send, recv):
+        self.n, self.halved, self.w, self.send, self.recv = shards, halved, w, send, recv
+        self.s, self.c, self.t = (lax.axis_index(a) for a in ("shard", "ctx", "tp"))
+        odd = lax.rem(self.t, 2)
+        self.pair_tp = self.t + 1 - 2 * odd
+        self.across_tp = lax.rem(self.t + 2, 4)
+        self.pair = {"tp": self.pair_tp}
+        self.across = {"tp": self.across_tp}
+        self.beside = {"ctx": self.c + 1 - 2 * lax.rem(self.c, 2)}
+
+    def copy(self, kind, source, tp, g, device, half=None):
         lo, hi = GROUPS[g]
         block = self.w.at[source * 4 + tp, lo:hi]
+        if half is not None:
+            size = self.w.shape[2] // 2
+            block = self.w.at[source * 4 + tp, lo:hi, pl.ds(pl.multiple_of(half * size, size), size)]
         return pltpu.make_async_remote_copy(
             src_ref=block, dst_ref=block, send_sem=self.send.at[kind, source, g],
             recv_sem=self.recv.at[kind, source, g], device_id=device, device_id_type=MESH,
         )
 
-    def up(self, source, g):
-        return self.copy(0, source, self.t, g, {"shard": self.s + 1})
-
-    def down(self, source, g):
-        return self.copy(1, source, self.t, g, {"shard": self.s - 1})
-
-    def to_partner(self, source, g):
-        return self.copy(2, source, self.t, g, {"tp": self.partner})
-
-    def from_partner(self, source, g):
-        return self.copy(2, source, self.partner, g, {"tp": self.partner})
-
-    def to_across(self, source, g):
-        return self.copy(3, source, self.t, g, {"tp": self.across})
-
-    def from_across(self, source, g):
-        return self.copy(3, source, self.across, g, {"tp": self.across})
-
-    def relay(self, source, g):
-        return self.copy(4, source, self.across, g, {"tp": self.partner})
-
-    def from_relay(self, source, g):
-        other = lax.rem(self.partner + 2, 4)
-        return self.copy(4, source, other, g, {"tp": self.partner})
+    @property
+    def mine(self):
+        return self.c if self.halved else None
+
+    @property
+    def others(self):
+        return 1 - self.c
+
+    def up(self, source, g, far):
+        return self.copy(self.UP, source, self.t, g, {"shard": self.s + 1}, self.mine if far else None)
+
+    def down(self, source, g, far):
+        return self.copy(self.DOWN, source, self.t, g, {"shard": self.s - 1}, self.mine if far else None)
+
+    def to_across(self, source, g, tp=None):
+        return self.copy(self.ACROSS, source, self.t if tp is None else tp, g, self.across, self.mine)
+
+    def to_pair(self, source, g, far, tp=None):
+        return self.copy(self.PAIR, source, self.t if tp is None else tp, g, self.pair, self.mine if far else None)
+
+    def far(self, d):
+        return self.halved and d == self.n - 1
 
     def start_own(self, g):
         s, n = self.s, self.n
@@ -752,69 +650,144 @@
 
             @pl.when(s < n - 1)
             def _():
-                self.up(s, g).start()
+                self.up(s, g, self.far(1)).start()
 
             @pl.when(s > 0)
             def _():
-                self.down(s, g).start()
+                self.down(s, g, self.far(1)).start()
 
         self.to_across(s, g).start()
-        self.to_partner(s, g).start()
+        self.to_pair(s, g, False).start()
+
+    def came(self, source, g, d):
+        self.to_across(source, g).start()
+        self.to_pair(source, g, self.far(d)).start()
+        if self.far(d):
+            self.copy(self.FAR, source, self.t, g, self.beside, self.c).start()
 
     def line_step(self, d, g):
         s, n = self.s, self.n
 
         @pl.when(s - d >= 0)
         def _():
-            self.up(s - d, g).wait_recv()
+            self.up(s - d, g, self.far(d)).wait_recv()
 
             @pl.when(s < n - 1)
             def _():
-                self.up(s - d, g).start()
-
-            self.to_across(s - d, g).start()
-            self.to_partner(s - d, g).start()
+                self.up(s - d, g, self.far(d + 1)).start()
+
+            self.came(s - d, g, d)
 
         @pl.when(s + d <= n - 1)
         def _():
-            self.down(s + d, g).wait_recv()
+            self.down(s + d, g, self.far(d)).wait_recv()
 
             @pl.when(s > 0)
             def _():
-                self.down(s + d, g).start()
-
-            self.to_across(s + d, g).start()
-            self.to_partner(s + d, g).start()
+                self.down(s + d, g, self.far(d + 1)).start()
+
+            self.came(s + d, g, d)
+
+    def sources(self, d):
+        s, n = self.s, self.n
+        both = ((s - d, s - d >= 0), (s + d, s + d <= n - 1))
+        return both[:1] if d == 0 else both
 
     def across_step(self, d, g):
-        s, n = self.s, self.n
-        for source, cond in ((s - d, s - d >= 0), (s + d, s + d <= n - 1))[: 1 if d == 0 else 2]:
+        for source, cond in self.sources(d):
 
             @pl.when(cond)
             def _(source=source):
-                self.from_across(source, g).wait_recv()
-                self.relay(source, g).start()
-
-    def finish(self, g):
-        s, n = self.s, self.n
-        for source in range(n):
-            self.from_partner(source, g).wait_recv()
-            self.from_relay(source, g).wait_recv()
+                tp = self.across_tp
+                self.to_across(source, g, tp).wait_recv()
+                self.copy(self.PAIR_ACROSS, source, tp, g, self.pair, self.mine).start()
+                if self.halved:
+                    self.copy(self.BESIDE, source, tp, g, self.beside, self.c).start()
+
+    def beside_step(self, d, g):
+        if not self.halved:
+            return
+        for source, cond in self.sources(d):
+
+            @pl.when(cond)
+            def _(source=source):
+                tp = self.across_tp
+                self.copy(self.BESIDE, source, tp, g, self.beside, self.others).wait_recv()
+                self.copy(self.PAIR_BESIDE, source, tp, g, self.pair, self.others).start()
+
+    def far_step(self, g):
+        if not self.halved:
+            return
+        for source, cond in self.sources(self.n - 1):
+
+            @pl.when(cond)
+            def _(source=source):
+                self.copy(self.FAR, source, self.t, g, self.beside, self.others).wait_recv()
+                self.copy(self.PAIR_FAR, source, self.t, g, self.pair, self.others).start()
+
+    def finish(self, g, own=False):
+        tp = self.t if own else self.pair_tp
+        other = self.across_tp if own else lax.rem(self.pair_tp + 2, 4)
+        for d in range(self.n):
+            for source, cond in self.sources(d):
+
+                @pl.when(cond)
+                def _(source=source, d=d):
+                    copies = [
+                        self.to_pair(source, g, self.far(d), tp),
+                        self.copy(self.PAIR_ACROSS, source, other, g, self.pair, self.mine),
+                    ]
+                    if self.halved:
+                        copies.append(self.copy(self.PAIR_BESIDE, source, other, g, self.pair, self.others))
+                    if self.far(d):
+                        copies.append(self.copy(self.PAIR_FAR, source, tp, g, self.pair, self.others))
+                    if own:
+                        copies.append(self.to_across(source, g))
+                        if self.halved:
+                            copies.append(self.copy(self.BESIDE, source, other, g, self.beside, self.c))
+                        if self.far(d):
+                            copies.append(self.copy(self.FAR, source, tp, g, self.beside, self.c))
+                    for copy in copies:
+                        if own:
+                            copy.wait_send()
+                        else:
+                            copy.wait_recv()
 
     def drain(self, g):
         s, n = self.s, self.n
-        for source in range(n):
-            self.to_across(source, g).wait_send()
-            self.to_partner(source, g).wait_send()
-            self.relay(source, g).wait_send()
-
-            @pl.when(jnp.logical_and(s >= source, s < n - 1))
-            def _(source=source):
-                self.up(source, g).wait_send()
-
-            @pl.when(jnp.logical_and(s <= source, s > 0))
-            def _(source=source):
-                self.down(source, g).wait_send()
+        self.finish(g, own=True)
+        for d in range(n - 1):
+
+            @pl.when(jnp.logical_and(s - d >= 0, s < n - 1))
+            def _(d=d):
+                self.up(s - d, g, self.far(d + 1)).wait_send()
+
+            @pl.when(jnp.logical_and(s + d <= n - 1, s > 0))
+            def _(d=d):
+                self.down(s + d, g, self.far(d + 1)).wait_send()
+
+    def events(self, time, ready):
+        n = self.n
+        groups = range(len(GROUPS))
+        for g in groups:
+            if time == max(2 * g - 2, 0):
+                ready(g)
+                self.start_own(g)
+        for g in groups:
+            d = time - 2 * g
+            if 1 <= d <= n - 1:
+                self.line_step(d, g)
+            if 0 <= d - 1 <= n - 1:
+                self.across_step(d - 1, g)
+            if 0 <= d - 2 <= n - 1:
+                self.beside_step(d - 2, g)
+            if d == n + 1:
+                self.far_step(g)
+                self.finish(g)
+
+    @property
+    def last(self):
+        return 2 * (len(GROUPS) - 1) + self.n + 1
 
 
 def line_peers(n):
@@ -843,72 +816,9 @@
     return out
 
 
-def gather_kernel(shards, *refs):
-    weights, out_grad, w, og = refs[:11], refs[11], refs[12], refs[13]
-    local, send, recv, og_send, og_recv = refs[14:]
-    s, t = lax.axis_index("shard"), lax.axis_index("tp")
-    copies = own_tiles(weights, w, s * 4 + t, local)
-    for c in copies:
-        c.start()
-    mine = pltpu.make_async_copy(out_grad.at[t], og.at[t], og_send.at[0])
-    mine.start()
-    greet(line_peers(shards) + tp_peers())
-    gather = Gather(shards, w, send, recv)
-
-    def og_copy(d):
-        to = lax.rem(t + d, 4)
-        return pltpu.make_async_remote_copy(
-            src_ref=out_grad.at[to], dst_ref=og.at[t], send_sem=og_send.at[d],
-            recv_sem=og_recv.at[d], device_id={"tp": to}, device_id_type=MESH,
-        )
-
-    groups = range(len(GROUPS))
-    for g in groups:
-        for c in copies[GROUPS[g][0] : GROUPS[g][1]]:
-            c.wait()
-        gather.start_own(g)
-    for d in range(1, shards):
-        for g in groups:
-            gather.line_step(d, g)
-        for g in groups:
-            gather.across_step(d - 1, g)
-    for d in (1, 2, 3):
-        og_copy(d).start()
-    for g in groups:
-        gather.across_step(shards - 1, g)
-    for g in groups:
-        gather.finish(g)
-    for d in (1, 2, 3):
-        og_copy(d).wait_recv()
-        og_copy(d).wait_send()
-    mine.wait()
-    for g in groups:
-        gather.drain(g)
-
-
-def run_gather(shards, weights, out_grad):
-    rows, width = weights[0].shape
-    share = out_grad.shape[1]
-    vm = pl.BlockSpec(memory_space=pltpu.VMEM)
-    hbm = pl.BlockSpec(memory_space=pl.ANY)
-    dma = pltpu.SemaphoreType.DMA
-    shape = jax.ShapeDtypeStruct
-    return pl.pallas_call(
-        partial(gather_kernel, shards),
-        out_shape=(shape((shards * 4, TILES, rows, width), BF), shape((4, share, width), BF)),
-        in_specs=[hbm] * 12,
-        out_specs=(vm, vm),
-        scratch_shapes=[
-            dma((TILES,)), dma((5, shards, len(GROUPS))), dma((5, shards, len(GROUPS))), dma((4,)), dma((4,)),
-        ],
-        compiler_params=pltpu.CompilerParams(
-            vmem_limit_bytes=VMEM_LIMIT, collective_id=2, has_side_effects=True
-        ),
-        name="gather",
-    )(*weights, out_grad)
-
-
 class Reduce:
+    ORDER = (0, 0, 1, 0, 1)
+
     def __init__(self, shards, g, r1, r2, r3, zu, zd, send, recv):
         self.n = shards
         self.g, self.r1, self.r2, self.r3, self.zu, self.zd = g, r1, r2, r3, zu, zd
@@ -934,14 +844,14 @@
         return self.copy(src, self.r1.at[:, :, :, rows], self.sem(0, k), self.partner)
 
     def second(self, k, rows):
-        if k % 2 == 0:
+        if self.ORDER[k] == 0:
             src, device = self.r1.at[:, :, 1 - self.x, rows], self.across
         else:
             src, device = self.r1.at[:, 1 - self.c, :, rows], self.beside
         return self.copy(src, self.r2.at[:, :, rows], self.sem(1, k), device)
 
     def third(self, k, rows):
-        if k % 2 == 0:
+        if self.ORDER[k] == 0:
             src, device = self.r2.at[:, 1 - self.c, rows], self.beside
         else:
             src, device = self.r2.at[:, 1 - self.x, rows], self.across
@@ -959,7 +869,7 @@
         self.second(k, rows).wait_recv()
         for i in range(self.n):
             for j in range(2):
-                if k % 2 == 0:
+                if self.ORDER[k] == 0:
                     self.r2[i, j, rows] += self.r1[i, j, self.x, rows]
                 else:
                     self.r2[i, j, rows] += self.r1[i, self.c, j, rows]
@@ -967,7 +877,7 @@
 
     def add_third(self, k, rows):
         self.third(k, rows).wait_recv()
-        own = self.c if k % 2 == 0 else self.x
+        own = self.c if self.ORDER[k] == 0 else self.x
         for i in range(self.n):
             self.r3[i, rows] += self.r2[i, own, rows]
 
@@ -1132,94 +1042,385 @@
         self.copy(i, 0).wait()
 
 
-def store_owned(pk, total, outs):
-    wq, wk, wv, wo, up, down, uq, uk, uv, uo, ugate = outs
+class Comm:
+    pass
+
+
+def step_scratch(shards, pk, direct, tokens, slots, width):
+    v, dma = pltpu.VMEM, pltpu.SemaphoreType.DMA
+    n = shards
+    out = dict(
+        w=v((n * 4, TILES, width // (n * 4), width), BF),
+        x=v((tokens, width), BF),
+        m0=v((slots, width), F32),
+        og=v((4, tokens // 4, width), BF),
+        y=v((tokens, width), BF),
+        xg=v((tokens, width), BF),
+        mem_out=v((slots, width), F32),
+        mig=v((slots, width), F32),
+        small=v((8, width), F32),
+        m_send=v((slots, width), BF),
+        m_recv=v((slots, width), BF),
+        g_send=v((slots, width), BF),
+        g_recv=v((slots, width), BF),
+        chain=dma((4,)),
+        loads=dma((3,)),
+        local=dma((TILES,)),
+        w_send=dma((9, n, len(GROUPS))),
+        w_recv=dma((9, n, len(GROUPS))),
+        og_send=dma((4,)),
+        og_recv=dma((4,)),
+        o_send=dma((4, 4)),
+        o_recv=dma((4, 4)),
+    )
+    if direct:
+        c = len(pk.chunks)
+        out.update(
+            g=v(pk.shape, BF),
+            r1=v((n, 2, 2, pk.rows, 128), BF),
+            r2=v((n, 2, pk.rows, 128), BF),
+            r3=v((n, pk.rows, 128), BF),
+            zu=v((n, pk.rows, 128), BF),
+            zd=v((n, pk.rows, 128), BF),
+            own=v((5, 8, width), F32),
+            got=v((5, 8, width), F32),
+            r_send=dma((9 * c,)),
+            r_recv=dma((9 * c,)),
+            s_send=dma((5,)),
+            s_recv=dma((5,)),
+        )
+    return out
+
+
+def step_kernel(dims, pk, direct, names, unit_names, *refs):
+    shards, ctxs, halved = dims
+    first, length, inputs, first_memory, memory_grad, out_grad = refs[:6]
+    weights, gains, outs = refs[6:17], refs[17], refs[18:24]
+    scratch = refs[24:]
+    b = Comm()
+    b.__dict__.update(zip(names, scratch))
+    unit_refs = dict(zip(unit_names, scratch[len(names) :]))
+    if not direct:
+        b.g = outs[4]
+    s, c, t = (lax.axis_index(a) for a in ("shard", "ctx", "tp"))
+    u = Unit(unit_refs, Weights(b.w), b.x, gains, b.small)
+
+    loads = [
+        pltpu.make_async_copy(inputs.at[t], b.x, b.loads.at[0]),
+        pltpu.make_async_copy(first_memory.at[t], b.m0, b.loads.at[1]),
+        pltpu.make_async_copy(memory_grad.at[t], u.gm, b.loads.at[2]),
+    ]
+    copies = own_tiles(weights, b.w, s * 4 + t, b.local)
+    for copy in copies + loads:
+        copy.start()
+    mine = pltpu.make_async_copy(out_grad.at[t], b.og.at[t], b.og_send.at[0])
+    mine.start()
+    peers = line_peers(shards) + tp_peers()
+    if ctxs > 1:
+        peers += [(c > 0, {"ctx": c - 1}), (c < ctxs - 1, {"ctx": c + 1})]
+    greet(peers)
+    gather = Gather(shards, halved, b.w, b.w_send, b.w_recv)
+
+    def ready(g):
+        for copy in copies[GROUPS[g][0] : GROUPS[g][1]]:
+            copy.wait()
+
+    def gather_until(start, stop):
+        for time in range(start, stop):
+            gather.events(time, ready)
+
+    def chain_copy(i, to):
+        src, dst = ((b.m_send, b.m_recv), (b.g_send, b.g_recv))[i]
+        return pltpu.make_async_remote_copy(
+            src_ref=src, dst_ref=dst, send_sem=b.chain.at[2 * i], recv_sem=b.chain.at[2 * i + 1],
+            device_id={"ctx": to}, device_id_type=MESH,
+        )
+
+    def og_copy(d):
+        to = lax.rem(t + d, 4)
+        return pltpu.make_async_remote_copy(
+            src_ref=out_grad.at[to], dst_ref=b.og.at[t], send_sem=b.og_send.at[d],
+            recv_sem=b.og_recv.at[d], device_id={"tp": to}, device_id_type=MESH,
+        )
+
+    spread = Spread(
+        [(b.y, outs[0], True), (b.mem_out, outs[1], False), (b.xg, outs[2], True), (b.mig, outs[3], False)],
+        b.o_send, b.o_recv,
+    )
+    lead, follow = pl.when(c == 0), pl.when(c > 0)
+    pairs = u.width // 128
+
+    gather_until(0, 1)
+    for copy in loads:
+        copy.wait()
+    u.make_bias(first[t, 0], length[t, 0])
+    gather_until(1, 2)
+    u.tokens_in()
+    at_first = shards + 2
+    gather_until(2, at_first)
+    u.project_tokens()
+
+    @lead
+    def _():
+        u.mem[...] = b.m0[...]
+        u.memory_in()
+        u.attend(0, pairs // 2)
+
+    gather_until(at_first, at_first + 1)
+
+    @lead
+    def _():
+        u.attend(pairs // 2, pairs - pairs // 2)
+
+    gather_until(at_first + 1, at_first + 2)
+
+    @lead
+    def _():
+        u.after_attention()
+        u.feed_forward_up()
+
+    gather_until(at_first + 2, at_first + 4)
+
+    @lead
+    def _():
+        u.feed_forward_down()
+
+    gather_until(at_first + 4, gather.last + 1)
+    for d in (1, 2, 3):
+        og_copy(d).start()
+
+    if ctxs > 1:
+
+        @follow
+        def _():
+            chain_copy(0, c - 1).wait_recv()
+            u.mem[...] = b.m_recv[...].astype(F32)
+            u.memory_in()
+            u.attend(0, pairs)
+            u.after_attention()
+            u.feed_forward_up()
+            u.feed_forward_down()
+
+    after = u.write_memory()
+    b.mem_out[...] = after
+    b.y[...] = u.af[...].astype(BF)
+    if ctxs > 1:
+        b.m_send[...] = after.astype(BF)
+
+        @pl.when(c < ctxs - 1)
+        def _():
+            chain_copy(0, c + 1).start()
+
+    spread.start(0)
+    spread.start(1)
+    u.backward_early()
+    mine.wait()
+    for d in (1, 2, 3):
+        og_copy(d).wait_recv()
+
+    if ctxs > 1:
+
+        @pl.when(c < ctxs - 1)
+        def _():
+            chain_copy(1, c + 1).wait_recv()
+            u.gm[...] += b.g_recv[...].astype(F32)
+
+    def out_grad_rows(i):
+        per = b.og.shape[1] // 32
+        return b.og[lax.div(i, per), pl.ds(lax.rem(i, per) * 32, 32), :].astype(F32)
+
+    def grads(*which):
+        weight_grads(u, b.g, pk, which)
+
+    if direct:
+        red = Reduce(shards, b.g, b.r1, b.r2, b.r3, b.zu, b.zd, b.r_send, b.r_recv)
+        rows = [pl.ds(lo, hi - lo) for lo, hi in pk.chunks]
+        sums = SmallSum(shards, b.own, b.got, b.s_send, b.s_recv)
+
+    def reduce(*todo):
+        if direct:
+            for what, k in todo:
+                if what == "first":
+                    red.first(k, rows[k]).start()
+                else:
+                    getattr(red, what)(k, rows[k])
+
+    A, DOWN, UP, C0, C1 = range(5)
+    u.write_back(out_grad_rows)
+
+    @lead
+    def _():
+        grads("write")
+        reduce(("first", A))
+
+    u.feed_forward_back()
+
+    @lead
+    def _():
+        reduce(("add_first", A))
+        grads("down")
+        reduce(("first", DOWN))
+        grads("up")
+        reduce(("first", UP))
+
+    u.project_back()
+
+    @lead
+    def _():
+        reduce(("add_first", DOWN), ("add_second", A))
+
+    u.attend_back(0, pairs // 2)
+
+    @lead
+    def _():
+        reduce(("add_first", UP), ("add_second", DOWN))
+
+    u.attend_back(pairs // 2, pairs - pairs // 2)
+
+    @lead
+    def _():
+        reduce(("add_third", A), ("along", A), ("add_second", UP))
+
+    back = u.enter_back(b.xg)
+    b.mig[...] = back
+
+    if ctxs > 1:
+
+        @follow
+        def _():
+            b.g_send[...] = back.astype(BF)
+            chain_copy(1, c - 1).start()
+            grads("write")
+            reduce(("first", A))
+            grads("down")
+            reduce(("first", DOWN))
+            grads("up")
+            reduce(("first", UP))
+
+    grads("wo", "wq")
+    reduce(("first", C0))
+    grads("wkv")
+    reduce(("first", C1))
+    spread.start(2)
+    spread.start(3)
+    if direct:
+        sums.start(b.small[...])
+
+    @lead
+    def _():
+        reduce(("add_third", DOWN), ("along", DOWN), ("add_third", UP), ("along", UP), ("arrive", A))
+        reduce(("add_first", C0), ("add_first", C1), ("arrive", DOWN), ("arrive", UP))
+        reduce(("add_second", C0), ("add_second", C1))
+
+    @follow
+    def _():
+        reduce(*(("add_first", k) for k in range(5)))
+        reduce(*(("add_second", k) for k in (A, DOWN, C0)))
+        reduce(("add_third", A), ("along", A), ("add_second", UP), ("add_third", DOWN), ("along", DOWN))
+        reduce(("add_third", UP), ("along", UP), ("arrive", A), ("arrive", DOWN), ("arrive", UP), ("add_second", C1))
+
+    reduce(("add_third", C0), ("along", C0), ("add_third", C1), ("along", C1))
+    if direct:
+        for i in range(3):
+            sums.step(i)
+        sums.line(outs[5])
+    reduce(("arrive", C0), ("arrive", C1))
+    if direct:
+        outs[4][...] = b.r3[s]
+    else:
+        outs[5][...] = b.small[...]
+
+    for i in range(4):
+        spread.finish(i)
+    for d in (1, 2, 3):
+        og_copy(d).wait_send()
+    for g in range(len(GROUPS)):
+        gather.drain(g)
+    if ctxs > 1:
+
+        @pl.when(c < ctxs - 1)
+        def _():
+            chain_copy(0, c + 1).wait_send()
+
+        @pl.when(c > 0)
+        def _():
+            chain_copy(1, c - 1).wait_send()
+
+    if direct:
+        sums.drain()
+    reduce(*(("drain", k) for k in range(5)))
+
+
+def run_step(dims, pk, direct, first, length, inputs, first_memory, memory_grad, out_grad, weights, gains):
+    _, tokens, width = inputs.shape
+    slots = first_memory.shape[1]
+    vm = pl.BlockSpec(memory_space=pltpu.VMEM)
+    sm = pl.BlockSpec(memory_space=pltpu.SMEM)
+    hbm = pl.BlockSpec(memory_space=pl.ANY)
+    scratch = step_scratch(dims[0], pk, direct, tokens, slots, width)
+    unit = unit_scratch(tokens, slots, width, pk.ff)
+    shape = jax.ShapeDtypeStruct
+    return pl.pallas_call(
+        partial(step_kernel, dims, pk, direct, tuple(scratch), tuple(unit)),
+        out_shape=(
+            shape((4, tokens // 4, width), BF), shape((4, slots, width), F32),
+            shape((4, tokens // 4, width), BF), shape((4, slots, width), F32),
+            shape((pk.rows, 128) if direct else pk.shape, BF), shape((8, width), F32),
+        ),
+        in_specs=[sm, sm] + [hbm] * 15 + [vm],
+        out_specs=(hbm,) * 4 + (vm, vm),
+        scratch_shapes=list(scratch.values()) + list(unit.values()),
+        compiler_params=pltpu.CompilerParams(
+            vmem_limit_bytes=VMEM_LIMIT, collective_id=1, has_side_effects=True
+        ),
+        name="step",
+    )(first, length, inputs, first_memory, memory_grad, out_grad, *weights, gains)
+
+
+def store_kernel(pk, owners, *refs):
+    rows_in, total, small = refs[:4], refs[4], refs[5]
+    rows_out, (wq, wk, wv, wo, up, down, uq, uk, uv, uo, ugate), vectors = refs[6:10], refs[10:21], refs[21:]
+    for src, dst in zip(rows_in, rows_out):
+        dst[...] = src[...]
+
+    def part(at, size):
+        return total[at : at + size, :].astype(F32)
+
     h = pk.head_rows
     for name, ref in dict(wq=wq, wk=wk, wv=wv, uq=uq, uk=uk, uv=uv).items():
-        at = pk.at_heads + pk.HEADS[name] * h
-        ref[...] = total(at, h)
+        ref[...] = part(pk.heads[name], h)
     for name, ref in dict(uo=uo, ugate=ugate).items():
-        at = pk.at_heads + pk.HEADS[name] * h
-        ref[...] = total(at, h).T
+        ref[...] = part(pk.heads[name], h).T
     for at, r, ref in ((pk.at_wo, pk.row_rows, wo), (pk.at_up, pk.row_rows, up), (pk.at_down, pk.down_rows, down)):
         for j in range(ref.shape[1] // 128):
-            ref[:, j * 128 : j * 128 + 128] = total(at + j * r, r)
-
-
-def reduce_kernel(shards, pk, chunks, grads, small, y, mem, xg, mig, *refs):
-    spread_outs, small_out, weight_outs = refs[:4], refs[4], refs[5:16]
-    r1, r2, r3, zu, zd, own, got, send, recv, s_send, s_recv, o_send, o_recv = refs[16:]
-    c = lax.axis_index("ctx")
-    greet(line_peers(shards) + tp_peers() + [(c >= 0, {"ctx": 1 - c})])
-    red = Reduce(shards, grads, r1, r2, r3, zu, zd, send, recv)
-    rows = [pl.ds(lo, hi - lo) for lo, hi in chunks]
-    n = len(rows)
-    for k in range(n):
-        red.first(k, rows[k]).start()
-    sums = SmallSum(shards, own, got, s_send, s_recv)
-    sums.start(small[...])
-    spread = Spread(
-        [(y, spread_outs[0], True), (mem, spread_outs[1], False), (xg, spread_outs[2], True), (mig, spread_outs[3], False)],
-        o_send, o_recv,
-    )
-    for i in range(4):
-        spread.start(i)
-    for step in range(n + 4):
-        if step < n:
-            red.add_first(step, rows[step])
-        if step < 3:
-            sums.step(step)
-        if 0 <= step - 1 < n:
-            red.add_second(step - 1, rows[step - 1])
-        if 0 <= step - 2 < n:
-            red.add_third(step - 2, rows[step - 2])
-            red.along(step - 2, rows[step - 2])
-        if 0 <= step - 4 < n:
-            red.arrive(step - 4, rows[step - 4])
-    sums.line(small_out)
-    s = lax.axis_index("shard")
-    store_owned(pk, lambda at, size: r3[s, at : at + size, :].astype(F32), weight_outs)
-    for i in range(4):
-        spread.finish(i)
-    sums.drain()
-    for k in range(n):
-        red.drain(k, rows[k])
-
-
-def run_reduce(shards, pk, chunks, grads, small, y, mem, xg, mig):
+            ref[:, j * 128 : j * 128 + 128] = part(at + j * r, r)
+    share = small.shape[1] // owners
+    owner = lax.axis_index("shard")
+    for axis in ("ctx", "tp"):
+        owner = owner * lax.axis_size(axis) + lax.axis_index(axis)
+    turned = pltpu.roll(small[...], small.shape[1] - owner * share, 1)
+    for i, ref in enumerate(vectors):
+        ref[...] = turned[i : i + 1, 0:share]
+
+
+def run_store(pk, owners, rows, total, small):
     vm = pl.BlockSpec(memory_space=pltpu.VMEM)
-    hbm = pl.BlockSpec(memory_space=pl.ANY)
-    dma = pltpu.SemaphoreType.DMA
     shape = jax.ShapeDtypeStruct
-    tokens, width = y.shape
-    slots = mem.shape[0]
+    width = small.shape[1]
     h = pk.head_rows
     head, turned = shape((h, 128), F32), shape((128, h), F32)
-    outs = (
-        shape((4, tokens // 4, width), BF), shape((4, slots, width), F32),
-        shape((4, tokens // 4, width), BF), shape((4, slots, width), F32),
-        shape((8, width), F32),
+    outs = tuple(shape(r.shape, r.dtype) for r in rows) + (
         head, head, head, shape((pk.row_rows, width), F32), shape((pk.row_rows, pk.ff), F32),
         shape((pk.down_rows, width), F32), head, head, head, turned, turned,
-    )
-    v = pltpu.VMEM
-    n = shards
+    ) + (shape((1, width // owners), F32),) * 4
     return pl.pallas_call(
-        partial(reduce_kernel, shards, pk, chunks),
+        partial(store_kernel, pk, owners),
         out_shape=outs,
         in_specs=[vm] * 6,
-        out_specs=(hbm,) * 4 + (vm,) * 12,
-        scratch_shapes=[
-            v((n, 2, 2, pk.rows, 128), BF), v((n, 2, pk.rows, 128), BF), v((n, pk.rows, 128), BF),
-            v((n, pk.rows, 128), BF), v((n, pk.rows, 128), BF),
-            v((5, 8, width), F32), v((5, 8, width), F32),
-            dma((9 * len(chunks),)), dma((9 * len(chunks),)), dma((5,)), dma((5,)), dma((4, 4)), dma((4, 4)),
-        ],
-        compiler_params=pltpu.CompilerParams(
-            vmem_limit_bytes=VMEM_LIMIT, collective_id=3, has_side_effects=True
-        ),
-        name="reduce",
-    )(grads, small, y, mem, xg, mig)
+        out_specs=(vm,) * len(outs),
+        compiler_params=pltpu.CompilerParams(vmem_limit_bytes=VMEM_LIMIT),
+        name="store",
+    )(*rows, total, small)
 
 
 def full_gradients(pk, grads):
@@ -1228,7 +1429,7 @@
     by_owner = grads.reshape(owners, pk.rows, 128)
 
     def head(name):
-        at = pk.at_heads + pk.HEADS[name] * pk.head_rows
+        at = pk.heads[name]
         got = by_head[:, :, at : at + pk.head_rows]
         return got.transpose(0, 2, 1, 3).reshape(pk.width, pk.width).astype(F32)
 
@@ -1251,40 +1452,25 @@
     gain_attn, gain_ffn, gain_write, gate_bias, out_grad, memory_grad,
 ):
     shards, ctxs, tps = (lax.axis_size(a) for a in ("shard", "ctx", "tp"))
-    s, c, t = (lax.axis_index(a) for a in ("shard", "ctx", "tp"))
     seqs, tokens, width = inputs.shape
     ff = w_up.shape[1]
     assert seqs == tps == 4 and tokens == width == 512 and ff == 2048
-
-    def mine(array):
-        return lax.dynamic_index_in_dim(array, t, 0, keepdims=False)
-
     weights = (w_query, w_key, w_value, w_out, w_up, w_down, u_query, u_key, u_value, u_out, u_gate)
-    gathered, og = run_gather(shards, weights, out_grad)
     gains = jnp.stack([gain_attn, gain_ffn, gain_write, gate_bias] * 2)
-    direct = ctxs == 2 and width % (shards * ctxs * tps * 16) == 0
+    owners = shards * ctxs * tps
+    direct = ctxs == 2 and width % (owners * 16) == 0
+    halved = ctxs == 2 and w_query.shape[0] % 32 == 0
     pk = Packing(shards if direct else 4, 2, width, ff)
-    y, mem, xg, mig, grads, small = run_unit(
-        ctxs, pk, mine(piece_start), mine(piece_len), gathered, mine(inputs), mine(first_memory),
-        gains, og.reshape(tokens, width), mine(memory_grad),
+    got = run_step(
+        (shards, ctxs, halved), pk, direct, piece_start, piece_len, inputs, first_memory, memory_grad,
+        out_grad, weights, gains,
     )
+    if direct:
+        out = run_store(pk, owners, got[:4], got[4], got[5])
+        return out[:15] + tuple(v.reshape(-1) for v in out[15:])
     every = ("shard", "ctx", "tp")
-    if direct:
-        bounds = [pk.rows * i // 4 // 16 * 16 for i in range(5)]
-        chunks = tuple(zip(bounds[:-1], bounds[1:]))
-        got = run_reduce(shards, pk, chunks, grads, small, y, mem, xg, mig)
-        owner = (s * ctxs + c) * tps + t
-        share = width // (shards * ctxs * tps)
-        vectors = lax.dynamic_slice_in_dim(got[4][:4], owner * share, share, 1)
-        return got[:4] + got[5:16] + tuple(vectors[i] for i in range(4))
-    share = tokens // tps
-
-    def rows_out(array):
-        return lax.all_to_all(array.reshape(tps, share, width), "tp", 0, 0, tiled=True)
-
-    full = full_gradients(pk, grads)
-    out = [rows_out(y), lax.all_gather(mem, "tp"), rows_out(xg), lax.all_gather(mig, "tp")]
-    for i, g in enumerate(full):
+    out = list(got[:4])
+    for i, g in enumerate(full_gradients(pk, got[4])):
         if i in (3, 4, 5):
             out.append(lax.psum_scatter(g, every, scatter_dimension=0, tiled=True))
             continue
@@ -1292,7 +1478,7 @@
         cut = lax.psum_scatter(g, "tp", scatter_dimension=1 - sum_dim, tiled=True)
         out.append(lax.psum_scatter(cut, ("shard", "ctx"), scatter_dimension=sum_dim, tiled=True))
     for i in range(4):
-        out.append(lax.psum_scatter(small[i], every, scatter_dimension=0, tiled=True))
+        out.append(lax.psum_scatter(got[5][i], every, scatter_dimension=0, tiled=True))
     return tuple(out)
 
 

time: 329 us -> 250 us (0.76)
  Pallas kernels: 297 us -> 242 us
  local copies, waits for them, and re-layouts: 30.9 us -> 7.12 us
    pallas_call x3 -> x2, Pallas kernels: 297 us -> 242 us  [the longest x1 239 us: run_step(): pl.pallas_call(partial(step_kernel, dims, pk, direct, tuple(scratch), tup...]
    unnamed x15 -> x4, local copies, waits for them, and re-layouts: 23.3 us -> 5.7 us
    squeeze x3 -> x0, local copies, waits for them, and re-layouts: 4.08 us -> none  [the longest x2 3.55 us: mine(): return lax.dynamic_index_in_dim(array, t, 0, keepdims=False)]
where the time goes in v2:
time: 250 us
  Pallas kernels  242 us (97%)
  local copies, waits for them, and re-layouts  7.12 us (3%)
    pallas_call x1, Pallas kernels, run_step(): pl.pallas_call(partial(step_kernel, dims, pk, direct, tuple(scratch), tup...  239 us
    unnamed x4, local copies, waits for them, and re-layouts  5.7 us

profile of v2, /device:TPU:0, one launch (start us, length us, event | category | flops | bytes accessed | tf_op | source)
XLA Modules:
  0.0 249.8 jit_solution(1406572211146420646)
XLA Ops:
  0.7 1.3 copy.40.refs_0_
  2.0 1.3 copy.41.refs_1_
  3.3 1.4 stack.23.refs_17_
  4.7 238.8 %step.1 = (bf16[4,128,512]{2,1,0:T(8,128)(2,1)}, f32[4,64,512]{2,1,0:T(8,128)}, bf16[4,128,512]{2,1,0:T(8,128)(2,1)}, f32[4,64,512]{2,1,0:T(8,128)}, bf16[1088,128]{1,0:T(8,128)(2,1)}, /*index=5*/f32[8,512]{1,0:T(8,128)}) custom-call(s32[4,1]{1,0:T(4,128)} %copy.40.refs_0_, s32[4,1]{1,0:T(4,128)} %copy.41.refs_1_, bf16[4,512,512]{2,1,0:T(8,128)(2,1)} %refs_2_.1, ...), custom_call_target="tpu_custom_call" | custom-call | tf_op jit(solution)/shard_map/step/pallas_call | solution.py:1363
  243.6 3.2 %store.1 = (bf16[4,128,512]{2,1,0:T(8,128)(2,1)}, f32[4,64,512]{2,1,0:T(8,128)}, bf16[4,128,512]{2,1,0:T(8,128)(2,1)}, f32[4,64,512]{2,1,0:T(8,128)}, f32[64,128...) custom-call(bf16[4,128,512]{2,1,0:T(8,128)(2,1)} %get-tuple-element., ...), custom_call_target="tpu_custom_call" | custom-call | tf_op jit(solution)/shard_map/store/pallas_call | solution.py:1416
  246.7 1.5 copy.42
  248.3 1.5 copy.43

commit v3 on v2

--- a/solution.py
+++ b/solution.py
@@ -157,7 +157,7 @@
         self.ff = self.act.shape[0] * 512
 
     def gain(self, i):
-        return self.gains[i : i + 1, :]
+        return self.gains[i][...]
 
     def make_bias(self, first, length):
         t = self.tokens
@@ -402,6 +402,10 @@
                     got = dot_nt(self.gyb[rows, :], weights)
                     self.gpre[j, rows, cols] = (got * self.dg[j, rows, cols].astype(F32)).astype(BF)
 
+    def feed_forward_enter(self):
+        t = self.tokens
+        chunks = self.ff // 512
+
         @loop(2)
         def _(n):
             cols = rows_at(n, self.width // 2)
@@ -456,9 +460,11 @@
             dk = jnp.where(half == 0, dot(self.dst[0], q), dot(self.dst[1], q))
             self.dk[:, cols] = dk.astype(BF)
 
-    def enter_back(self, input_grad):
-        t, r = self.tokens, self.r
+    def queries_back(self):
         self.dq[...] = self.dqt[...].T
+
+    def enter_back(self):
+        t = self.tokens
 
         @loop(2)
         def _(n):
@@ -468,6 +474,8 @@
             )
             self.e[0:t, cols] += dot_nt(self.dq[...], self.w.row_part(WQ, n, 2))
 
+    def norm_enter(self, input_grad):
+        t, r = self.tokens, self.r
         e = self.e[t:r, :]
         hat = self.xh[t:r, :]
         self.small[0:1, :] = jnp.sum(e * hat, axis=0, keepdims=True)
@@ -492,14 +500,21 @@
         self.head_rows = h = width // (shards * ctxs)
         self.row_rows = width // (shards * ctxs * 4)
         self.down_rows = ff // (shards * ctxs * 4)
-        self.heads = dict(uq=0, uk=h, uv=2 * h, uo=3 * h, ugate=4 * h)
-        self.at_down = 5 * h
-        self.at_up = self.at_down + self.down_rows * (width // 128)
-        self.at_wo = self.at_up + self.row_rows * (ff // 128)
-        at = self.at_wo + self.row_rows * (width // 128)
-        self.heads.update(wq=at, wk=at + h, wv=at + 2 * h)
-        self.rows = at + 3 * h
-        bounds = (0, self.at_down, self.at_up, self.at_wo, at + h, self.rows)
+        self.at_down = 0
+        at = self.down_rows * (width // 128)
+        self.heads = {}
+        for name in ("uq", "uk", "uv", "uo", "ugate"):
+            self.heads[name] = at
+            at += h
+        self.at_up = at
+        self.at_wo = at + self.row_rows * (ff // 128)
+        last = at = self.at_wo + self.row_rows * (width // 128)
+        for name in ("wq", "wk", "wv"):
+            self.heads[name] = at
+            at += h
+        self.rows = at
+        middle = last + (at - last) // 2 // 16 * 16
+        bounds = (0, self.heads["uq"], self.at_up, self.at_wo, last, middle, at)
         self.chunks = tuple(zip(bounds[:-1], bounds[1:]))
 
     @property
@@ -574,9 +589,8 @@
         head("uv", u.wri, u.dsv)
         head("uo", u.gup, u.wrt)
         head("ugate", u.ggl, u.wri.at[t:r])
-    if "wq" in names:
+    if "enter" in names:
         head("wq", u.enc.at[0:t], u.dq)
-    if "wkv" in names:
         head("wk", u.enc, u.dk)
         head("wv", u.enc, u.dv)
 
@@ -792,7 +806,7 @@
 
 def line_peers(n):
     s = lax.axis_index("shard")
-    return [(s > 0, {"shard": s - 1}), (s < n - 1, {"shard": s + 1})] if n > 1 else []
+    return [(s >= 0, {"shard": lax.rem(s + d, n)}) for d in range(1, n)]
 
 
 def tp_peers():
@@ -817,135 +831,90 @@
 
 
 class Reduce:
-    ORDER = (0, 0, 1, 0, 1)
-
-    def __init__(self, shards, g, r1, r2, r3, zu, zd, send, recv):
+    ORDER = (0, 1, 0, 1, 0, 1)
+
+    def __init__(self, shards, chunks, g, r1, r2, r3, z, send, recv):
         self.n = shards
-        self.g, self.r1, self.r2, self.r3, self.zu, self.zd = g, r1, r2, r3, zu, zd
+        self.rows = [pl.ds(lo, hi - lo) for lo, hi in chunks]
+        self.g, self.r1, self.r2, self.r3, self.z = g, r1, r2, r3, z
         self.send, self.recv = send, recv
         self.s, self.c, self.t = (lax.axis_index(a) for a in ("shard", "ctx", "tp"))
         self.core = lax.rem(self.t, 2)
         self.x = lax.div(self.t, 2)
-        self.partner = {"tp": self.t + 1 - 2 * self.core}
+        self.pair = {"tp": self.t + 1 - 2 * self.core}
         self.across = {"tp": lax.rem(self.t + 2, 4)}
         self.beside = {"ctx": 1 - self.c}
 
-    def copy(self, src, dst, sem, device):
+    def copy(self, src, dst, k, kind, device):
         return pltpu.make_async_remote_copy(
-            src_ref=src, dst_ref=dst, send_sem=self.send.at[sem], recv_sem=self.recv.at[sem],
+            src_ref=src, dst_ref=dst, send_sem=self.send.at[k, kind], recv_sem=self.recv.at[k, kind],
             device_id=device, device_id_type=MESH,
         )
 
-    def sem(self, kind, chunk):
-        return chunk * 9 + kind
-
-    def first(self, k, rows):
-        src = self.g.at[:, :, :, 1 - self.core, rows]
-        return self.copy(src, self.r1.at[:, :, :, rows], self.sem(0, k), self.partner)
-
-    def second(self, k, rows):
+    def one(self, k):
+        rows = self.rows[k]
+        return self.copy(self.g.at[:, :, :, 1 - self.core, rows], self.r1.at[:, :, :, rows], k, 0, self.pair)
+
+    def two(self, k):
+        rows = self.rows[k]
         if self.ORDER[k] == 0:
             src, device = self.r1.at[:, :, 1 - self.x, rows], self.across
         else:
             src, device = self.r1.at[:, 1 - self.c, :, rows], self.beside
-        return self.copy(src, self.r2.at[:, :, rows], self.sem(1, k), device)
-
-    def third(self, k, rows):
+        return self.copy(src, self.r2.at[:, :, rows], k, 1, device)
+
+    def three(self, k):
+        rows = self.rows[k]
         if self.ORDER[k] == 0:
             src, device = self.r2.at[:, 1 - self.c, rows], self.beside
         else:
             src, device = self.r2.at[:, 1 - self.x, rows], self.across
-        return self.copy(src, self.r3.at[:, rows], self.sem(2, k), device)
-
-    def add_first(self, k, rows):
-        self.first(k, rows).wait_recv()
-        for i in range(self.r1.shape[0]):
-            for j in range(2):
-                for x in range(2):
-                    self.r1[i, j, x, rows] += self.g[i, j, x, self.core, rows]
-        self.second(k, rows).start()
-
-    def add_second(self, k, rows):
-        self.second(k, rows).wait_recv()
-        for i in range(self.n):
-            for j in range(2):
-                if self.ORDER[k] == 0:
-                    self.r2[i, j, rows] += self.r1[i, j, self.x, rows]
-                else:
-                    self.r2[i, j, rows] += self.r1[i, self.c, j, rows]
-        self.third(k, rows).start()
-
-    def add_third(self, k, rows):
-        self.third(k, rows).wait_recv()
+        return self.copy(src, self.r3.at[:, rows], k, 2, device)
+
+    def along(self, k, d):
+        to = lax.rem(self.s + d, self.n)
+        rows = self.rows[k]
+        return self.copy(self.r3.at[to, rows], self.z.at[d - 1, rows], k, 2 + d, {"shard": to})
+
+    def start(self, k):
+        self.one(k).start()
+
+    def to_second(self, k):
+        self.one(k).wait_recv()
+        rows = self.rows[k]
+        for j in range(2):
+            for x in range(2):
+                self.r1[:, j, x, rows] += self.g[:, j, x, self.core, rows]
+        self.two(k).start()
+
+    def to_third(self, k):
+        self.two(k).wait_recv()
+        rows = self.rows[k]
+        for j in range(2):
+            own = self.r1[:, j, self.x, rows] if self.ORDER[k] == 0 else self.r1[:, self.c, j, rows]
+            self.r2[:, j, rows] += own
+        self.three(k).start()
+
+    def to_last(self, k):
+        self.three(k).wait_recv()
+        rows = self.rows[k]
         own = self.c if self.ORDER[k] == 0 else self.x
-        for i in range(self.n):
-            self.r3[i, rows] += self.r2[i, own, rows]
-
-    def line(self, k, rows, d, up, first):
-        buf = self.zu if up else self.zd
-        src = self.r3 if first else buf
-        device = {"shard": self.s + 1} if up else {"shard": self.s - 1}
-        sem = self.sem(3 + (0 if up else 3) + (d - 1 if up else d), k)
-        return self.copy(src.at[d, rows], buf.at[d, rows], sem, device)
-
-    def along(self, k, rows, drain=False):
-        s, n = self.s, self.n
-
-        def send(d, up, first):
-            copy = self.line(k, rows, d, up, first)
-            if drain:
-                copy.wait_send()
-                return
-            if not first:
-                self.line(k, rows, d, up, first).wait_recv()
-                buf = self.zu if up else self.zd
-                buf[d, rows] += self.r3[d, rows]
-            copy.start()
-
-        for d in range(n - 1, 0, -1):
-            e = n - 1 - d
-
-            @pl.when(s == 0)
-            def _(d=d):
-                send(d, True, True)
-
-            @pl.when(s == n - 1)
-            def _(e=e):
-                send(e, False, True)
-
-        for d in range(n - 1, 0, -1):
-            e = n - 1 - d
-
-            @pl.when(jnp.logical_and(s > 0, s < d))
-            def _(d=d):
-                send(d, True, False)
-
-            @pl.when(jnp.logical_and(s < n - 1, s > e))
-            def _(e=e):
-                send(e, False, False)
-
-    def arrive(self, k, rows):
-        s, n = self.s, self.n
-        for d in range(n):
-            if d > 0:
-
-                @pl.when(s == d)
-                def _(d=d):
-                    self.line(k, rows, d, True, False).wait_recv()
-                    self.r3[d, rows] += self.zu[d, rows]
-
-            if d < n - 1:
-
-                @pl.when(s == d)
-                def _(d=d):
-                    self.line(k, rows, d, False, False).wait_recv()
-                    self.r3[d, rows] += self.zd[d, rows]
-
-    def drain(self, k, rows):
-        self.first(k, rows).wait_send()
-        self.second(k, rows).wait_send()
-        self.third(k, rows).wait_send()
-        self.along(k, rows, drain=True)
+        self.r3[:, rows] += self.r2[:, own, rows]
+        for d in range(1, self.n):
+            self.along(k, d).start()
+
+    def arrive(self, k, out):
+        for d in range(1, self.n):
+            self.along(k, d).wait_recv()
+        rows = self.rows[k]
+        total = self.r3[self.s, rows].astype(F32)
+        for d in range(1, self.n):
+            total = total + self.z[d - 1, rows].astype(F32)
+        out[rows, :] = total.astype(out.dtype)
+
+    def drain(self, k):
+        for copy in [self.one(k), self.two(k), self.three(k)] + [self.along(k, d) for d in range(1, self.n)]:
+            copy.wait_send()
 
 
 class SmallSum:
@@ -954,15 +923,10 @@
         self.s, self.c, self.t = (lax.axis_index(a) for a in ("shard", "ctx", "tp"))
 
     def copy(self, i):
-        device = [
-            {"tp": self.t + 1 - 2 * lax.rem(self.t, 2)},
-            {"tp": lax.rem(self.t + 2, 4)},
-            {"ctx": 1 - self.c},
-            {"shard": self.s + 1},
-            {"shard": self.s - 1},
-        ][i]
+        near = [{"tp": self.t + 1 - 2 * lax.rem(self.t, 2)}, {"tp": lax.rem(self.t + 2, 4)}, {"ctx": 1 - self.c}]
+        device = near[i] if i < 3 else {"shard": lax.rem(self.s + i - 2, self.n)}
         return pltpu.make_async_remote_copy(
-            src_ref=self.own.at[i], dst_ref=self.got.at[i], send_sem=self.send.at[i],
+            src_ref=self.own.at[min(i, 3)], dst_ref=self.got.at[i], send_sem=self.send.at[i],
             recv_sem=self.recv.at[i], device_id=device, device_id_type=MESH,
         )
 
@@ -975,71 +939,77 @@
         self.own[i + 1] = self.own[i] + self.got[i]
         if i < 2:
             self.copy(i + 1).start()
-
-    def line(self, out):
-        s, n = self.s, self.n
-        mine = self.own[3]
-        self.own[4] = mine
-        out[...] = mine
-
-        @pl.when(s > 0)
-        def _():
-            self.copy(3).wait_recv()
-            self.own[3] = mine + self.got[3]
-            out[...] += self.got[3]
-
-        @pl.when(s < n - 1)
-        def _():
-            self.copy(3).start()
-            self.copy(4).wait_recv()
-            self.own[4] = mine + self.got[4]
-            out[...] += self.got[4]
-
-        @pl.when(s > 0)
-        def _():
-            self.copy(4).start()
+        else:
+            for d in range(1, self.n):
+                self.copy(2 + d).start()
+
+    def arrive(self, out):
+        total = self.own[3]
+        for d in range(1, self.n):
+            self.copy(2 + d).wait_recv()
+            total = total + self.got[2 + d]
+        out[...] = total
 
     def drain(self):
-        for i in range(3):
+        for i in range(2 + self.n):
             self.copy(i).wait_send()
 
-        @pl.when(self.s < self.n - 1)
-        def _():
-            self.copy(3).wait_send()
-
-        @pl.when(self.s > 0)
-        def _():
-            self.copy(4).wait_send()
-
 
 class Spread:
-    def __init__(self, refs, send, recv):
-        self.refs, self.send, self.recv = refs, send, recv
+    def __init__(self, src, dst, send, recv):
+        self.src, self.dst, self.send, self.recv = src, dst, send, recv
         self.t = lax.axis_index("tp")
 
-    def copy(self, i, d):
-        src, dst, split = self.refs[i]
+    def copy(self, d):
         to = lax.rem(self.t + d, 4)
-        if split:
-            share = dst.shape[1]
-            src = src.at[pl.ds(pl.multiple_of(to * share, share), share)]
-        dst = dst.at[self.t]
+        share = self.dst.shape[1]
+        src = self.src.at[pl.ds(pl.multiple_of(to * share, share), share)]
+        dst = self.dst.at[self.t]
         if d == 0:
-            return pltpu.make_async_copy(src, dst, self.send.at[i, d])
+            return pltpu.make_async_copy(src, dst, self.send.at[d])
         return pltpu.make_async_remote_copy(
-            src_ref=src, dst_ref=dst, send_sem=self.send.at[i, d], recv_sem=self.recv.at[i, d],
+            src_ref=src, dst_ref=dst, send_sem=self.send.at[d], recv_sem=self.recv.at[d],
             device_id={"tp": to}, device_id_type=MESH,
         )
 
-    def start(self, i):
-        for d in (1, 2, 3, 0):
-            self.copy(i, d).start()
-
-    def finish(self, i):
+    def start(self):
+        for d in (2, 3, 1, 0):
+            self.copy(d).start()
+
+    def finish(self):
         for d in (1, 2, 3):
-            self.copy(i, d).wait_recv()
-            self.copy(i, d).wait_send()
-        self.copy(i, 0).wait()
+            self.copy(d).wait_recv()
+            self.copy(d).wait_send()
+        self.copy(0).wait()
+
+
+class Share:
+    def __init__(self, held, send, recv):
+        self.held, self.send, self.recv = held, send, recv
+        self.t = lax.axis_index("tp")
+        self.pair_tp = self.t + 1 - 2 * lax.rem(self.t, 2)
+        self.across_tp = lax.rem(self.t + 2, 4)
+
+    def copy(self, i, tp, to):
+        return pltpu.make_async_remote_copy(
+            src_ref=self.held.at[tp], dst_ref=self.held.at[tp], send_sem=self.send.at[i],
+            recv_sem=self.recv.at[i], device_id={"tp": to}, device_id_type=MESH,
+        )
+
+    def start(self):
+        self.copy(0, self.t, self.across_tp).start()
+        self.copy(1, self.t, self.pair_tp).start()
+
+    def relay(self):
+        self.copy(0, self.across_tp, self.across_tp).wait_recv()
+        self.copy(2, self.across_tp, self.pair_tp).start()
+
+    def finish(self):
+        self.copy(1, self.pair_tp, self.pair_tp).wait_recv()
+        self.copy(2, lax.rem(self.pair_tp + 2, 4), self.pair_tp).wait_recv()
+        self.copy(0, self.t, self.across_tp).wait_send()
+        self.copy(1, self.t, self.pair_tp).wait_send()
+        self.copy(2, self.across_tp, self.pair_tp).wait_send()
 
 
 class Comm:
@@ -1056,8 +1026,8 @@
         og=v((4, tokens // 4, width), BF),
         y=v((tokens, width), BF),
         xg=v((tokens, width), BF),
-        mem_out=v((slots, width), F32),
-        mig=v((slots, width), F32),
+        mems=v((4, slots, width), BF),
+        migs=v((4, slots, width), BF),
         small=v((8, width), F32),
         m_send=v((slots, width), BF),
         m_recv=v((slots, width), BF),
@@ -1070,8 +1040,14 @@
         w_recv=dma((9, n, len(GROUPS))),
         og_send=dma((4,)),
         og_recv=dma((4,)),
-        o_send=dma((4, 4)),
-        o_recv=dma((4, 4)),
+        y_send=dma((4,)),
+        y_recv=dma((4,)),
+        xg_send=dma((4,)),
+        xg_recv=dma((4,)),
+        mem_send=dma((3,)),
+        mem_recv=dma((3,)),
+        mig_send=dma((3,)),
+        mig_recv=dma((3,)),
     )
     if direct:
         c = len(pk.chunks)
@@ -1080,14 +1056,13 @@
             r1=v((n, 2, 2, pk.rows, 128), BF),
             r2=v((n, 2, pk.rows, 128), BF),
             r3=v((n, pk.rows, 128), BF),
-            zu=v((n, pk.rows, 128), BF),
-            zd=v((n, pk.rows, 128), BF),
-            own=v((5, 8, width), F32),
-            got=v((5, 8, width), F32),
-            r_send=dma((9 * c,)),
-            r_recv=dma((9 * c,)),
-            s_send=dma((5,)),
-            s_recv=dma((5,)),
+            z=v((n - 1, pk.rows, 128), BF),
+            own=v((4, 8, width), F32),
+            got=v((2 + n, 8, width), F32),
+            r_send=dma((c, 2 + n)),
+            r_recv=dma((c, 2 + n)),
+            s_send=dma((2 + n,)),
+            s_recv=dma((2 + n,)),
         )
     return out
 
@@ -1095,8 +1070,8 @@
 def step_kernel(dims, pk, direct, names, unit_names, *refs):
     shards, ctxs, halved = dims
     first, length, inputs, first_memory, memory_grad, out_grad = refs[:6]
-    weights, gains, outs = refs[6:17], refs[17], refs[18:24]
-    scratch = refs[24:]
+    weights, gains, outs = refs[6:17], refs[17:21], refs[21:27]
+    scratch = refs[27:]
     b = Comm()
     b.__dict__.update(zip(names, scratch))
     unit_refs = dict(zip(unit_names, scratch[len(names) :]))
@@ -1143,17 +1118,17 @@
             recv_sem=b.og_recv.at[d], device_id={"tp": to}, device_id_type=MESH,
         )
 
-    spread = Spread(
-        [(b.y, outs[0], True), (b.mem_out, outs[1], False), (b.xg, outs[2], True), (b.mig, outs[3], False)],
-        b.o_send, b.o_recv,
-    )
+    spread_y = Spread(b.y, outs[0], b.y_send, b.y_recv)
+    spread_xg = Spread(b.xg, outs[2], b.xg_send, b.xg_recv)
+    share_mem = Share(b.mems, b.mem_send, b.mem_recv)
+    share_mig = Share(b.migs, b.mig_send, b.mig_recv)
     lead, follow = pl.when(c == 0), pl.when(c > 0)
     pairs = u.width // 128
 
     gather_until(0, 1)
     for copy in loads:
         copy.wait()
-    u.make_bias(first[t, 0], length[t, 0])
+    u.make_bias(first[0, t], length[0, t])
     gather_until(1, 2)
     u.tokens_in()
     at_first = shards + 2
@@ -1202,21 +1177,22 @@
             u.feed_forward_down()
 
     after = u.write_memory()
-    b.mem_out[...] = after
-    b.y[...] = u.af[...].astype(BF)
+    b.m_send[...] = after.astype(BF)
     if ctxs > 1:
-        b.m_send[...] = after.astype(BF)
 
         @pl.when(c < ctxs - 1)
         def _():
             chain_copy(0, c + 1).start()
 
-    spread.start(0)
-    spread.start(1)
+    b.mems[t] = after.astype(BF)
+    b.y[...] = u.af[...].astype(BF)
+    share_mem.start()
+    spread_y.start()
     u.backward_early()
     mine.wait()
     for d in (1, 2, 3):
         og_copy(d).wait_recv()
+    share_mem.relay()
 
     if ctxs > 1:
 
@@ -1232,57 +1208,60 @@
     def grads(*which):
         weight_grads(u, b.g, pk, which)
 
-    if direct:
-        red = Reduce(shards, b.g, b.r1, b.r2, b.r3, b.zu, b.zd, b.r_send, b.r_recv)
-        rows = [pl.ds(lo, hi - lo) for lo, hi in pk.chunks]
-        sums = SmallSum(shards, b.own, b.got, b.s_send, b.s_recv)
+    red = Reduce(shards, pk.chunks, b.g, b.r1, b.r2, b.r3, b.z, b.r_send, b.r_recv) if direct else None
+    sums = SmallSum(shards, b.own, b.got, b.s_send, b.s_recv) if direct else None
+    DOWN, WRITE, UP, OUT, IN0, IN1 = range(6)
 
     def reduce(*todo):
-        if direct:
-            for what, k in todo:
-                if what == "first":
-                    red.first(k, rows[k]).start()
-                else:
-                    getattr(red, what)(k, rows[k])
-
-    A, DOWN, UP, C0, C1 = range(5)
+        for what, k in todo if direct else ():
+            getattr(red, what)(k)
+
     u.write_back(out_grad_rows)
 
     @lead
     def _():
+        grads("down")
+        reduce(("start", DOWN))
         grads("write")
-        reduce(("first", A))
+        reduce(("start", WRITE), ("to_second", DOWN))
 
     u.feed_forward_back()
 
     @lead
     def _():
-        reduce(("add_first", A))
-        grads("down")
-        reduce(("first", DOWN))
         grads("up")
-        reduce(("first", UP))
-
-    u.project_back()
+        reduce(("start", UP), ("to_second", WRITE))
+
+    u.feed_forward_enter()
 
     @lead
     def _():
-        reduce(("add_first", DOWN), ("add_second", A))
-
+        grads("wo")
+        reduce(("start", OUT), ("to_second", UP), ("to_third", DOWN))
+
+    u.project_back()
     u.attend_back(0, pairs // 2)
 
     @lead
     def _():
-        reduce(("add_first", UP), ("add_second", DOWN))
+        reduce(("to_second", OUT), ("to_third", WRITE))
 
     u.attend_back(pairs // 2, pairs - pairs // 2)
+    u.queries_back()
 
     @lead
     def _():
-        reduce(("add_third", A), ("along", A), ("add_second", UP))
-
-    back = u.enter_back(b.xg)
-    b.mig[...] = back
+        grads("enter")
+        reduce(("start", IN0), ("start", IN1), ("to_last", DOWN), ("to_third", UP), ("to_third", OUT))
+
+    u.enter_back()
+
+    @lead
+    def _():
+        reduce(("to_second", IN0), ("to_second", IN1), ("to_last", WRITE), ("to_last", UP))
+
+    back = u.norm_enter(b.xg)
+    b.migs[t] = back.astype(BF)
 
     if ctxs > 1:
 
@@ -1290,48 +1269,50 @@
         def _():
             b.g_send[...] = back.astype(BF)
             chain_copy(1, c - 1).start()
+            grads("down")
+            reduce(("start", DOWN))
             grads("write")
-            reduce(("first", A))
-            grads("down")
-            reduce(("first", DOWN))
+            reduce(("start", WRITE))
             grads("up")
-            reduce(("first", UP))
-
-    grads("wo", "wq")
-    reduce(("first", C0))
-    grads("wkv")
-    reduce(("first", C1))
-    spread.start(2)
-    spread.start(3)
+            reduce(("start", UP), ("to_second", DOWN))
+            grads("wo")
+            reduce(("start", OUT), ("to_second", WRITE))
+            grads("enter")
+            reduce(("start", IN0), ("start", IN1))
+            reduce(*(("to_second", k) for k in (UP, OUT, IN0, IN1)))
+
+    share_mig.start()
     if direct:
         sums.start(b.small[...])
+    spread_xg.start()
 
     @lead
     def _():
-        reduce(("add_third", DOWN), ("along", DOWN), ("add_third", UP), ("along", UP), ("arrive", A))
-        reduce(("add_first", C0), ("add_first", C1), ("arrive", DOWN), ("arrive", UP))
-        reduce(("add_second", C0), ("add_second", C1))
-
-    @follow
-    def _():
-        reduce(*(("add_first", k) for k in range(5)))
-        reduce(*(("add_second", k) for k in (A, DOWN, C0)))
-        reduce(("add_third", A), ("along", A), ("add_second", UP), ("add_third", DOWN), ("along", DOWN))
-        reduce(("add_third", UP), ("along", UP), ("arrive", A), ("arrive", DOWN), ("arrive", UP), ("add_second", C1))
-
-    reduce(("add_third", C0), ("along", C0), ("add_third", C1), ("along", C1))
+        reduce(("to_third", IN0), ("to_third", IN1), ("to_last", OUT))
+
+    if ctxs > 1:
+
+        @follow
+        def _():
+            reduce(*(("to_third", k) for k in (DOWN, UP, IN0, WRITE)))
+            reduce(("to_last", DOWN), ("to_third", OUT), ("to_last", WRITE), ("to_last", UP))
+            reduce(("to_last", OUT), ("to_third", IN1))
+
+    share_mig.relay()
+    reduce(("to_last", IN0), ("to_last", IN1))
     if direct:
         for i in range(3):
             sums.step(i)
-        sums.line(outs[5])
-    reduce(("arrive", C0), ("arrive", C1))
-    if direct:
-        outs[4][...] = b.r3[s]
+        for k in range(6):
+            red.arrive(k, outs[4])
+        sums.arrive(outs[5])
     else:
         outs[5][...] = b.small[...]
 
-    for i in range(4):
-        spread.finish(i)
+    for spread in (spread_y, spread_xg, share_mem, share_mig):
+        spread.finish()
+    outs[1][...] = b.mems[...].astype(F32)
+    outs[3][...] = b.migs[...].astype(F32)
     for d in (1, 2, 3):
         og_copy(d).wait_send()
     for g in range(len(GROUPS)):
@@ -1348,7 +1329,7 @@
 
     if direct:
         sums.drain()
-    reduce(*(("drain", k) for k in range(5)))
+    reduce(*(("drain", k) for k in range(6)))
 
 
 def run_step(dims, pk, direct, first, length, inputs, first_memory, memory_grad, out_grad, weights, gains):
@@ -1367,14 +1348,14 @@
             shape((4, tokens // 4, width), BF), shape((4, slots, width), F32),
             shape((pk.rows, 128) if direct else pk.shape, BF), shape((8, width), F32),
         ),
-        in_specs=[sm, sm] + [hbm] * 15 + [vm],
-        out_specs=(hbm,) * 4 + (vm, vm),
+        in_specs=[sm, sm] + [hbm] * 15 + [vm] * 4,
+        out_specs=(hbm, vm, hbm, vm, vm, vm),
         scratch_shapes=list(scratch.values()) + list(unit.values()),
         compiler_params=pltpu.CompilerParams(
             vmem_limit_bytes=VMEM_LIMIT, collective_id=1, has_side_effects=True
         ),
         name="step",
-    )(first, length, inputs, first_memory, memory_grad, out_grad, *weights, gains)
+    )(first, length, inputs, first_memory, memory_grad, out_grad, *weights, *gains)
 
 
 def store_kernel(pk, owners, *refs):
@@ -1390,7 +1371,7 @@
     for name, ref in dict(wq=wq, wk=wk, wv=wv, uq=uq, uk=uk, uv=uv).items():
         ref[...] = part(pk.heads[name], h)
     for name, ref in dict(uo=uo, ugate=ugate).items():
-        ref[...] = part(pk.heads[name], h).T
+        ref[...] = part(pk.heads[name], h)
     for at, r, ref in ((pk.at_wo, pk.row_rows, wo), (pk.at_up, pk.row_rows, up), (pk.at_down, pk.down_rows, down)):
         for j in range(ref.shape[1] // 128):
             ref[:, j * 128 : j * 128 + 128] = part(at + j * r, r)
@@ -1408,10 +1389,10 @@
     shape = jax.ShapeDtypeStruct
     width = small.shape[1]
     h = pk.head_rows
-    head, turned = shape((h, 128), F32), shape((128, h), F32)
+    head = shape((h, 128), F32)
     outs = tuple(shape(r.shape, r.dtype) for r in rows) + (
         head, head, head, shape((pk.row_rows, width), F32), shape((pk.row_rows, pk.ff), F32),
-        shape((pk.down_rows, width), F32), head, head, head, turned, turned,
+        shape((pk.down_rows, width), F32), head, head, head, head, head,
     ) + (shape((1, width // owners), F32),) * 4
     return pl.pallas_call(
         partial(store_kernel, pk, owners),
@@ -1456,18 +1437,18 @@
     ff = w_up.shape[1]
     assert seqs == tps == 4 and tokens == width == 512 and ff == 2048
     weights = (w_query, w_key, w_value, w_out, w_up, w_down, u_query, u_key, u_value, u_out, u_gate)
-    gains = jnp.stack([gain_attn, gain_ffn, gain_write, gate_bias] * 2)
+    gains = [v.reshape(1, -1) for v in (gain_attn, gain_ffn, gain_write, gate_bias)]
     owners = shards * ctxs * tps
     direct = ctxs == 2 and width % (owners * 16) == 0
     halved = ctxs == 2 and w_query.shape[0] % 32 == 0
     pk = Packing(shards if direct else 4, 2, width, ff)
     got = run_step(
-        (shards, ctxs, halved), pk, direct, piece_start, piece_len, inputs, first_memory, memory_grad,
+        (shards, ctxs, halved), pk, direct, piece_start.T, piece_len.T, inputs, first_memory, memory_grad,
         out_grad, weights, gains,
     )
     if direct:
         out = run_store(pk, owners, got[:4], got[4], got[5])
-        return out[:15] + tuple(v.reshape(-1) for v in out[15:])
+        return out[:13] + (out[13].T, out[14].T) + tuple(v.reshape(-1) for v in out[15:])
     every = ("shard", "ctx", "tp")
     out = list(got[:4])
     for i, g in enumerate(full_gradients(pk, got[4])):

time: 250 us -> 191 us (0.76)
  Pallas kernels: 242 us -> 190 us
  local copies, waits for them, and re-layouts: 7.12 us -> 0 us
    pallas_call x1, Pallas kernels: 239 us -> 186 us  [run_step(): pl.pallas_call(partial(step_kernel, dims, pk, direct, tuple(scratch), tup...]
    unnamed x4 -> x0, local copies, waits for them, and re-layouts: 5.7 us -> none
where the time goes in v3:
time: 191 us; the launch traced here: 190 us
  Pallas kernels  190 us (99%)
    pallas_call x1, Pallas kernels, run_step(): pl.pallas_call(partial(step_kernel, dims, pk, direct, tuple(scratch), tup...  186 us

profile of v3, /device:TPU:0, one launch (start us, length us, event | category | flops | bytes accessed | tf_op | source)
XLA Modules:
  0.0 190.5 jit_solution(1691536523291725703)
XLA Ops:
  0.7 186.5 %step.1 = (bf16[4,128,512]{2,1,0:T(8,128)(2,1)}, f32[4,64,512]{2,1,0:T(8,128)}, bf16[4,128,512]{2,1,0:T(8,128)(2,1)}, f32[4,64,512]{2,1,0:T(8,128)}, bf16[1088,128]{1,0:T(8,128)(2,1)}, /*index=5*/f32[8,512]{1,0:T(8,128)}) custom-call(s32[1,4]{1,0:T(1,128)} %bitcast.16, s32[1,4]{1,0:T(1,128)} %bitcast.17, bf16[4,512,512]{2,1,0:T(8,128)(2,1)} %refs_2_.1, ...), custom_call_target="tpu_custom_call" | custom-call | tf_op jit(solution)/shard_map/step/pallas_call | solution.py:1344
  187.2 3.1 %store.1 = (bf16[4,128,512]{2,1,0:T(8,128)(2,1)}, f32[4,64,512]{2,1,0:T(8,128)}, bf16[4,128,512]{2,1,0:T(8,128)(2,1)}, f32[4,64,512]{2,1,0:T(8,128)}, f32[64,128...) custom-call(bf16[4,128,512]{2,1,0:T(8,128)(2,1)} %get-tuple-element., ...), custom_call_target="tpu_custom_call" | custom-call | tf_op jit(solution)/shard_map/store/pallas_call | solution.py:1397

commit v4 on v3

--- a/solution.py
+++ b/solution.py
@@ -44,6 +44,24 @@
         lax.fori_loop(0, count, step, 0, unroll=unroll)
 
     return run
+
+
+BLOCK = 64
+UNROLL = 4
+
+
+def blocks(total, body, carry=None):
+    def step(n, carry):
+        for k in range(UNROLL):
+            i = n * UNROLL + k
+            carry = body(rows_at(i, BLOCK), i, carry)
+        return carry
+
+    return lax.fori_loop(0, total // (BLOCK * UNROLL), step, carry)
+
+
+def fold(values):
+    return jnp.sum(values.reshape(values.shape[0] // 8, 8, values.shape[1]), axis=0)
 
 
 def normed(v):
@@ -178,10 +196,10 @@
         self.enc[rows, :] = (hat * self.gain(0)).astype(BF)
 
     def tokens_in(self):
-        @loop(self.tokens // 32, unroll=2)
-        def _(i):
-            rows = rows_at(i, 32)
+        def body(rows, i, carry):
             self.norm_in(rows, self.x[rows, :].astype(F32))
+
+        blocks(self.tokens, body)
 
     def project_tokens(self):
         t = self.tokens
@@ -245,13 +263,13 @@
             got = dot(self.gmx[...], self.w.cols(WO, n * 256, 256))
             self.af[:, cols] = self.x[:, cols].astype(F32) + got
 
-        @loop(t // 32, unroll=2)
-        def _(i):
-            rows = rows_at(i, 32)
+        def body(rows, i, carry):
             hat, inv = normed(self.af[rows, :])
             self.ah[rows, :] = hat
             self.ar[rows, :] = inv
             self.fin[rows, :] = (hat * self.gain(1)).astype(BF)
+
+        blocks(t, body)
 
     def feed_forward_up(self):
         t = self.tokens
@@ -285,13 +303,13 @@
                 )
             self.af[:, cols] = total
 
-        @loop(t // 32, unroll=2)
-        def _(i):
-            rows = rows_at(i, 32)
+        def body(rows, i, carry):
             hat, inv = normed(self.af[rows, :])
             self.yh[rows, :] = hat
             self.yr[rows, :] = inv
             self.wri[rows, :] = (hat * self.gain(2)).astype(BF)
+
+        blocks(t, body)
 
         self.wri[t : self.r, :] = (self.xh[t : self.r, :] * self.gain(2)).astype(BF)
 
@@ -375,17 +393,17 @@
         em = em + dot_nt(ggl, self.w.row_part(UGATE, 0, 1))
         hat = self.xh[t:r, :]
         self.bwm[...] = norm_pull(em, self.gain(2), hat, self.xr[t:r, :])
-        self.small[2:3, :] = jnp.sum(em * hat, axis=0, keepdims=True)
-
-        @loop(t // 32, unroll=2)
-        def _(i):
-            rows = rows_at(i, 32)
+
+        def body(rows, i, carry):
             e = self.e[rows, :]
             hat = self.yh[rows, :]
-            self.small[2:3, :] += jnp.sum(e * hat, axis=0, keepdims=True)
             grad = out_grad(i) + norm_pull(e, self.gain(2), hat, self.yr[rows, :])
             self.gy[rows, :] = grad
             self.gyb[rows, :] = grad.astype(BF)
+            return carry + fold(e * hat)
+
+        total = blocks(t, body, fold(em * hat))
+        self.small[2:3, :] = jnp.sum(total, axis=0, keepdims=True)
 
     def feed_forward_back(self):
         t = self.tokens
@@ -414,17 +432,16 @@
                 total = total + dot_nt(self.gpre[j], self.w.row_part(WUP + j, n, 2))
             self.e[0:t, cols] = total
 
-        self.small[1:2, :] = jnp.zeros((1, self.width), F32)
-
-        @loop(t // 32, unroll=2)
-        def _(i):
-            rows = rows_at(i, 32)
+        def body(rows, i, carry):
             e = self.e[rows, :]
             hat = self.ah[rows, :]
-            self.small[1:2, :] += jnp.sum(e * hat, axis=0, keepdims=True)
             grad = self.gy[rows, :] + norm_pull(e, self.gain(1), hat, self.ar[rows, :])
             self.gy[rows, :] = grad
             self.gab[rows, :] = grad.astype(BF)
+            return carry + fold(e * hat)
+
+        total = blocks(t, body, jnp.zeros((8, self.width), F32))
+        self.small[1:2, :] = jnp.sum(total, axis=0, keepdims=True)
 
     def project_back(self):
         @loop(2)
@@ -478,18 +495,19 @@
         t, r = self.tokens, self.r
         e = self.e[t:r, :]
         hat = self.xh[t:r, :]
-        self.small[0:1, :] = jnp.sum(e * hat, axis=0, keepdims=True)
+        first = fold(e * hat)
         mem_grad = self.gm[...] * self.gate[...] + self.bwm[...]
         mem_grad = mem_grad + norm_pull(e, self.gain(0), hat, self.xr[t:r, :])
 
-        @loop(t // 32, unroll=2)
-        def _(i):
-            rows = rows_at(i, 32)
+        def body(rows, i, carry):
             e = self.e[rows, :]
             hat = self.xh[rows, :]
-            self.small[0:1, :] += jnp.sum(e * hat, axis=0, keepdims=True)
             grad = self.gy[rows, :] + norm_pull(e, self.gain(0), hat, self.xr[rows, :])
             input_grad[rows, :] = grad.astype(BF)
+            return carry + fold(e * hat)
+
+        total = blocks(t, body, first)
+        self.small[0:1, :] = jnp.sum(total, axis=0, keepdims=True)
 
         return mem_grad
 
@@ -612,10 +630,12 @@
 
 
 class Gather:
-    UP, DOWN, PAIR, ACROSS, PAIR_ACROSS, BESIDE, PAIR_BESIDE, FAR, PAIR_FAR = range(9)
-
-    def __init__(self, shards, halved, w, send, recv):
-        self.n, self.halved, self.w, self.send, self.recv = shards, halved, w, send, recv
+    UP, DOWN, ACROSS, BESIDE, FAR, PAIR, PAIR_ACROSS, PAIR_BESIDE, PAIR_FAR = range(9)
+    LINKS = {ACROSS: 0, BESIDE: 1, FAR: 2, PAIR: 3, PAIR_ACROSS: 3, PAIR_BESIDE: 3, PAIR_FAR: 3}
+
+    def __init__(self, shards, halved, w, send, line_send, recv, pair_recv):
+        self.n, self.halved, self.w = shards, halved, w
+        self.send, self.line_send, self.recv, self.pair_recv = send, line_send, recv, pair_recv
         self.s, self.c, self.t = (lax.axis_index(a) for a in ("shard", "ctx", "tp"))
         odd = lax.rem(self.t, 2)
         self.pair_tp = self.t + 1 - 2 * odd
@@ -630,9 +650,17 @@
         if half is not None:
             size = self.w.shape[2] // 2
             block = self.w.at[source * 4 + tp, lo:hi, pl.ds(pl.multiple_of(half * size, size), size)]
+        return self.between(block, kind, source, g, device)
+
+    def between(self, block, kind, source, g, device):
+        if kind in (self.UP, self.DOWN):
+            send = self.line_send.at[kind, source]
+        else:
+            send = self.send.at[self.LINKS[kind]]
+        to_pair = kind in (self.PAIR, self.PAIR_ACROSS, self.PAIR_BESIDE, self.PAIR_FAR)
+        recv = self.pair_recv.at[g] if to_pair else self.recv.at[kind, source, g]
         return pltpu.make_async_remote_copy(
-            src_ref=block, dst_ref=block, send_sem=self.send.at[kind, source, g],
-            recv_sem=self.recv.at[kind, source, g], device_id=device, device_id_type=MESH,
+            src_ref=block, dst_ref=block, send_sem=send, recv_sem=recv, device_id=device, device_id_type=MESH,
         )
 
     @property
@@ -739,46 +767,33 @@
                 self.copy(self.FAR, source, self.t, g, self.beside, self.others).wait_recv()
                 self.copy(self.PAIR_FAR, source, self.t, g, self.pair, self.others).start()
 
-    def finish(self, g, own=False):
-        tp = self.t if own else self.pair_tp
-        other = self.across_tp if own else lax.rem(self.pair_tp + 2, 4)
-        for d in range(self.n):
-            for source, cond in self.sources(d):
-
-                @pl.when(cond)
-                def _(source=source, d=d):
-                    copies = [
-                        self.to_pair(source, g, self.far(d), tp),
-                        self.copy(self.PAIR_ACROSS, source, other, g, self.pair, self.mine),
-                    ]
-                    if self.halved:
-                        copies.append(self.copy(self.PAIR_BESIDE, source, other, g, self.pair, self.others))
-                    if self.far(d):
-                        copies.append(self.copy(self.PAIR_FAR, source, tp, g, self.pair, self.others))
-                    if own:
-                        copies.append(self.to_across(source, g))
-                        if self.halved:
-                            copies.append(self.copy(self.BESIDE, source, other, g, self.beside, self.c))
-                        if self.far(d):
-                            copies.append(self.copy(self.FAR, source, tp, g, self.beside, self.c))
-                    for copy in copies:
-                        if own:
-                            copy.wait_send()
-                        else:
-                            copy.wait_recv()
-
-    def drain(self, g):
+    def finish(self, g):
+        lo, hi = GROUPS[g]
+        self.between(self.w.at[0 : 2 * self.n, lo:hi], self.PAIR, 0, g, self.pair).wait_recv()
+
+    def drain(self):
         s, n = self.s, self.n
-        self.finish(g, own=True)
+        parts = n // 2 if self.halved else n
+        half = self.w.at[0, :, 0 : self.w.shape[2] // 2]
+        self.between(self.w.at[0 : 2 * n], self.PAIR, 0, 0, self.pair).wait_send()
+        self.between(self.w.at[0:parts], self.ACROSS, 0, 0, self.across).wait_send()
+        if self.halved:
+            self.between(self.w.at[0:parts], self.BESIDE, 0, 0, self.beside).wait_send()
+
+            @pl.when(jnp.logical_or(s == 0, s == n - 1))
+            def _():
+                self.between(half, self.FAR, 0, 0, self.beside).wait_send()
+
         for d in range(n - 1):
+            block = half if self.far(d + 1) else self.w.at[0]
 
             @pl.when(jnp.logical_and(s - d >= 0, s < n - 1))
-            def _(d=d):
-                self.up(s - d, g, self.far(d + 1)).wait_send()
+            def _(d=d, block=block):
+                self.between(block, self.UP, s - d, 0, {"shard": s + 1}).wait_send()
 
             @pl.when(jnp.logical_and(s + d <= n - 1, s > 0))
-            def _(d=d):
-                self.down(s + d, g, self.far(d + 1)).wait_send()
+            def _(d=d, block=block):
+                self.between(block, self.DOWN, s + d, 0, {"shard": s - 1}).wait_send()
 
     def events(self, time, ready):
         n = self.n
@@ -847,7 +862,7 @@
 
     def copy(self, src, dst, k, kind, device):
         return pltpu.make_async_remote_copy(
-            src_ref=src, dst_ref=dst, send_sem=self.send.at[k, kind], recv_sem=self.recv.at[k, kind],
+            src_ref=src, dst_ref=dst, send_sem=self.send.at[kind], recv_sem=self.recv.at[k, kind],
             device_id=device, device_id_type=MESH,
         )
 
@@ -912,9 +927,11 @@
             total = total + self.z[d - 1, rows].astype(F32)
         out[rows, :] = total.astype(out.dtype)
 
-    def drain(self, k):
-        for copy in [self.one(k), self.two(k), self.three(k)] + [self.along(k, d) for d in range(1, self.n)]:
-            copy.wait_send()
+    def drain(self):
+        whole = [(self.r1, 0), (self.r1.at[:, :, 0], 1), (self.r1.at[:, 0, 0], 2)]
+        whole += [(self.r3.at[0], 2 + d) for d in range(1, self.n)]
+        for ref, kind in whole:
+            self.copy(ref, ref, 0, kind, self.pair).wait_send()
 
 
 class SmallSum:
@@ -1036,8 +1053,10 @@
         chain=dma((4,)),
         loads=dma((3,)),
         local=dma((TILES,)),
-        w_send=dma((9, n, len(GROUPS))),
-        w_recv=dma((9, n, len(GROUPS))),
+        w_send=dma((4,)),
+        w_line_send=dma((2, n)),
+        w_recv=dma((5, n, len(GROUPS))),
+        w_pair_recv=dma((len(GROUPS),)),
         og_send=dma((4,)),
         og_recv=dma((4,)),
         y_send=dma((4,)),
@@ -1059,7 +1078,7 @@
             z=v((n - 1, pk.rows, 128), BF),
             own=v((4, 8, width), F32),
             got=v((2 + n, 8, width), F32),
-            r_send=dma((c, 2 + n)),
+            r_send=dma((2 + n,)),
             r_recv=dma((c, 2 + n)),
             s_send=dma((2 + n,)),
             s_recv=dma((2 + n,)),
@@ -1094,7 +1113,7 @@
     if ctxs > 1:
         peers += [(c > 0, {"ctx": c - 1}), (c < ctxs - 1, {"ctx": c + 1})]
     greet(peers)
-    gather = Gather(shards, halved, b.w, b.w_send, b.w_recv)
+    gather = Gather(shards, halved, b.w, b.w_send, b.w_line_send, b.w_recv, b.w_pair_recv)
 
     def ready(g):
         for copy in copies[GROUPS[g][0] : GROUPS[g][1]]:
@@ -1168,6 +1187,7 @@
 
         @follow
         def _():
+            gather.drain()
             chain_copy(0, c - 1).wait_recv()
             u.mem[...] = b.m_recv[...].astype(F32)
             u.memory_in()
@@ -1194,6 +1214,10 @@
         og_copy(d).wait_recv()
     share_mem.relay()
 
+    @lead
+    def _():
+        gather.drain()
+
     if ctxs > 1:
 
         @pl.when(c < ctxs - 1)
@@ -1202,8 +1226,8 @@
             u.gm[...] += b.g_recv[...].astype(F32)
 
     def out_grad_rows(i):
-        per = b.og.shape[1] // 32
-        return b.og[lax.div(i, per), pl.ds(lax.rem(i, per) * 32, 32), :].astype(F32)
+        per = b.og.shape[1] // BLOCK
+        return b.og[lax.div(i, per), pl.ds(lax.rem(i, per) * BLOCK, BLOCK), :].astype(F32)
 
     def grads(*which):
         weight_grads(u, b.g, pk, which)
@@ -1315,8 +1339,6 @@
     outs[3][...] = b.migs[...].astype(F32)
     for d in (1, 2, 3):
         og_copy(d).wait_send()
-    for g in range(len(GROUPS)):
-        gather.drain(g)
     if ctxs > 1:
 
         @pl.when(c < ctxs - 1)
@@ -1329,7 +1351,7 @@
 
     if direct:
         sums.drain()
-    reduce(*(("drain", k) for k in range(6)))
+        red.drain()
 
 
 def run_step(dims, pk, direct, first, length, inputs, first_memory, memory_grad, out_grad, weights, gains):

time: 191 us -> 183 us (0.958)
  Pallas kernels: 190 us -> 182 us
    pallas_call x1, Pallas kernels: 186 us -> 179 us  [run_step(): pl.pallas_call(partial(step_kernel, dims, pk, direct, tuple(scratch), tup...]
where the time goes in v4:
time: 183 us
  Pallas kernels  182 us (99%)
    pallas_call x1, Pallas kernels, run_step(): pl.pallas_call(partial(step_kernel, dims, pk, direct, tuple(scratch), tup...  179 us

profile of v4, /device:TPU:0, one launch (start us, length us, event | category | flops | bytes accessed | tf_op | source)
XLA Modules:
  0.0 183.1 jit_solution(18434316768009188897)
XLA Ops:
  0.7 179.2 %step.1 = (bf16[4,128,512]{2,1,0:T(8,128)(2,1)}, f32[4,64,512]{2,1,0:T(8,128)}, bf16[4,128,512]{2,1,0:T(8,128)(2,1)}, f32[4,64,512]{2,1,0:T(8,128)}, bf16[1088,128]{1,0:T(8,128)(2,1)}, /*index=5*/f32[8,512]{1,0:T(8,128)}) custom-call(s32[1,4]{1,0:T(1,128)} %bitcast.16, s32[1,4]{1,0:T(1,128)} %bitcast.17, bf16[4,512,512]{2,1,0:T(8,128)(2,1)} %refs_2_.1, ...), custom_call_target="tpu_custom_call" | custom-call | tf_op jit(solution)/shard_map/step/pallas_call | solution.py:1366
  179.8 3.1 %store.1 = (bf16[4,128,512]{2,1,0:T(8,128)(2,1)}, f32[4,64,512]{2,1,0:T(8,128)}, bf16[4,128,512]{2,1,0:T(8,128)(2,1)}, f32[4,64,512]{2,1,0:T(8,128)}, f32[64,128...) custom-call(bf16[4,128,512]{2,1,0:T(8,128)(2,1)} %get-tuple-element., ...), custom_call_target="tpu_custom_call" | custom-call | tf_op jit(solution)/shard_map/store/pallas_call | solution.py:1419
